TPU v7x, 32 devices: a whole 2x2x4 slice. The times are simulated.
32 devices in a mesh: dp: 4 (over z), row: 4 (over x, core), col: 2 (over y).
Axes of the slice: x: 2, y: 2, z: 4, core: 2. Of those that a mesh axis runs over, the one named last changes fastest.
Arguments:
- inputs: bfloat16 [2, 32768, 768], P(None, ('dp', 'row', 'col')), may hold values from -6 to 6
- qkv_weight: bfloat16 [768, 2304], P('row', 'col'), may hold values from -0.3125 to 0.3125
- out_weight: bfloat16 [768, 768], P('row', 'col'), may hold values from -0.625 to 0.625
- up_weight: bfloat16 [768, 3072], P('row', 'col'), may hold values from -0.21875 to 0.21875
- down_weight: bfloat16 [3072, 768], P('row', 'col'), may hold values from -0.15625 to 0.15625
- vectors: float32 [768, 8], replicated, may hold values from -1 to 2
- up_bias: float32 [3072], replicated, may hold values from -1.2 to 1.2
- cont_lengths: int32 [2, 16, 8], P(None, ('dp', 'row')), may hold values from 1 to 128
- out_cotangent: bfloat16 [2, 32768, 768], P(None, ('dp', 'row', 'col')), may hold values from -6 to 6
Outputs:
- outputs: bfloat16 [2, 32768, 768], P(None, ('dp', 'row', 'col'))
- input_grad: bfloat16 [2, 32768, 768], P(None, ('dp', 'row', 'col'))
- qkv_grad: float32 [768, 2304], P('row', 'col')
- out_grad: float32 [768, 768], P('row', 'col')
- up_grad: float32 [768, 3072], P('row', 'col')
- down_grad: float32 [3072, 768], P('row', 'col')
- vector_grad: float32 [768, 8], P(('row', 'col'))
- up_bias_grad: float32 [3072], P(('row', 'col'))
All inputs are finite; a program needn't handle non-finite values.
Results may differ from a plain program's by a relative error of at most 0.017.
Values may be sent and summed in bfloat16 or wider, within the bound.
A program may use at most 256 MiB of HBM per device.

v0:
```python
import jax
import jax.numpy as jnp
from jax import lax
from jax.sharding import PartitionSpec as P

H = 12
CLEN = 128


EPSILON = 1e-05


def swapped(value, axis, apart):
    mask = 2**apart
    pairs = [(source, source ^ mask) for source in range(lax.axis_size(axis))]
    return lax.ppermute(value, axis, pairs)


def project(acts, blocks):
    count = acts.shape[0]
    shaped = acts.reshape(count, blocks.shape[0], blocks.shape[2])
    result = jnp.einsum("tri,rcio->tco", shaped, blocks, preferred_element_type=jnp.float32)
    return result.reshape(count, blocks.shape[1] * blocks.shape[3])


def project_back(grads, blocks):
    count = grads.shape[0]
    shaped = grads.reshape(count, blocks.shape[1], blocks.shape[3])
    result = jnp.einsum("tco,rcio->tri", shaped, blocks, preferred_element_type=jnp.float32)
    return result.reshape(count, blocks.shape[0] * blocks.shape[2])


def block_grad(acts, grads, blocks):
    count = acts.shape[0]
    left = acts.reshape(count, blocks.shape[0], blocks.shape[2])
    right = grads.reshape(count, blocks.shape[1], blocks.shape[3])
    result = jnp.einsum("tri,tco->rcio", left, right, preferred_element_type=jnp.float32)
    return result.reshape(blocks.shape[0] * blocks.shape[1], blocks.shape[2] * blocks.shape[3])


def normalize(value):
    average = jnp.mean(value, axis=-1, keepdims=True)
    centred = value - average
    spread = jnp.mean(centred * centred, axis=-1, keepdims=True)
    inverse = lax.rsqrt(spread + EPSILON)
    return (centred * inverse, inverse)


def normalize_back(grad_normed, normed, inverse):
    first = jnp.mean(grad_normed, axis=-1, keepdims=True)
    second = jnp.mean(grad_normed * normed, axis=-1, keepdims=True)
    return inverse * (grad_normed - first - normed * second)


def exact_gelu(value):
    return jax.nn.gelu(value, approximate=False)


def allowed_pairs(lengths):
    place = jnp.arange(CLEN, dtype=jnp.int32)
    causal = place[None, :] <= place[:, None]
    inside = place[None, None, :] < lengths[:, None, None]
    return jnp.logical_and(causal[None], inside)


def score_pair(query_block, key_block, prompt_keys, scale):
    wide = (
        jnp.einsum("qhd,khd->hqk", query_block, prompt_keys, preferred_element_type=jnp.float32)
        * scale
    )
    grouped = query_block.reshape(
        key_block.shape[0], key_block.shape[1], query_block.shape[1], query_block.shape[2]
    )
    narrow = (
        jnp.einsum("cqhd,ckhd->hcqk", grouped, key_block, preferred_element_type=jnp.float32)
        * scale
    )
    return (wide, grouped, narrow)


def log_total(wide, narrow):
    heads = wide.shape[0]
    queries = wide.shape[1]
    top = jnp.maximum(jnp.max(wide, axis=-1), jnp.max(narrow, axis=-1).reshape(heads, queries))
    inner = top.reshape(narrow.shape[:3])
    total = jnp.sum(jnp.exp(wide - top[..., None]), axis=-1)
    total = total + jnp.sum(jnp.exp(narrow - inner[..., None]), axis=-1).reshape(heads, queries)
    return top + jnp.log(total)


def probabilities(wide, narrow, lse):
    inner = lse.reshape(narrow.shape[:3])
    return (jnp.exp(wide - lse[..., None]), jnp.exp(narrow - inner[..., None]))


def run_layer(tokens, cotangent, lengths, weights, vectors, up_bias, side):
    qkv_blocks, out_blocks, up_blocks, down_blocks = weights
    rows = tokens.shape[0]
    half = rows // 2
    width = tokens.shape[1]
    head_size = width // H
    scale = head_size ** (-0.5)
    block = min(512, rows)
    count = rows // block
    groups = block // CLEN
    is_first = side == 0
    merged = project(tokens, qkv_blocks)
    shift = jnp.concatenate([vectors[:, 0], jnp.zeros((width,), jnp.float32), vectors[:, 1]])
    qkv = (merged + shift).astype(jnp.bfloat16)
    own_pairs = qkv[:half, width:]
    partner_pairs = swapped(own_pairs, "col", 0)
    prompt_pairs = jnp.concatenate(
        [
            jnp.where(is_first, own_pairs, partner_pairs),
            jnp.where(is_first, partner_pairs, own_pairs),
        ],
        axis=0,
    )
    prompt_keys = prompt_pairs[:, :width].reshape(rows, H, head_size)
    prompt_values = prompt_pairs[:, width:].reshape(rows, H, head_size)
    query_blocks = qkv[:, :width].reshape(count, block, H, head_size)
    key_blocks = qkv[:, width : 2 * width].reshape(count, groups, CLEN, H, head_size)
    value_blocks = qkv[:, 2 * width :].reshape(count, groups, CLEN, H, head_size)
    length_blocks = lengths.reshape(count, groups)

    def forward_block(items):
        query_block, key_block, value_block, length_block = items
        wide, grouped, narrow = score_pair(query_block, key_block, prompt_keys, scale)
        narrow = jnp.where(allowed_pairs(length_block)[None], narrow, -jnp.inf)
        lse = log_total(wide, narrow)
        weight_wide, weight_narrow = probabilities(wide, narrow, lse)
        mixed = jnp.einsum(
            "hqk,khd->qhd",
            weight_wide.astype(jnp.bfloat16),
            prompt_values,
            preferred_element_type=jnp.float32,
        )
        nearby = jnp.einsum(
            "hcqk,ckhd->cqhd",
            weight_narrow.astype(jnp.bfloat16),
            value_block,
            preferred_element_type=jnp.float32,
        )
        return ((mixed + nearby.reshape(mixed.shape)).reshape(block, width), lse)

    attended, log_totals = lax.map(
        forward_block, (query_blocks, key_blocks, value_blocks, length_blocks)
    )
    attended = attended.reshape(rows, width).astype(jnp.bfloat16)
    branch = project(attended, out_blocks) + vectors[:, 2]
    first_sum = tokens.astype(jnp.float32) + branch
    first_normed, first_inverse = normalize(first_sum)
    hidden = first_normed * vectors[:, 3] + vectors[:, 4]
    hidden_low = hidden.astype(jnp.bfloat16)
    pre_act = project(hidden_low, up_blocks) + up_bias
    act_value, act_pullback = jax.vjp(exact_gelu, pre_act)
    act_low = act_value.astype(jnp.bfloat16)
    second_sum = hidden + project(act_low, down_blocks) + vectors[:, 5]
    second_normed, second_inverse = normalize(second_sum)
    result = (second_normed * vectors[:, 6] + vectors[:, 7]).astype(jnp.bfloat16)
    grad_out = cotangent.astype(jnp.float32)
    grad_second = normalize_back(grad_out * vectors[:, 6], second_normed, second_inverse)
    grad_second_low = grad_second.astype(jnp.bfloat16)
    grad_act = project_back(grad_second_low, down_blocks)
    grad_pre = act_pullback(grad_act)[0]
    grad_pre_low = grad_pre.astype(jnp.bfloat16)
    grad_hidden = grad_second + project_back(grad_pre_low, up_blocks)
    grad_first = normalize_back(grad_hidden * vectors[:, 3], first_normed, first_inverse)
    grad_first_low = grad_first.astype(jnp.bfloat16)
    grad_attended = project_back(grad_first_low, out_blocks).astype(jnp.bfloat16)
    grad_blocks = grad_attended.reshape(count, block, H, head_size)

    def backward_block(carry, items):
        sum_keys, sum_values = carry
        query_block, key_block, value_block, length_block, grad_block, lse = items
        wide, grouped, narrow = score_pair(query_block, key_block, prompt_keys, scale)
        narrow = jnp.where(allowed_pairs(length_block)[None], narrow, -jnp.inf)
        weight_wide, weight_narrow = probabilities(wide, narrow, lse)
        grad_grouped = grad_block.reshape(grouped.shape)
        dots_wide = jnp.einsum(
            "qhd,khd->hqk", grad_block, prompt_values, preferred_element_type=jnp.float32
        )
        dots_narrow = jnp.einsum(
            "cqhd,ckhd->hcqk", grad_grouped, value_block, preferred_element_type=jnp.float32
        )
        delta = jnp.sum(weight_wide * dots_wide, axis=-1)
        delta = delta + jnp.sum(weight_narrow * dots_narrow, axis=-1).reshape(delta.shape)
        inner = delta.reshape(narrow.shape[:3])
        grad_wide = (weight_wide * (dots_wide - delta[..., None])).astype(jnp.bfloat16)
        grad_narrow = (weight_narrow * (dots_narrow - inner[..., None])).astype(jnp.bfloat16)
        query_part = jnp.einsum(
            "hqk,khd->qhd", grad_wide, prompt_keys, preferred_element_type=jnp.float32
        )
        query_near = jnp.einsum(
            "hcqk,ckhd->cqhd", grad_narrow, key_block, preferred_element_type=jnp.float32
        )
        grad_query = (query_part + query_near.reshape(query_part.shape)) * scale
        key_part = (
            jnp.einsum("hqk,qhd->khd", grad_wide, query_block, preferred_element_type=jnp.float32)
            * scale
        )
        value_part = jnp.einsum(
            "hqk,qhd->khd",
            weight_wide.astype(jnp.bfloat16),
            grad_block,
            preferred_element_type=jnp.float32,
        )
        near_keys = (
            jnp.einsum("hcqk,cqhd->ckhd", grad_narrow, grouped, preferred_element_type=jnp.float32)
            * scale
        )
        near_values = jnp.einsum(
            "hcqk,cqhd->ckhd",
            weight_narrow.astype(jnp.bfloat16),
            grad_grouped,
            preferred_element_type=jnp.float32,
        )
        outputs = (
            grad_query.reshape(block, width),
            near_keys.reshape(block, width),
            near_values.reshape(block, width),
        )
        return ((sum_keys + key_part, sum_values + value_part), outputs)

    empty = jnp.zeros((rows, H, head_size), jnp.float32)
    (prompt_grad_keys, prompt_grad_values), (grad_queries, near_keys, near_values) = lax.scan(
        backward_block,
        (empty, empty),
        (query_blocks, key_blocks, value_blocks, length_blocks, grad_blocks, log_totals),
    )
    near_grads = jnp.concatenate(
        [near_keys.reshape(rows, width), near_values.reshape(rows, width)], axis=1
    )
    prompt_grads = jnp.concatenate(
        [prompt_grad_keys.reshape(rows, width), prompt_grad_values.reshape(rows, width)], axis=1
    )
    mine = jnp.where(is_first, prompt_grads[:half], prompt_grads[half:])
    theirs = jnp.where(is_first, prompt_grads[half:], prompt_grads[:half])
    received = swapped(theirs.astype(jnp.bfloat16), "col", 0).astype(theirs.dtype)
    prompt_part = jnp.concatenate(
        [mine + received, jnp.zeros((rows - half, 2 * width), jnp.float32)], axis=0
    )
    pair_grads = near_grads + prompt_part
    grad_qkv = jnp.concatenate([grad_queries.reshape(rows, width), pair_grads], axis=1)
    grad_qkv_low = grad_qkv.astype(jnp.bfloat16)
    grad_tokens = (grad_first + project_back(grad_qkv_low, qkv_blocks)).astype(jnp.bfloat16)
    vector_term = jnp.stack(
        [
            jnp.sum(grad_qkv[:, :width], axis=0),
            jnp.sum(grad_qkv[:, 2 * width :], axis=0),
            jnp.sum(grad_first, axis=0),
            jnp.sum(grad_hidden * first_normed, axis=0),
            jnp.sum(grad_hidden, axis=0),
            jnp.sum(grad_second, axis=0),
            jnp.sum(grad_out * second_normed, axis=0),
            jnp.sum(grad_out, axis=0),
        ],
        axis=1,
    )
    bias_term = jnp.sum(grad_pre, axis=0)
    terms = (
        block_grad(tokens, grad_qkv_low, qkv_blocks),
        block_grad(attended, grad_first_low, out_blocks),
        block_grad(hidden_low, grad_pre_low, up_blocks),
        block_grad(act_low, grad_second_low, down_blocks),
        vector_term,
        bias_term,
    )
    return (result, grad_tokens, terms)


def local(
    inputs,
    qkv_weight,
    out_weight,
    up_weight,
    down_weight,
    vectors,
    up_bias,
    cont_lengths,
    out_cotangent,
):
    grid_rows = lax.axis_size("row")
    grid_cols = lax.axis_size("col")
    grid_size = grid_rows * grid_cols
    place = lax.axis_index("col")
    side = place % 2
    rows = inputs.shape[1]
    half_conts = cont_lengths.shape[2] // 2
    group_lengths = lax.dynamic_index_in_dim(cont_lengths, place // 2, 1, keepdims=False)
    own_lengths = lax.dynamic_slice_in_dim(group_lengths, side * half_conts, half_conts, 1)
    prompt_slots = jnp.zeros((inputs.shape[0], rows // 2 // CLEN), jnp.int32)
    device_lengths = jnp.concatenate([prompt_slots, own_lengths], axis=1)
    own_blocks = (qkv_weight, out_weight, up_weight, down_weight)
    flat_qkv = qkv_weight.reshape(1, -1)
    flat_out = out_weight.reshape(1, -1)
    flat_up = up_weight.reshape(1, -1)
    flat_down = down_weight.reshape(1, -1)
    term_widths = (
        qkv_weight.size,
        out_weight.size,
        up_weight.size,
        down_weight.size,
        vectors.size // grid_size,
        up_bias.size // grid_size,
    )

    def arrange(gathered):
        return tuple(
            (
                whole.reshape(grid_rows, grid_cols, part.shape[0], part.shape[1])
                for whole, part in zip(gathered, own_blocks)
            )
        )

    def spread(terms):
        return terms[:4] + (terms[4].reshape(grid_size, -1), terms[5].reshape(grid_size, -1))

    def layer_step(weights, items):
        tokens, cotangent, lengths = items
        return run_layer(tokens, cotangent, lengths, weights, vectors, up_bias, side)

    def fresh_step(carry, items):
        gathered = (
            lax.all_gather(flat_qkv, ("row", "col"), axis=0, tiled=True),
            lax.all_gather(flat_out, ("row", "col"), axis=0, tiled=True),
            lax.all_gather(flat_up, ("row", "col"), axis=0, tiled=True),
            lax.all_gather(flat_down, ("row", "col"), axis=0, tiled=True),
        )
        result, grad_tokens, terms = layer_step(arrange(gathered), items)
        terms = spread(terms)
        pieces = (
            lax.psum_scatter(terms[0], ("row", "col"), scatter_dimension=0, tiled=True),
            lax.psum_scatter(terms[1], ("row", "col"), scatter_dimension=0, tiled=True),
            lax.psum_scatter(terms[2], ("row", "col"), scatter_dimension=0, tiled=True),
            lax.psum_scatter(terms[3], ("row", "col"), scatter_dimension=0, tiled=True),
            lax.psum_scatter(terms[4], ("row", "col"), scatter_dimension=0, tiled=True),
            lax.psum_scatter(terms[5], ("row", "col"), scatter_dimension=0, tiled=True),
        )
        return (
            tuple((total + piece for total, piece in zip(carry, pieces))),
            (result, grad_tokens),
        )

    start = tuple((jnp.zeros((1, columns), jnp.float32) for columns in term_widths))
    summed, (results, grad_inputs) = lax.scan(
        fresh_step, start, (inputs, out_cotangent, device_lengths)
    )
    combined = (
        lax.psum(summed[0].astype(jnp.bfloat16), "dp").astype(jnp.float32),
        lax.psum(summed[1].astype(jnp.bfloat16), "dp").astype(jnp.float32),
        lax.psum(summed[2].astype(jnp.bfloat16), "dp").astype(jnp.float32),
        lax.psum(summed[3].astype(jnp.bfloat16), "dp").astype(jnp.float32),
        lax.psum(summed[4].astype(jnp.bfloat16), "dp").astype(jnp.float32),
        lax.psum(summed[5].astype(jnp.bfloat16), "dp").astype(jnp.float32),
    )
    final_shapes = (
        qkv_weight.shape,
        out_weight.shape,
        up_weight.shape,
        down_weight.shape,
        (vectors.shape[0] // grid_size, vectors.shape[1]),
        (up_bias.shape[0] // grid_size,),
    )
    grads = tuple((piece.reshape(target) for piece, target in zip(combined, final_shapes)))
    return (results, grad_inputs, grads[0], grads[1], grads[2], grads[3], grads[4], grads[5])


def solution(mesh):
    return jax.shard_map(
        local,
        mesh=mesh,
        in_specs=(
            P(None, ("dp", "row", "col"), None),
            P("row", "col"),
            P("row", "col"),
            P("row", "col"),
            P("row", "col"),
            P(),
            P(),
            P(None, ("dp", "row"), None),
            P(None, ("dp", "row", "col"), None),
        ),
        out_specs=(
            P(None, ("dp", "row", "col"), None),
            P(None, ("dp", "row", "col"), None),
            P("row", "col"),
            P("row", "col"),
            P("row", "col"),
            P("row", "col"),
            P(("row", "col"), None),
            P(("row", "col")),
        ),
        check_vma=False,
    )
```

profile of v0, /device:TPU:8, one launch (start us, length us, event | category | flops | bytes accessed | tf_op | source)
XLA Modules:
  0.0 2557.7 jit_solution(18114576951347129066)
XLA Ops:
  16.2 2424.0 %while.89 = (s32[]{:T(128)}, f32[1,221184]{1,0:T(1,128)}, f32[1,73728]{1,0:T(1,128)}, f32[1,294912]{1,0:T(1,128)}, f32[1,294912]{1,0:T(1,128)}, /*index=5*/f32[1...) while((s32[]{:T(128)}, f32[1,221184]{1,0:T(1,128)}, ...), condition=%wide.region_34.35_spmd.clone.clone, body=%wide.region_0.34_spmd.clone.sunk.clone | while | flops 50343448576 | bytes 1685835264 | solution.py:346
  23.7 45.5 %all-gather.25.cloned.1.call-done = bf16[8,1,221184]{2,1,0:T(2,128)(2,1)} async-done(((bf16[1,1,221184]{2,1,0:T(2,128)(2,1)}), bf16[8,1,221184]{2,1,0:T(2,128)(2,1)}) %all-gather.25.cloned.1.call-update) | async-done | bytes 3538960 | tf_op jit(solution)/shard_map/while/body/eval_jaxpr/all_gather | solution.py:325
  69.1 62.4 %reduce.52 = bf16[8,221184]{1,0:T(8,128)(2,1)S(1)} reduce(bf16[8,1,221184]{2,1,0:T(2,128)(2,1)} %all-gather.25.cloned.1.call-done, bf16[]{:T(256)} %constant.463..sunk.1), dimensions={1}, to_apply=%all-gather.4.reduce_sub_computation | reduce | bytes 7077890 | tf_op jit(solution)/shard_map/while/body/eval_jaxpr/all_gather | solution.py:325
  182.1 15.9 collective-permute-done
  204.5 97.1 %while.87 = (s32[]{:T(128)}, bf16[2,512,768]{1,2,0:T(8,128)(2,1)}, f32[2,12,512]{2,1,0:T(8,128)S(1)}, bf16[2,512,12,64]{1,3,2,0:T(8,128)(2,1)}, bf16[1024,12,64]...) while((s32[]{:T(128)}, bf16[2,512,768]{1,2,0:T(8,128)(2,1)}, ...), condition=%wide.region_6.6_spmd, body=%wide.region_1.5_spmd.sunk | while | flops 1871821312 | bytes 106039504 | solution.py:146
  213.3 10.3 multiply_reduce_fusion.17
  226.3 11.0 exponential_reduce_fusion.4
  241.6 10.6 bitcast_add_fusion.14
  261.9 10.1 multiply_reduce_fusion.17
  274.8 11.0 exponential_reduce_fusion.4
  290.0 10.6 bitcast_add_fusion.14
  322.1 29.5 %reduce.55 = bf16[8,294912]{1,0:T(8,128)(2,1)} reduce(bf16[8,1,294912]{2,1,0:T(2,128)(2,1)} %all-gather.31.cloned.1.call-done, bf16[]{:T(256)} %constant.463..sunk.1), dimensions={1}, to_apply=%all-gather.7.reduce_sub_computation | reduce | bytes 9437186 | tf_op jit(solution)/shard_map/while/body/eval_jaxpr/all_gather | solution.py:328
  363.8 29.5 %reduce.54 = bf16[8,294912]{1,0:T(8,128)(2,1)} reduce(bf16[8,1,294912]{2,1,0:T(2,128)(2,1)} %all-gather.29.cloned.1.call-done, bf16[]{:T(256)} %constant.463..sunk.1), dimensions={1}, to_apply=%all-gather.6.reduce_sub_computation | reduce | bytes 9437186 | tf_op jit(solution)/shard_map/while/body/eval_jaxpr/all_gather | solution.py:327
  398.6 37.0 %multiply_convert_fusion.7 = (bf16[1024,3072]{1,0:T(8,128)(2,1)}, f32[1024,3072]{1,0:T(8,128)}, f32[1024,3072,1]{1,0,2:T(8,128)}) fusion(f32[3072]{0:T(1024)S(1)} %copy-done.84, bf16[1024,4,192]{0,2,1:T(8,128)(2,1)S(1)} %bitcast.775, bf16[3072,192,4]{0,1,2:T(8,128)(2,1)S(1)} %bitcast.755), kind=kOutput, calls=%fused_computation.95.clone.1.clone | convolution fusion | flops 5039456256 | bytes 37761024 | tf_op jit(solution)/shard_map/while/body/eval_jaxpr/tri,rcio->tco/dot_general | solution.py:22
  455.2 18.1 fusion.322
  473.4 15.4 reshape.694
  488.8 12.8 multiply_reduce_fusion.22
  512.8 245.6 %while.88 = (s32[]{:T(128)}, f32[1024,12,64]{0,2,1:T(8,128)}, f32[1024,12,64]{0,2,1:T(8,128)}, f32[2,512,768]{1,2,0:T(8,128)}, f32[2,512,768]{2,1,0:T(8,128)}, /...) while((s32[]{:T(128)}, f32[1024,12,64]{0,2,1:T(8,128)}, ...), condition=%wide.region_18.18_spmd.clone, body=%wide.region_15.17_spmd.clone.sunk | while | flops 4617617920 | bytes 352365696 | solution.py:226
  526.1 10.1 fusion.286
  536.2 16.8 multiply_reduce_fusion.18
  579.1 21.6 multiply_convert_fusion.6
  622.0 12.7 bitcast_add_fusion.16
  647.8 10.1 fusion.286
  657.9 16.8 multiply_reduce_fusion.18
  700.7 21.6 multiply_convert_fusion.6
  744.5 13.6 bitcast_add_fusion.16
  772.1 10.2 fusion.327
  792.0 12.9 copy.497
  837.9 10.3 convert_element_type.280
  886.7 26.4 %all-reduce.17 = (f32[8,768]{1,0:T(8,128)S(1)}, f32[8,384]{1,0:T(8,128)S(1)}) all-reduce(f32[8,768]{1,0:T(8,128)S(1)} %reshape.695, f32[8,384]{1,0:T(8,128)S(1)} %reshape.696), channel_id=6, replica_groups=mesh['dp'=4,'row'=4,'col'=2] {'row','col'}, use_global_device_ids=true, to_apply=%region_31.31.clone | all-reduce | flops 9216 | bytes 73728 | tf_op jit(solution)/shard_map/while
  915.7 290.4 %all-reduce.23.cloned.1.call-done = (f32[8,221184]{1,0:T(8,128)}, f32[8,73728]{1,0:T(8,128)}, f32[8,294912]{1,0:T(8,128)}, f32[8,294912]{1,0:T(8,128)}) async-done(((f32[8,221184]{1,0:T(8,128)}, f32[8,73728]{1,0:T(8,128)}, f32[8,294912]{1,0:T(8,128)}, f32[8,294912]{1,0:T(8,128)}), (f32[8,221184]{1,0:T(8,128)}, f32[8,73728]{1,0:T(8,128)}, f32[8,294912]{1,0:T(8,128)}, ...) | async-done | bytes 28311568 | tf_op jit(solution)/shard_map/while
  1231.8 44.3 %all-gather.25.cloned.1.call-done = bf16[8,1,221184]{2,1,0:T(2,128)(2,1)} async-done(((bf16[1,1,221184]{2,1,0:T(2,128)(2,1)}), bf16[8,1,221184]{2,1,0:T(2,128)(2,1)}) %all-gather.25.cloned.1.call-update) | async-done | bytes 3538960 | tf_op jit(solution)/shard_map/while/body/eval_jaxpr/all_gather | solution.py:325
  1276.1 62.4 %reduce.52 = bf16[8,221184]{1,0:T(8,128)(2,1)S(1)} reduce(bf16[8,1,221184]{2,1,0:T(2,128)(2,1)} %all-gather.25.cloned.1.call-done, bf16[]{:T(256)} %constant.463..sunk.1), dimensions={1}, to_apply=%all-gather.4.reduce_sub_computation | reduce | bytes 7077890 | tf_op jit(solution)/shard_map/while/body/eval_jaxpr/all_gather | solution.py:325
  1389.0 15.8 collective-permute-done
  1411.2 97.1 %while.87 = (s32[]{:T(128)}, bf16[2,512,768]{1,2,0:T(8,128)(2,1)}, f32[2,12,512]{2,1,0:T(8,128)S(1)}, bf16[2,512,12,64]{1,3,2,0:T(8,128)(2,1)}, bf16[1024,12,64]...) while((s32[]{:T(128)}, bf16[2,512,768]{1,2,0:T(8,128)(2,1)}, ...), condition=%wide.region_6.6_spmd, body=%wide.region_1.5_spmd.sunk | while | flops 1871821312 | bytes 106039504 | solution.py:146
  1420.0 10.3 multiply_reduce_fusion.17
  1433.1 11.0 exponential_reduce_fusion.4
  1448.4 10.6 bitcast_add_fusion.14
  1468.7 10.1 multiply_reduce_fusion.17
  1481.5 11.0 exponential_reduce_fusion.4
  1496.8 10.6 bitcast_add_fusion.14
  1528.9 29.5 %reduce.55 = bf16[8,294912]{1,0:T(8,128)(2,1)} reduce(bf16[8,1,294912]{2,1,0:T(2,128)(2,1)} %all-gather.31.cloned.1.call-done, bf16[]{:T(256)} %constant.463..sunk.1), dimensions={1}, to_apply=%all-gather.7.reduce_sub_computation | reduce | bytes 9437186 | tf_op jit(solution)/shard_map/while/body/eval_jaxpr/all_gather | solution.py:328
  1570.6 29.5 %reduce.54 = bf16[8,294912]{1,0:T(8,128)(2,1)} reduce(bf16[8,1,294912]{2,1,0:T(2,128)(2,1)} %all-gather.29.cloned.1.call-done, bf16[]{:T(256)} %constant.463..sunk.1), dimensions={1}, to_apply=%all-gather.6.reduce_sub_computation | reduce | bytes 9437186 | tf_op jit(solution)/shard_map/while/body/eval_jaxpr/all_gather | solution.py:327
  1605.4 37.0 %multiply_convert_fusion.7 = (bf16[1024,3072]{1,0:T(8,128)(2,1)}, f32[1024,3072]{1,0:T(8,128)}, f32[1024,3072,1]{1,0,2:T(8,128)}) fusion(f32[3072]{0:T(1024)S(1)} %copy-done.84, bf16[1024,4,192]{0,2,1:T(8,128)(2,1)S(1)} %bitcast.775, bf16[3072,192,4]{0,1,2:T(8,128)(2,1)S(1)} %bitcast.755), kind=kOutput, calls=%fused_computation.95.clone.1.clone | convolution fusion | flops 5039456256 | bytes 37761024 | tf_op jit(solution)/shard_map/while/body/eval_jaxpr/tri,rcio->tco/dot_general | solution.py:22
  1662.0 18.1 fusion.322
  1680.2 15.4 reshape.694
  1695.6 12.8 multiply_reduce_fusion.22
  1719.6 245.6 %while.88 = (s32[]{:T(128)}, f32[1024,12,64]{0,2,1:T(8,128)}, f32[1024,12,64]{0,2,1:T(8,128)}, f32[2,512,768]{1,2,0:T(8,128)}, f32[2,512,768]{2,1,0:T(8,128)}, /...) while((s32[]{:T(128)}, f32[1024,12,64]{0,2,1:T(8,128)}, ...), condition=%wide.region_18.18_spmd.clone, body=%wide.region_15.17_spmd.clone.sunk | while | flops 4617617920 | bytes 352365696 | solution.py:226
  1732.9 10.1 fusion.286
  1743.0 16.8 multiply_reduce_fusion.18
  1785.8 21.6 multiply_convert_fusion.6
  1828.8 12.7 bitcast_add_fusion.16
  1854.6 10.1 fusion.286
  1864.7 16.8 multiply_reduce_fusion.18
  1907.5 21.6 multiply_convert_fusion.6
  1951.3 13.6 bitcast_add_fusion.16
  1979.0 10.2 fusion.327
  1998.9 12.9 copy.497
  2044.8 10.3 convert_element_type.280
  2093.6 26.1 %all-reduce.17 = (f32[8,768]{1,0:T(8,128)S(1)}, f32[8,384]{1,0:T(8,128)S(1)}) all-reduce(f32[8,768]{1,0:T(8,128)S(1)} %reshape.695, f32[8,384]{1,0:T(8,128)S(1)} %reshape.696), channel_id=6, replica_groups=mesh['dp'=4,'row'=4,'col'=2] {'row','col'}, use_global_device_ids=true, to_apply=%region_31.31.clone | all-reduce | flops 9216 | bytes 73728 | tf_op jit(solution)/shard_map/while
  2122.3 290.5 %all-reduce.23.cloned.1.call-done = (f32[8,221184]{1,0:T(8,128)}, f32[8,73728]{1,0:T(8,128)}, f32[8,294912]{1,0:T(8,128)}, f32[8,294912]{1,0:T(8,128)}) async-done(((f32[8,221184]{1,0:T(8,128)}, f32[8,73728]{1,0:T(8,128)}, f32[8,294912]{1,0:T(8,128)}, f32[8,294912]{1,0:T(8,128)}), (f32[8,221184]{1,0:T(8,128)}, f32[8,73728]{1,0:T(8,128)}, f32[8,294912]{1,0:T(8,128)}, ...) | async-done | bytes 28311568 | tf_op jit(solution)/shard_map/while
  2440.3 13.6 convert_reduce_fusion.1
  2468.7 17.2 all-reduce.10
  2487.2 56.7 %all-reduce.21.cloned.1.call-done = (bf16[192,1152]{1,0:T(8,128)(2,1)}, bf16[192,384]{1,0:T(8,128)(2,1)}, bf16[192,1536]{1,0:T(8,128)(2,1)}, bf16[768,384]{1,0:T(8,128)(2,1)}) async-done(((bf16[192,1152]{1,0:T(8,128)(2,1)}, bf16[192,384]{1,0:T(8,128)(2,1)}, bf16[192,1536]{1,0:T(8,128)(2,1)}, bf16[768,384]{1,0:T(8,128)(2,1)}), (bf16[192,1152]{1,0:T(8,128)(2,1)}, bf16[192,384]{1,0:T(8,128)(2,1)}, ...) | async-done | bytes 1769488 | tf_op jit(solution)/shard_map/psum | solution.py:350
  (925 shorter events, 835.8 us)
Async XLA Ops:
  16.5 52.6 %all-gather.25.cloned.1.call-start = ((), (), s32[]{:S(2)}) async-start(), calls=%async_computation.1 | async-start | bytes 7962624 | tf_op jit(solution)/shard_map/while/body/eval_jaxpr/all_gather | solution.py:325
  17.3 131.1 %all-gather.27.cloned.1.call-start = ((), (), s32[]{:S(2)}) async-start(), calls=%async_computation.2 | async-start | bytes 2654208 | tf_op jit(solution)/shard_map/while/body/eval_jaxpr/all_gather | solution.py:326
  18.0 304.1 %all-gather.31.cloned.1.call-start = ((), (), s32[]{:S(2)}) async-start(), calls=%async_computation.4 | async-start | bytes 10616832 | tf_op jit(solution)/shard_map/while/body/eval_jaxpr/all_gather | solution.py:328
  18.8 345.1 %all-gather.29.cloned.1.call-start = ((), (), s32[]{:S(2)}) async-start(), calls=%async_computation.3 | async-start | bytes 10616832 | tf_op jit(solution)/shard_map/while/body/eval_jaxpr/all_gather | solution.py:327
  142.3 55.7 %collective-permute-start = (bf16[512,1536]{1,0:T(8,128)(2,1)}, bf16[512,1536]{1,0:T(8,128)(2,1)}, u32[]{:S(2)}, u32[]{:S(2)}) collective-permute-start(bf16[512,1536]{1,0:T(8,128)(2,1)} %slice.181), channel_id=1, source_target_pairs={{0,1},{1,0},{2,3},{3,2},{4,5},{5,4},{6,7},{7,6},{8,9},{9,8},{10,11... | collective-permute-start | bytes 4718600 | tf_op jit(solution)/shard_map/while/body/eval_jaxpr/ppermute | solution.py:16
  143.6 1062.5 %all-reduce.23.cloned.1.call-start = ((), (), s32[]{:S(2)}) async-start(), calls=%async_computation.5 | async-start | bytes 56623104 | tf_op jit(solution)/shard_map/while
  397.2 38.4 %slice-start.2 = ((s8[4718592]{0:T(1024)(128)(4,1)}), s8[4194304]{0:T(1024)(128)(4,1)S(1)}, s32[]{:S(2)}) async-start(s8[4718592]{0:T(1024)(128)(4,1)} %bitcast.751), calls=%async_computation.8 | async-start | bytes 8388608 | tf_op jit(solution)/shard_map/while
  398.6 37.0 %copy-start.21 = (f32[1024,768]{0,1:T(8,128)S(1)}, f32[1024,768]{0,1:T(8,128)}, u32[]{:S(2)}) copy-start(f32[1024,768]{0,1:T(8,128)} %copy-done.20) | copy-start | bytes 9437188 | tf_op jit(solution)/shard_map/while
  398.6 37.0 %slice-start.3 = ((s8[4718592]{0:T(1024)(128)(4,1)}), s8[524288]{0:T(1024)(128)(4,1)S(1)}, s32[]{:S(2)}) async-start(s8[4718592]{0:T(1024)(128)(4,1)} %bitcast.751), calls=%async_computation.9 | async-start | bytes 1048576 | tf_op jit(solution)/shard_map/while
  398.6 37.0 %copy-start.57 = (f32[1024]{0:T(1024)S(1)}, f32[1024]{0:T(1024)}, u32[]{:S(2)}) copy-start(f32[1024]{0:T(1024)} %copy-done.56) | copy-start | bytes 12292 | tf_op jit(solution)/shard_map/while
  398.6 37.0 %copy-start.59 = (f32[768]{0:T(1024)S(1)}, f32[768]{0:T(1024)}, u32[]{:S(2)}) copy-start(f32[768]{0:T(1024)} %get-tuple-element.1269) | copy-start | bytes 9220 | tf_op jit(solution)/shard_map/while
  398.6 37.0 %copy-start.61 = (f32[1024]{0:T(1024)S(1)}, f32[1024]{0:T(1024)}, u32[]{:S(2)}) copy-start(f32[1024]{0:T(1024)} %copy-done.60) | copy-start | bytes 12292 | tf_op jit(solution)/shard_map/while
  398.6 37.0 %copy-start.67 = (f32[768]{0:T(1024)S(1)}, f32[768]{0:T(1024)}, u32[]{:S(2)}) copy-start(f32[768]{0:T(1024)} %get-tuple-element.1270) | copy-start | bytes 9220 | tf_op jit(solution)/shard_map/while
  398.6 37.0 %copy-start.76 = (f32[768]{0:T(1024)S(1)}, f32[768]{0:T(1024)}, u32[]{:S(2)}) copy-start(f32[768]{0:T(1024)} %get-tuple-element.1272) | copy-start | bytes 9220 | tf_op jit(solution)/shard_map/while
  435.6 11.1 slice-start
  435.7 11.0 slice-start.1
  455.2 18.1 copy-start.47
  579.1 21.6 copy-start.4
  622.0 12.7 copy-start.27
  700.7 21.6 copy-start.4
  744.5 13.6 copy-start.27
  769.1 57.7 %collective-permute-start.1 = (bf16[512,1536]{1,0:T(8,128)(2,1)}, bf16[512,1536]{1,0:T(8,128)(2,1)}, u32[]{:S(2)}, u32[]{:S(2)}) collective-permute-start(bf16[512,1536]{1,0:T(8,128)(2,1)} %select_convert_fusion.3), channel_id=1, source_target_pairs={{0,1},{1,0},{2,3},{3,2},{4,5},{5,4},{6,7},{7,6},{8,9},{9,8},{10,11... | collective-permute-start | bytes 4718600 | tf_op jit(solution)/shard_map/while/body/eval_jaxpr/ppermute | solution.py:16
  792.0 12.9 copy-start.44
  884.1 30.3 %copy-start.80 = (f32[1,384]{1,0:T(1,128)S(1)}, f32[1,384]{1,0:T(1,128)}, u32[]{:S(2)}) copy-start(f32[1,384]{1,0:T(1,128)} %get-tuple-element.1465) | copy-start | bytes 4612 | tf_op jit(solution)/shard_map/while
  884.1 30.9 %copy-start.73 = (f32[1,768]{1,0:T(1,128)S(1)}, f32[1,768]{1,0:T(1,128)}, u32[]{:S(2)}) copy-start(f32[1,768]{1,0:T(1,128)} %get-tuple-element.1464) | copy-start | bytes 9220 | tf_op jit(solution)/shard_map/while
  886.5 324.6 %copy-start.53 = (f32[1,73728]{1,0:T(1,128)S(1)}, f32[1,73728]{1,0:T(1,128)}, u32[]{:S(2)}) copy-start(f32[1,73728]{1,0:T(1,128)} %get-tuple-element.1461) | copy-start | bytes 884740 | tf_op jit(solution)/shard_map/while
  913.1 300.7 %copy-start.36 = (f32[1,294912]{1,0:T(1,128)S(1)}, f32[1,294912]{1,0:T(1,128)}, u32[]{:S(2)}) copy-start(f32[1,294912]{1,0:T(1,128)} %get-tuple-element.1462) | copy-start | bytes 3538948 | tf_op jit(solution)/shard_map/while
  915.0 308.6 %copy-start.81 = (f32[1,384]{1,0:T(1,128)}, f32[1,384]{1,0:T(1,128)S(1)}, u32[]{:S(2)}) copy-start(f32[1,384]{1,0:T(1,128)S(1)} %fusion.332) | copy-start | bytes 4612 | tf_op jit(solution)/shard_map/while
  915.7 307.9 %copy-start.74 = (f32[1,768]{1,0:T(1,128)}, f32[1,768]{1,0:T(1,128)S(1)}, u32[]{:S(2)}) copy-start(f32[1,768]{1,0:T(1,128)S(1)} %fusion.331) | copy-start | bytes 9220 | tf_op jit(solution)/shard_map/while
  1224.8 51.2 %all-gather.25.cloned.1.call-start = ((), (), s32[]{:S(2)}) async-start(), calls=%async_computation.1 | async-start | bytes 7962624 | tf_op jit(solution)/shard_map/while/body/eval_jaxpr/all_gather | solution.py:325
  1225.4 129.9 %all-gather.27.cloned.1.call-start = ((), (), s32[]{:S(2)}) async-start(), calls=%async_computation.2 | async-start | bytes 2654208 | tf_op jit(solution)/shard_map/while/body/eval_jaxpr/all_gather | solution.py:326
  1226.1 302.7 %all-gather.31.cloned.1.call-start = ((), (), s32[]{:S(2)}) async-start(), calls=%async_computation.4 | async-start | bytes 10616832 | tf_op jit(solution)/shard_map/while/body/eval_jaxpr/all_gather | solution.py:328
  1226.9 343.7 %all-gather.29.cloned.1.call-start = ((), (), s32[]{:S(2)}) async-start(), calls=%async_computation.3 | async-start | bytes 10616832 | tf_op jit(solution)/shard_map/while/body/eval_jaxpr/all_gather | solution.py:327
  1349.2 55.6 %collective-permute-start = (bf16[512,1536]{1,0:T(8,128)(2,1)}, bf16[512,1536]{1,0:T(8,128)(2,1)}, u32[]{:S(2)}, u32[]{:S(2)}) collective-permute-start(bf16[512,1536]{1,0:T(8,128)(2,1)} %slice.181), channel_id=1, source_target_pairs={{0,1},{1,0},{2,3},{3,2},{4,5},{5,4},{6,7},{7,6},{8,9},{9,8},{10,11... | collective-permute-start | bytes 4718600 | tf_op jit(solution)/shard_map/while/body/eval_jaxpr/ppermute | solution.py:16
  1350.5 1062.4 %all-reduce.23.cloned.1.call-start = ((), (), s32[]{:S(2)}) async-start(), calls=%async_computation.5 | async-start | bytes 56623104 | tf_op jit(solution)/shard_map/while
  1603.9 38.4 %slice-start.2 = ((s8[4718592]{0:T(1024)(128)(4,1)}), s8[4194304]{0:T(1024)(128)(4,1)S(1)}, s32[]{:S(2)}) async-start(s8[4718592]{0:T(1024)(128)(4,1)} %bitcast.751), calls=%async_computation.8 | async-start | bytes 8388608 | tf_op jit(solution)/shard_map/while
  1605.3 37.0 %copy-start.21 = (f32[1024,768]{0,1:T(8,128)S(1)}, f32[1024,768]{0,1:T(8,128)}, u32[]{:S(2)}) copy-start(f32[1024,768]{0,1:T(8,128)} %copy-done.20) | copy-start | bytes 9437188 | tf_op jit(solution)/shard_map/while
  1605.3 37.0 %slice-start.3 = ((s8[4718592]{0:T(1024)(128)(4,1)}), s8[524288]{0:T(1024)(128)(4,1)S(1)}, s32[]{:S(2)}) async-start(s8[4718592]{0:T(1024)(128)(4,1)} %bitcast.751), calls=%async_computation.9 | async-start | bytes 1048576 | tf_op jit(solution)/shard_map/while
  1605.3 37.0 %copy-start.57 = (f32[1024]{0:T(1024)S(1)}, f32[1024]{0:T(1024)}, u32[]{:S(2)}) copy-start(f32[1024]{0:T(1024)} %copy-done.56) | copy-start | bytes 12292 | tf_op jit(solution)/shard_map/while
  1605.3 37.0 %copy-start.59 = (f32[768]{0:T(1024)S(1)}, f32[768]{0:T(1024)}, u32[]{:S(2)}) copy-start(f32[768]{0:T(1024)} %get-tuple-element.1269) | copy-start | bytes 9220 | tf_op jit(solution)/shard_map/while
  1605.3 37.0 %copy-start.61 = (f32[1024]{0:T(1024)S(1)}, f32[1024]{0:T(1024)}, u32[]{:S(2)}) copy-start(f32[1024]{0:T(1024)} %copy-done.60) | copy-start | bytes 12292 | tf_op jit(solution)/shard_map/while
  1605.4 37.0 %copy-start.67 = (f32[768]{0:T(1024)S(1)}, f32[768]{0:T(1024)}, u32[]{:S(2)}) copy-start(f32[768]{0:T(1024)} %get-tuple-element.1270) | copy-start | bytes 9220 | tf_op jit(solution)/shard_map/while
  1605.4 37.0 %copy-start.76 = (f32[768]{0:T(1024)S(1)}, f32[768]{0:T(1024)}, u32[]{:S(2)}) copy-start(f32[768]{0:T(1024)} %get-tuple-element.1272) | copy-start | bytes 9220 | tf_op jit(solution)/shard_map/while
  1642.3 11.1 slice-start
  1642.4 11.0 slice-start.1
  1662.0 18.1 copy-start.47
  1785.8 21.6 copy-start.4
  1828.8 12.7 copy-start.27
  1907.5 21.6 copy-start.4
  1951.3 13.6 copy-start.27
  1975.8 57.8 %collective-permute-start.1 = (bf16[512,1536]{1,0:T(8,128)(2,1)}, bf16[512,1536]{1,0:T(8,128)(2,1)}, u32[]{:S(2)}, u32[]{:S(2)}) collective-permute-start(bf16[512,1536]{1,0:T(8,128)(2,1)} %select_convert_fusion.3), channel_id=1, source_target_pairs={{0,1},{1,0},{2,3},{3,2},{4,5},{5,4},{6,7},{7,6},{8,9},{9,8},{10,11... | collective-permute-start | bytes 4718600 | tf_op jit(solution)/shard_map/while/body/eval_jaxpr/ppermute | solution.py:16
  1998.9 12.9 copy-start.44
  2091.0 30.0 %copy-start.80 = (f32[1,384]{1,0:T(1,128)S(1)}, f32[1,384]{1,0:T(1,128)}, u32[]{:S(2)}) copy-start(f32[1,384]{1,0:T(1,128)} %get-tuple-element.1465) | copy-start | bytes 4612 | tf_op jit(solution)/shard_map/while
  2091.0 30.6 %copy-start.73 = (f32[1,768]{1,0:T(1,128)S(1)}, f32[1,768]{1,0:T(1,128)}, u32[]{:S(2)}) copy-start(f32[1,768]{1,0:T(1,128)} %get-tuple-element.1464) | copy-start | bytes 9220 | tf_op jit(solution)/shard_map/while
  2093.4 324.8 %copy-start.53 = (f32[1,73728]{1,0:T(1,128)S(1)}, f32[1,73728]{1,0:T(1,128)}, u32[]{:S(2)}) copy-start(f32[1,73728]{1,0:T(1,128)} %get-tuple-element.1461) | copy-start | bytes 884740 | tf_op jit(solution)/shard_map/while
  2119.7 301.1 %copy-start.36 = (f32[1,294912]{1,0:T(1,128)S(1)}, f32[1,294912]{1,0:T(1,128)}, u32[]{:S(2)}) copy-start(f32[1,294912]{1,0:T(1,128)} %get-tuple-element.1462) | copy-start | bytes 3538948 | tf_op jit(solution)/shard_map/while
  2121.6 309.1 %copy-start.81 = (f32[1,384]{1,0:T(1,128)}, f32[1,384]{1,0:T(1,128)S(1)}, u32[]{:S(2)}) copy-start(f32[1,384]{1,0:T(1,128)S(1)} %fusion.332) | copy-start | bytes 4612 | tf_op jit(solution)/shard_map/while
  2122.3 308.4 %copy-start.74 = (f32[1,768]{1,0:T(1,128)}, f32[1,768]{1,0:T(1,128)S(1)}, u32[]{:S(2)}) copy-start(f32[1,768]{1,0:T(1,128)S(1)} %fusion.331) | copy-start | bytes 9220 | tf_op jit(solution)/shard_map/while
  2440.2 16.3 copy-start.49
  2440.2 103.6 %all-reduce.21.cloned.1.call-start = ((), (), s32[]{:S(2)}) async-start(), calls=%async_computation | async-start | bytes 3538944 | tf_op jit(solution)/shard_map/psum | solution.py:350
  2453.9 13.1 copy-start.55
  2455.4 13.1 copy-start.75
  2455.4 13.2 copy-start.82
  2468.5 81.5 %copy-start.1 = (s32[2,1,8]{2,1,0:T(1,128)S(1)}, s32[2,1,8]{2,1,0:T(1,128)}, u32[]{:S(2)}) copy-start(s32[2,1,8]{2,1,0:T(1,128)} %param.22) | copy-start | bytes 196
  (155 other events, 661.5 us)
Sparse Core Ops, SparseCore 0:
  19.2 49.8 all-gather.24
  71.0 28.8 all-gather.26
  101.8 71.8 all-gather.30
  175.4 64.2 all-gather.28
  862.3 343.6 all-reduce.22
  1227.2 48.8 all-gather.24
  1277.9 28.8 all-gather.26
  1308.7 71.8 all-gather.30
  1382.5 64.1 all-gather.28
  2069.2 343.5 all-reduce.22
Sparse Core Ops, SparseCore 1:
  2468.6 75.2 all-reduce.20
where the time goes:
time: 2570 us; the launch traced here: 2560 us
  waiting for transfers between devices  763 us (30%)
  matrix products  621 us (24%)
  other arithmetic  558 us (22%)
  local copies, waits for them, and re-layouts  511 us (20%)
  blocking collectives  69.8 us (3%)
    while x12, waiting for transfers between devices  585 us
    all_gather x2, other arithmetic, fresh_step(): lax.all_gather(flat_qkv, ('row', 'col'), axis=0, tiled=True)  125 us
    while x434, local copies, waits for them, and re-layouts  121 us
    dot_general x8, matrix products, project(): jnp.einsum('tri,rcio->tco', shaped, blocks, preferred_element_type=jnp.fl...  105 us
    all_gather x2, waiting for transfers between devices, fresh_step(): lax.all_gather(flat_qkv, ('row', 'col'), axis=0, tiled=True)  89.7 us
    convert_element_type x4, other arithmetic, backward_block(): (weight_wide * (dots_wide - delta[..., None])).astype(jnp.bfloat16)  86.5 us
    dot_general x8, matrix products, project_back(): jnp.einsum('tco,rcio->tri', shaped, blocks, preferred_element_type=jnp.fl...  82 us
    dot_general x8, matrix products, score_pair(): jnp.einsum('qhd,khd->hqk', query_block, prompt_keys, preferred_element_ty...  81.1 us
  transfers between devices with their start and end apart: 15, of which 7 were waited for; matrix products, arithmetic and copies ran while one was open for 28% of the time, Pallas kernels for 0%

commit v1 on v0

v1 whole, which is shorter than its diff:
```python
import functools
import math

import jax
import jax.numpy as jnp
from jax import lax
from jax.experimental import pallas as pl
from jax.experimental.pallas import tpu as pltpu
from jax.sharding import PartitionSpec as P

H = 12
CLEN = 128
LANES = 128
EPSILON = 1e-05
LOG2E = math.log2(math.e)
LOW = jnp.bfloat16
FULL = jnp.float32
cat = jnp.concatenate


def nt(left, right):
    return lax.dot_general(left, right, (((1,), (1,)), ((), ())), preferred_element_type=FULL)


def nn(left, right):
    return lax.dot_general(left, right, (((1,), (0,)), ((), ())), preferred_element_type=FULL)


def tn(left, right):
    return lax.dot_general(left, right, (((0,), (0,)), ((), ())), preferred_element_type=FULL)


def only(pick, value):
    return jnp.where(pick, value, jnp.zeros_like(value))


def attend_kernel(own_ref, other_ref, mask_ref, out_ref, lse_ref, *, head, scale):
    rows = own_ref.shape[1]
    half = rows // 2
    heads = LANES // head
    queries = own_ref[0, :, :LANES]
    own_keys = own_ref[0, :, LANES : 2 * LANES] * jnp.asarray(scale, LOW)
    own_values = own_ref[0, :, 2 * LANES :]
    keys = cat([own_keys[:half], other_ref[0, :, :LANES] * jnp.asarray(scale, LOW)], axis=0)
    near = own_keys[half:]
    values_t = cat([own_values[:half], other_ref[0, :, LANES:]], axis=0).T
    near_values_t = own_values[half:].T
    lane = lax.broadcasted_iota(jnp.int32, (1, LANES), 1) // head
    spans = [(start, start + CLEN) for start in range(0, half, CLEN)]
    picked = lax.broadcasted_iota(jnp.int32, (8, LANES), 0) == lane
    chooser = jnp.where(picked, 1.0, 0.0).astype(LOW)

    def with_ones(value):
        return cat([value, jnp.ones((16, value.shape[1]), LOW)], axis=0)

    def squares(value):
        return nt(chooser, value * value)

    def run(exact):
        flags = []
        if not exact:
            largest = jnp.maximum(
                jnp.max(squares(keys), axis=1, keepdims=True),
                jnp.max(squares(near), axis=1, keepdims=True),
            )
            bound = jnp.sqrt(squares(queries) * largest) * LOG2E
        for part in range(2):
            span = slice(part * half, (part + 1) * half)
            query = queries[span]
            outs = []
            for h in range(heads):
                pick = lane == h
                lines = slice(h * head, (h + 1) * head)
                scores = nt(only(pick, keys), query)
                if part:
                    near_keys = only(pick, near)
                    local = cat([nt(near_keys[a:b], query[a:b]) for a, b in spans], axis=1)
                    local = local + mask_ref[0]
                if exact:
                    top = jnp.max(scores, axis=0, keepdims=True)
                    if part:
                        top = jnp.maximum(top, jnp.max(local, axis=0, keepdims=True))
                    top = top * LOG2E
                else:
                    top = bound[h : h + 1, span]
                weights = jnp.exp2(scores * LOG2E - top).astype(LOW)
                mixed = nn(with_ones(values_t[lines]), weights)
                if part:
                    weights = jnp.exp2(local * LOG2E - top).astype(LOW)
                    value = with_ones(near_values_t[lines])
                    mixed = mixed + cat(
                        [nn(value[:, a:b], weights[:, a:b]) for a, b in spans], axis=1
                    )
                total = mixed[head : head + 1]
                fine = jnp.logical_and(total > 1e-25, total < 1e30)
                flags.append(jnp.where(fine, 0.0, 1.0))
                outs.append(mixed[:head] / total)
                lse_ref[0, 0, h : h + 1, span] = top + jnp.log2(total)
            out_ref[0, span] = cat(outs, axis=0).T.astype(LOW)
        return jnp.max(sum(flags[1:], flags[0]))

    bad = run(False)

    @pl.when(bad > 0.5)
    def _():
        run(True)


def attend(own, other, mask, head):
    batch, rows, columns = own.shape
    steps = columns // (3 * LANES)
    heads = LANES // head
    work = batch * rows * (rows + CLEN) * steps * LANES

    def spec(count, width):
        return pl.BlockSpec((1, count, width), lambda m, p: (m, 0, p))

    return pl.pallas_call(
        functools.partial(attend_kernel, head=head, scale=head**-0.5),
        grid=(batch, steps),
        in_specs=[
            spec(rows, 3 * LANES),
            spec(rows // 2, 2 * LANES),
            pl.BlockSpec((1,) + mask.shape[1:], lambda m, p: (m, 0, 0)),
        ],
        out_specs=[
            spec(rows, LANES),
            pl.BlockSpec((1, 1, heads, rows), lambda m, p: (m, p, 0, 0)),
        ],
        out_shape=[
            jax.ShapeDtypeStruct((batch, rows, steps * LANES), LOW),
            jax.ShapeDtypeStruct((batch, steps, heads, rows), FULL),
        ],
        cost_estimate=pl.CostEstimate(
            flops=16 * work, bytes_accessed=own.size * 4, transcendentals=work // head
        ),
        name="attend",
    )(own, other, mask)


def attend_back_kernel(
    own_ref, other_ref, mask_ref, out_ref, grad_ref, lse_ref, own_grad_ref, other_grad_ref,
    *, head, scale,
):
    rows = own_ref.shape[1]
    half = rows // 2
    heads = LANES // head
    own_keys = own_ref[0, :, LANES : 2 * LANES] * jnp.asarray(scale, LOW)
    own_values = own_ref[0, :, 2 * LANES :]
    keys = cat([own_keys[:half], other_ref[0, :, :LANES] * jnp.asarray(scale, LOW)], axis=0)
    near = own_keys[half:]
    values = cat([own_values[:half], other_ref[0, :, LANES:]], axis=0)
    near_values = own_values[half:]
    keys_t = keys.T
    near_t = near.T
    lane = lax.broadcasted_iota(jnp.int32, (1, LANES), 1) // head
    spans = [(start, start + CLEN) for start in range(0, half, CLEN)]
    totals = [None, None, None, None]

    def add(place, value):
        totals[place] = value if totals[place] is None else totals[place] + value

    for part in range(2):
        span = slice(part * half, (part + 1) * half)
        query = own_ref[0, span, :LANES]
        grad = grad_ref[0, span]
        dots = (grad.astype(FULL) * out_ref[0, span].astype(FULL)).T
        query_grads = []
        for h in range(heads):
            pick = lane == h
            lines = slice(h * head, (h + 1) * head)
            lse = lse_ref[0, 0, h : h + 1, span]
            delta = jnp.sum(dots[lines], axis=0, keepdims=True)
            query_h = only(pick, query)
            grad_h = only(pick, grad)
            probs = jnp.exp2(nt(only(pick, keys), query) * LOG2E - lse)
            slopes = (probs * (nt(only(pick, values), grad) - delta)).astype(LOW)
            probs = probs.astype(LOW)
            query_grad = nn(keys_t[lines], slopes)
            add(0, nn(slopes, query_h))
            add(1, nn(probs, grad_h))
            if part:
                near_h = only(pick, near)
                near_values_h = only(pick, near_values)
                local = cat([nt(near_h[a:b], query[a:b]) for a, b in spans], axis=1)
                dlocal = cat([nt(near_values_h[a:b], grad[a:b]) for a, b in spans], axis=1)
                probs = jnp.exp2((local + mask_ref[0]) * LOG2E - lse)
                slopes = (probs * (dlocal - delta)).astype(LOW)
                probs = probs.astype(LOW)
                query_grad = query_grad + cat(
                    [nn(near_t[lines, a:b], slopes[:, a:b]) for a, b in spans], axis=1
                )
                add(2, cat([nn(slopes[:, a:b], query_h[a:b]) for a, b in spans], axis=0))
                add(3, cat([nn(probs[:, a:b], grad_h[a:b]) for a, b in spans], axis=0))
            query_grads.append(query_grad)
        own_grad_ref[0, span, :LANES] = cat(query_grads, axis=0).T.astype(LOW)
    key_grad = (totals[0] * scale).astype(LOW)
    value_grad = totals[1].astype(LOW)
    own_grad_ref[0, :half, LANES : 2 * LANES] = key_grad[:half]
    own_grad_ref[0, :half, 2 * LANES :] = value_grad[:half]
    other_grad_ref[0, :, :LANES] = key_grad[half:]
    other_grad_ref[0, :, LANES:] = value_grad[half:]
    own_grad_ref[0, half:, LANES : 2 * LANES] = (totals[2] * scale).astype(LOW)
    own_grad_ref[0, half:, 2 * LANES :] = totals[3].astype(LOW)


def attend_back(own, other, mask, out, grad, lse, head):
    batch, rows, columns = own.shape
    steps = columns // (3 * LANES)
    work = batch * rows * (rows + CLEN) * steps * LANES

    def spec(count, width):
        return pl.BlockSpec((1, count, width), lambda m, p: (m, 0, p))

    return pl.pallas_call(
        functools.partial(attend_back_kernel, head=head, scale=head**-0.5),
        grid=(batch, steps),
        in_specs=[
            spec(rows, 3 * LANES),
            spec(rows // 2, 2 * LANES),
            pl.BlockSpec((1,) + mask.shape[1:], lambda m, p: (m, 0, 0)),
            spec(rows, LANES),
            spec(rows, LANES),
            pl.BlockSpec((1, 1) + lse.shape[2:], lambda m, p: (m, p, 0, 0)),
        ],
        out_specs=[spec(rows, 3 * LANES), spec(rows // 2, 2 * LANES)],
        out_shape=[
            jax.ShapeDtypeStruct(own.shape, LOW),
            jax.ShapeDtypeStruct(other.shape, LOW),
        ],
        cost_estimate=pl.CostEstimate(
            flops=40 * work, bytes_accessed=own.size * 10, transcendentals=work // head
        ),
        name="attend_back",
    )(own, other, mask, out, grad, lse)


def swapped(value, axis, mask):
    pairs = [(source, source ^ mask) for source in range(lax.axis_size(axis))]
    return lax.ppermute(value, axis, pairs)


def masks_of(axis):
    return [1 << bit for bit in range(lax.axis_size(axis).bit_length() - 1)]


def bit_of(axis, mask):
    return jnp.where(lax.axis_index(axis) & mask == 0, 0, 1)


def joined(value, axis, mask, dim):
    other = swapped(value, axis, mask)
    first = bit_of(axis, mask) == 0
    return jnp.stack([jnp.where(first, value, other), jnp.where(first, other, value)], axis=dim)


def gathered(block):
    for mask in masks_of("col"):
        block = joined(block, "col", mask, 1).reshape(block.shape[0], -1)
    depth, columns = block.shape
    value = block[None]
    for mask in masks_of("row")[::-1]:
        value = joined(value, "row", mask, 1).reshape(-1, depth, columns)
    return value.reshape(-1, columns)


def parted(value, axis, mask, dim):
    bit = bit_of(axis, mask)
    keep = lax.dynamic_index_in_dim(value, bit, dim, keepdims=False)
    send = lax.dynamic_index_in_dim(value, 1 - bit, dim, keepdims=False)
    return keep + swapped(send.astype(LOW), axis, mask).astype(FULL)


def scattered(total, shape):
    value = total.reshape(-1, shape[0], total.shape[1])
    for mask in masks_of("row"):
        value = parted(value.reshape(-1, 2, *value.shape[1:]), "row", mask, 1)
    value = value.reshape(shape[0], -1)
    for mask in masks_of("col")[::-1]:
        value = parted(value.reshape(shape[0], 2, -1), "col", mask, 1)
    return over_dp(value)


def over_dp(value):
    for mask in masks_of("dp"):
        low = value.astype(LOW)
        value = low.astype(FULL) + swapped(low, "dp", 2 * mask - 1).astype(FULL)
    return value


def normalize(value):
    average = jnp.mean(value, axis=-1, keepdims=True)
    centred = value - average
    spread = jnp.mean(centred * centred, axis=-1, keepdims=True)
    inverse = lax.rsqrt(spread + EPSILON)
    return (centred * inverse, inverse)


def normalize_back(grad_normed, normed, inverse):
    first = jnp.mean(grad_normed, axis=-1, keepdims=True)
    second = jnp.mean(grad_normed * normed, axis=-1, keepdims=True)
    return inverse * (grad_normed - first - normed * second)


def near_mask(lengths, half):
    place = jnp.arange(CLEN, dtype=jnp.int32)[:, None]
    query = jnp.arange(half, dtype=jnp.int32)[None, :]
    limit = jnp.repeat(lengths, CLEN, axis=1)[:, None, :]
    seen = jnp.logical_and((place <= query % CLEN)[None], place[None] < limit)
    return jnp.where(seen, 0.0, -jnp.inf).astype(FULL)


def local(
    inputs,
    qkv_weight,
    out_weight,
    up_weight,
    down_weight,
    vectors,
    up_bias,
    cont_lengths,
    out_cotangent,
):
    grid_rows = lax.axis_size("row")
    grid_cols = lax.axis_size("col")
    place = lax.axis_index("col")
    side = place % 2
    batch, rows, width = inputs.shape
    half = rows // 2
    head = width // H
    steps = width // LANES
    half_conts = cont_lengths.shape[2] // 2
    group_lengths = lax.dynamic_index_in_dim(cont_lengths, place // 2, 1, keepdims=False)
    lengths = lax.dynamic_slice_in_dim(group_lengths, side * half_conts, half_conts, 1)
    mask = near_mask(lengths, half)

    other_tokens = swapped(inputs[:, :half], "col", 1).reshape(batch * half, width)
    tokens = inputs.reshape(batch * rows, width)

    def by_step(matrix):
        lead = matrix.shape[0]
        shaped = matrix.reshape(lead, 3, steps, LANES)
        return shaped.transpose(0, 2, 1, 3)

    qkv_matrix = by_step(gathered(qkv_weight))
    pair_matrix = qkv_matrix[:, :, 1:].reshape(width, 2 * width)
    qkv_matrix = qkv_matrix.reshape(width, 3 * width)
    shift = by_step(
        cat([vectors[:, 0], jnp.zeros((width,), FULL), vectors[:, 1]])[None]
    )
    pair_shift = shift[:, :, 1:].reshape(1, 2 * width)
    shift = shift.reshape(1, 3 * width)
    own = (nn(tokens, qkv_matrix) + shift).astype(LOW).reshape(batch, rows, 3 * width)
    other = (nn(other_tokens, pair_matrix) + pair_shift).astype(LOW)
    other = other.reshape(batch, half, 2 * width)
    attended, lse = attend(own, other, mask, head)

    out_matrix = gathered(out_weight)
    up_matrix = gathered(up_weight)
    down_matrix = gathered(down_weight)
    attended = attended.reshape(batch * rows, width)
    first_sum = tokens.astype(FULL) + nn(attended, out_matrix) + vectors[:, 2]
    first_normed, first_inverse = normalize(first_sum)
    hidden = first_normed * vectors[:, 3] + vectors[:, 4]
    hidden_low = hidden.astype(LOW)
    pre_act = nn(hidden_low, up_matrix) + up_bias
    phi = 0.5 * lax.erfc(pre_act * (-(0.5**0.5)))
    slope = phi + pre_act * (jnp.exp(-0.5 * pre_act * pre_act) * ((2 * math.pi) ** -0.5))
    act_low = (pre_act * phi).astype(LOW)
    slope_low = slope.astype(LOW)
    second_sum = hidden + nn(act_low, down_matrix) + vectors[:, 5]
    second_normed, second_inverse = normalize(second_sum)
    result = (second_normed * vectors[:, 6] + vectors[:, 7]).astype(LOW)

    grad_out = out_cotangent.reshape(batch * rows, width).astype(FULL)
    grad_second = normalize_back(grad_out * vectors[:, 6], second_normed, second_inverse)
    grad_second_low = grad_second.astype(LOW)
    grad_pre = nt(grad_second_low, down_matrix) * slope_low.astype(FULL)
    grad_pre_low = grad_pre.astype(LOW)
    grad_hidden = grad_second + nt(grad_pre_low, up_matrix)
    grad_first = normalize_back(grad_hidden * vectors[:, 3], first_normed, first_inverse)
    grad_first_low = grad_first.astype(LOW)
    grad_attended = nt(grad_first_low, out_matrix).astype(LOW)
    down_grad = scattered(tn(act_low, grad_second_low), down_weight.shape)
    up_grad = scattered(tn(hidden_low, grad_pre_low), up_weight.shape)
    out_grad = scattered(tn(attended, grad_first_low), out_weight.shape)

    own_grad, other_grad = attend_back(
        own,
        other,
        mask,
        attended.reshape(batch, rows, width),
        grad_attended.reshape(batch, rows, width),
        lse,
        head,
    )
    own_grad = own_grad.reshape(batch * rows, 3 * width)
    other_grad = other_grad.reshape(batch * half, 2 * width)
    sent = nt(other_grad, pair_matrix).astype(LOW).reshape(batch, half, width)
    received = swapped(sent, "col", 1).astype(FULL)
    grad_tokens = (grad_first + nt(own_grad, qkv_matrix)).reshape(batch, rows, width)
    grad_tokens = cat([grad_tokens[:, :half] + received, grad_tokens[:, half:]], axis=1)
    grad_tokens = grad_tokens.astype(LOW)
    qkv_total = tn(tokens, own_grad).reshape(width, steps, 3, LANES)
    pair_total = tn(other_tokens, other_grad).reshape(width, steps, 2, LANES)
    qkv_total = cat([qkv_total[:, :, :1], qkv_total[:, :, 1:] + pair_total], axis=2)
    qkv_total = qkv_total.transpose(0, 2, 1, 3).reshape(width, 3 * width)
    qkv_grad = scattered(qkv_total, qkv_weight.shape)

    own_sum = jnp.sum(own_grad.astype(FULL), axis=0).reshape(steps, 3, LANES)
    other_sum = jnp.sum(other_grad.astype(FULL), axis=0).reshape(steps, 2, LANES)
    sums = [
        own_sum[:, 0].reshape(width),
        (own_sum[:, 2] + other_sum[:, 1]).reshape(width),
        jnp.sum(grad_first, axis=0),
        jnp.sum(grad_hidden * first_normed, axis=0),
        jnp.sum(grad_hidden, axis=0),
        jnp.sum(grad_second, axis=0),
        jnp.sum(grad_out * second_normed, axis=0),
        jnp.sum(grad_out, axis=0),
        jnp.sum(grad_pre, axis=0),
    ]
    sums = lax.psum(cat(sums), ("dp", "row", "col"))
    index = lax.axis_index("row") * grid_cols + place
    devices = grid_rows * grid_cols
    split = sums[: 8 * width].reshape(8, width)
    vector_grad = lax.dynamic_slice_in_dim(split, index * (width // devices), width // devices, 1).T
    bias = sums[8 * width :]
    count = bias.shape[0] // devices
    bias_grad = lax.dynamic_slice_in_dim(bias, index * count, count, 0)
    return (
        result.reshape(batch, rows, width),
        grad_tokens,
        qkv_grad,
        out_grad,
        up_grad,
        down_grad,
        vector_grad,
        bias_grad,
    )


def solution(mesh):
    everywhere = ("dp", "row", "col")
    tokens = P(None, everywhere, None)
    matrix = P("row", "col")
    return jax.shard_map(
        local,
        mesh=mesh,
        in_specs=(
            tokens, matrix, matrix, matrix, matrix, P(), P(), P(None, ("dp", "row"), None), tokens,
        ),
        out_specs=(
            tokens, tokens, matrix, matrix, matrix, matrix, P(("row", "col"), None), P(("row", "col")),
        ),
        check_vma=False,
    )
```

time: 2570 us -> 921 us (0.36)
  waiting for transfers between devices: 763 us -> 242 us
  other arithmetic: 558 us -> 81.2 us
  matrix products: 621 us -> 241 us
  local copies, waits for them, and re-layouts: 511 us -> 134 us
  Pallas kernels: 0 us -> 140 us
  blocking collectives: 69.8 us -> 41.2 us
  starting transfers between devices: 5.51 us -> 32.1 us
    while x12 -> x0, waiting for transfers between devices: 585 us -> none
    dot_general x80 -> x15, matrix products: 621 us -> 241 us  [the longest x5 106 us: nn(): lax.dot_general(left, right, (((1,), (0,)), ((), ())), preferred_element_...]
    all_gather x8 -> x0, other arithmetic: 260 us -> none  [the longest x2 125 us: fresh_step(): lax.all_gather(flat_qkv, ('row', 'col'), axis=0, tiled=True)]
    ppermute x4 -> x34, waiting for transfers between devices: 31.7 us -> 242 us  [swapped(): return lax.ppermute(value, axis, pairs)]
    convert_element_type x19 -> x8, other arithmetic: 144 us -> 2.88 us  [over_dp(): low = value.astype(LOW)]
    pallas_call x0 -> x2, Pallas kernels: none -> 140 us  [the longest x1 77.4 us: attend_back(): pl.pallas_call(functools.partial(attend_back_kernel, head=head, scale=hea...]
    while x436 -> x0, local copies, waits for them, and re-layouts: 125 us -> none
    reshape x45 -> x3, local copies, waits for them, and re-layouts: 97.2 us -> 6.3 us  [the longest x1 6.28 us: local(): pair_total = tn(other_tokens, other_grad).reshape(width, steps, 2, LANES)]
  transfers between devices with their start and end apart: 15 -> 34, of which waited for: 7 -> 16; matrix products, arithmetic and copies ran while one was open for 28% -> 22% of each run, Pallas kernels for 0% -> 7%
where the time goes in v1:
time: 921 us; the launch traced here: 914 us
  waiting for transfers between devices  242 us (26%)
  matrix products  241 us (26%)
  Pallas kernels  140 us (15%)
  local copies, waits for them, and re-layouts  134 us (15%)
  other arithmetic  81.2 us (9%)
  blocking collectives  41.2 us (4%)
  starting transfers between devices  32.1 us (3%)
    ppermute x34, waiting for transfers between devices, swapped(): return lax.ppermute(value, axis, pairs)  242 us
    dot_general x5, matrix products, nn(): lax.dot_general(left, right, (((1,), (0,)), ((), ())), preferred_element_...  106 us
    pallas_call x1, Pallas kernels, attend_back(): pl.pallas_call(functools.partial(attend_back_kernel, head=head, scale=hea...  77.4 us
    dot_general x5, matrix products, nt(): lax.dot_general(left, right, (((1,), (1,)), ((), ())), preferred_element_...  74.7 us
    pallas_call x1, Pallas kernels, attend(): pl.pallas_call(functools.partial(attend_kernel, head=head, scale=head **...  63.1 us
    dot_general x5, matrix products, tn(): lax.dot_general(left, right, (((0,), (0,)), ((), ())), preferred_element_...  60.6 us
    psum x1, blocking collectives, local(): sums = lax.psum(cat(sums), ('dp', 'row', 'col'))  41.2 us
    ppermute x34, starting transfers between devices, swapped(): return lax.ppermute(value, axis, pairs)  32.1 us
  transfers between devices with their start and end apart: 34, of which 16 were waited for; matrix products, arithmetic and copies ran while one was open for 22% of the time, Pallas kernels for 7%

profile of v1, /device:TPU:8, one launch (start us, length us, event | category | flops | bytes accessed | tf_op | source)
XLA Modules:
  0.0 914.3 jit_solution(12914700496978764906)
XLA Ops:
  5.0 2.7 slice.76
  17.8 47.9 %collective-permute-done.4 = bf16[192,384]{1,0:T(8,128)(2,1)S(1)} collective-permute-done((bf16[192,384]{1,0:T(8,128)(2,1)}, bf16[192,384]{1,0:T(8,128)(2,1)S(1)}, u32[]{:S(2)}, u32[]{:S(2)}) %collective-permute-start.4) | collective-permute-done | bytes 147488 | tf_op jit(solution)/shard_map/ppermute | solution.py:240
  77.2 2.5 collective-permute-start.11
  84.7 9.7 %collective-permute-done.1 = bf16[1,192,2304]{2,1,0:T(8,128)(2,1)} collective-permute-done((bf16[1,192,2304]{2,1,0:T(8,128)(2,1)}, bf16[1,192,2304]{2,1,0:T(8,128)(2,1)}, u32[]{:S(2)}, u32[]{:S(2)}) %collective-permute-start.1) | collective-permute-done | bytes 884768 | tf_op jit(solution)/shard_map/ppermute | solution.py:240
  97.5 22.2 %collective-permute-done.11 = bf16[1,768,768]{1,2,0:T(8,128)(2,1)} collective-permute-done((bf16[1,768,768]{1,2,0:T(8,128)(2,1)S(1)}, bf16[1,768,768]{1,2,0:T(8,128)(2,1)}, u32[]{:S(2)}, u32[]{:S(2)}) %collective-permute-start.11) | collective-permute-done | bytes 1179680 | tf_op jit(solution)/shard_map/ppermute | solution.py:240
  123.2 19.4 %collective-permute-done.8 = bf16[1,192,3072]{2,1,0:T(8,128)(2,1)S(1)} collective-permute-done((bf16[1,192,3072]{2,1,0:T(8,128)(2,1)S(1)}, bf16[1,192,3072]{2,1,0:T(8,128)(2,1)S(1)}, u32[]{:S(2)}, u32[]{:S(2)}) %collective-permute-start.8) | collective-permute-done | bytes 1179680 | tf_op jit(solution)/shard_map/ppermute | solution.py:240
  146.3 5.4 reshape_reshape_reshape.6
  151.7 6.6 copy.48
  158.3 2.4 slice.94
  160.7 3.3 copy.50
  164.0 12.5 %add_convert_fusion = bf16[2304,2048]{0,1:T(8,128)(2,1)} fusion(bf16[768,2304]{0,1:T(8,128)(2,1)} %bitcast.263, bf16[2048,768]{1,0:T(8,128)(2,1)} %bitcast.275, f32[2304]{0:T(1024)S(1)} %copy-done.50), kind=kOutput, calls=%fused_computation.25 | convolution fusion | flops 7257194496 | bytes 16131072 | tf_op jit(solution)/shard_map/dot_general | solution.py:26
  176.6 5.5 add_convert_fusion.2
  182.0 63.1 %attend.1 = (bf16[2,1024,768]{2,1,0:T(8,128)(2,1)}, f32[2,6,2,1024]{3,2,1,0:T(2,128)}) custom-call(bf16[2,1024,2304]{2,1,0:T(8,128)(2,1)} %bitcast.284, bf16[2,512,1536]{2,1,0:T(8,128)(2,1)} %bitcast.286, f32[2,128,512]{2,1,0:T(8,128)} %fusion.40.mask_ref), custom_call_target="tpu_custom_call" | custom-call | flops 28991029248 | bytes 18874368 | tf_op jit(solution)/shard_map/attend/pallas_call | solution.py:118
  245.1 4.8 copy.65
  250.0 5.3 fusion.59
  255.3 2.9 copy-done.2
  261.0 2.5 pad_maximum_fusion.1
  263.6 6.9 copy.59
  273.5 2.5 slice-done
  277.4 69.3 %multiply_convert_fusion = (bf16[2048,3072]{1,0:T(8,128)(2,1)}, f32[2048,3072]{1,0:T(8,128)}, f32[2048,3072]{1,0:T(8,128)}) fusion(f32[3072]{0:T(1024)S(1)} %copy-done.39, bf16[768,3072]{1,0:T(8,128)(2,1)S(1)} %bitcast.258, f32[2048,768]{1,0:T(8,128)S(1)} %bitcast.229, f32[768]{0:T(1024)S(1)} %get-tuple-element.42, f32[768]{0:T(1024)S(1)} %get-tuple-element.43, ...), kind=kOutput, calls=%fused_computation.10 | convolution fusion | flops 10080485376 | bytes 73959424 | tf_op jit(solution)/shard_map/dot_general | solution.py:26
  346.7 13.5 %fusion.60 = (f32[2048]{0:T(1024)S(1)}, f32[2048,768]{1,0:T(8,128)S(1)}) fusion(f32[768]{0:T(1024)S(1)} %copy-done.52, bf16[2048,3072]{1,0:T(8,128)(2,1)} %get-tuple-element.56, bf16[3072,768]{1,0:T(8,128)(2,1)S(1)} %bitcast.241, f32[768]{0:T(1024)S(1)} %get-tuple-element.42, f32[768]{0:T(1024)S(1)} %get-tuple-element.43, f32[2048]{0:T(1024)S(1)} %add_rsqrt_fusion.1, ...), kind=kOutput, calls=%fused_computation.205 | convolution fusion | flops 9674684416 | bytes 29918208 | tf_op jit(solution)/shard_map/dot_general | solution.py:26
  362.1 2.9 fusion.21
  365.0 5.6 fusion.55
  370.6 35.8 %fusion.13 = (f32[3072]{0:T(1024)S(1)}, bf16[2048,3072]{1,0:T(8,128)(2,1)}, f32[2048,3072]{1,0:T(8,128)}) fusion(f32[2048,3072]{1,0:T(8,128)} %get-tuple-element.57, f32[2048,3072]{1,0:T(8,128)} %get-tuple-element.85, f32[3072]{0:T(1024)S(1)} %copy-done.39, bf16[3072,768]{1,0:T(8,128)(2,1)} %bitcast.240, f32[2048,768]{1,0:T(8,128)} %get-tuple-element.53), kind=kOutput, calls=%fused_computation.26 | convolution fusion | flops 9728160768 | bytes 99115008 | tf_op jit(solution)/shard_map/dot_general | solution.py:22
  406.4 23.2 %multiply_reduce_fusion = (f32[768]{0:T(1024)S(1)}, f32[2048]{0:T(1024)S(1)}, f32[2048]{0:T(1024)S(1)}, f32[768]{0:T(1024)S(1)}, f32[2048,768]{1,0:T(8,128)S(1)}) fusion(f32[2048,768]{1,0:T(8,128)} %copy-done.2, f32[2048]{0:T(1024)S(1)} %add_rsqrt_fusion.1, f32[2048]{0:T(1024)S(1)} %broadcast_multiply_fusion.4, f32[768]{0:T(1024)S(1)} %get-tuple-element.43, ...), kind=kOutput, calls=%fused_computation.40 | convolution fusion | flops 9698273280 | bytes 61383680 | tf_op jit(solution)/shard_map/dot_general | solution.py:22
  429.6 4.7 fusion.57
  434.3 4.1 convolution_convert_fusion
  438.4 77.4 %attend_back.1 = (bf16[2,1024,2304]{2,1,0:T(8,128)(2,1)}, bf16[2,512,1536]{2,1,0:T(8,128)(2,1)}) custom-call(bf16[2,1024,2304]{2,1,0:T(8,128)(2,1)} %bitcast.285, bf16[2,512,1536]{2,1,0:T(8,128)(2,1)} %bitcast.287, f32[2,128,512]{2,1,0:T(8,128)} %fusion.40.mask_ref, bf16[2,1024,768]{2,1,0:T(8,128)(2,1)} %get-tuple-element.12.out_ref, ...), custom_call_target="tpu_custom_call" | custom-call | flops 72477573120 | bytes 47185920 | tf_op jit(solution)/shard_map/attend_back/pallas_call | solution.py:215
  515.8 5.2 convert_reduce_fusion
  523.6 41.2 %psum.7 = f32[9216]{0:T(1024)S(1)} all-reduce(f32[9216]{0:T(1024)S(1)} %constant_dynamic-update-slice_fusion), channel_id=1, replica_groups=mesh['dp'=4,'row'=4,'col'=2] {'dp','row','col'}, use_global_device_ids=true, to_apply=%region_17.18 | all-reduce | flops 9216 | bytes 73728 | tf_op jit(solution)/shard_map/psum | solution.py:423
  564.9 17.2 %fusion.30 = f32[3072,768]{1,0:T(8,128)} fusion(bf16[2048,3072]{1,0:T(8,128)(2,1)} %get-tuple-element.56, f32[2048,768]{1,0:T(8,128)} %get-tuple-element.53), kind=kOutput, calls=%fused_computation.93 | convolution fusion | flops 9665249280 | bytes 28311552 | tf_op jit(solution)/shard_map/dot_general | solution.py:30
  582.1 20.9 %fusion.48 = f32[768,3072]{1,0:T(8,128)} fusion(f32[2048,3072]{1,0:T(8,128)} %get-tuple-element.88, bf16[2048,3072]{1,0:T(8,128)(2,1)} %get-tuple-element.51, f32[2048,768]{1,0:T(8,128)S(1)} %bitcast.231, f32[768]{0:T(1024)S(1)} %copy-done.43, f32[768]{0:T(1024)S(1)} %get-tuple-element.43, f32[2048]{0:T(1024)S(1)} %add_rsqrt_fusion.1, ...), kind=kOutput, calls=%fused_computation.200 | convolution fusion | flops 9690415104 | bytes 53499904 | tf_op jit(solution)/shard_map/dot_general | solution.py:30
  603.0 11.3 %fusion.61 = f32[2304,768,1]{1,0,2:T(8,128)S(1)} fusion(bf16[2,1024,2304]{2,1,0:T(8,128)(2,1)} %get-tuple-element.14, bf16[2,1024,768]{2,1,0:T(8,128)(2,1)} %param.9), kind=kOutput, calls=%fused_computation.206 | convolution fusion | flops 7247757312 | bytes 19660800 | tf_op jit(solution)/shard_map/dot_general | solution.py:30
  614.4 2.5 slice.99
  618.4 4.8 constant_dynamic-slice_fusion.2
  623.3 6.1 copy.68
  629.3 2.6 constant_dynamic-slice_fusion.1
  631.9 2.5 copy.83
  634.4 4.2 fusion.26
  638.9 5.4 fusion.24
  646.8 6.5 copy.80
  653.3 5.7 fusion.62
  659.0 6.3 copy.64
  665.3 2.5 copy.79
  667.7 5.6 add.282
  677.8 4.6 maximum_bitcast_fusion
  682.4 9.5 %reshape_reshape_reshape.7 = f32[2,2,192,2304]{3,2,1,0:T(8,128)} reshape(f32[768,3,6,128]{3,2,1,0:T(8,128)} %maximum_bitcast_fusion) | data formatting | bytes 14155776 | tf_op jit(solution)/shard_map/reshape;reshape;reshape | solution.py:277
  698.3 3.5 fusion.27
  704.2 3.9 convolution_convert_fusion.1
  710.3 7.7 convolution_add_fusion.1
  720.3 23.3 %collective-permute-done.13 = bf16[2,512,768]{2,1,0:T(8,128)(2,1)S(1)} collective-permute-done((bf16[2,512,768]{2,1,0:T(8,128)(2,1)}, bf16[2,512,768]{2,1,0:T(8,128)(2,1)S(1)}, u32[]{:S(2)}, u32[]{:S(2)}) %collective-permute-start.13) | collective-permute-done | bytes 1572896 | tf_op jit(solution)/shard_map/ppermute | solution.py:240
  745.9 2.4 bitcast_add_fusion.2
  754.7 2.6 bitcast_add_fusion.1
  762.0 9.0 collective-permute-done.15
  772.4 2.6 reshape_reshape.31
  778.6 17.7 %collective-permute-done.30 = bf16[1,768,768]{1,2,0:T(8,128)(2,1)} collective-permute-done((bf16[1,768,768]{1,2,0:T(8,128)(2,1)}, bf16[1,768,768]{1,2,0:T(8,128)(2,1)}, u32[]{:S(2)}, u32[]{:S(2)}) %collective-permute-start.30) | collective-permute-done | bytes 1179680 | tf_op jit(solution)/shard_map/ppermute | solution.py:240
  800.9 18.5 %collective-permute-done.25 = bf16[1,192,3072]{2,1,0:T(8,128)(2,1)} collective-permute-done((bf16[1,192,3072]{2,1,0:T(8,128)(2,1)}, bf16[1,192,3072]{2,1,0:T(8,128)(2,1)}, u32[]{:S(2)}, u32[]{:S(2)}) %collective-permute-start.25) | collective-permute-done | bytes 1179680 | tf_op jit(solution)/shard_map/ppermute | solution.py:240
  819.4 3.0 convert_add_fusion.1
  822.5 3.3 reshape_reshape.34
  833.8 6.3 collective-permute-done.26
  844.0 11.2 %collective-permute-done.32 = bf16[768,384]{0,1:T(8,128)(2,1)S(1)} collective-permute-done((bf16[768,384]{0,1:T(8,128)(2,1)S(1)}, bf16[768,384]{0,1:T(8,128)(2,1)S(1)}, u32[]{:S(2)}, u32[]{:S(2)}) %collective-permute-start.32) | collective-permute-done | bytes 589856 | tf_op jit(solution)/shard_map/ppermute | solution.py:240
  856.7 11.1 %collective-permute-done.27 = bf16[192,1536]{1,0:T(8,128)(2,1)S(1)} collective-permute-done((bf16[192,1536]{1,0:T(8,128)(2,1)S(1)}, bf16[192,1536]{1,0:T(8,128)(2,1)S(1)}, u32[]{:S(2)}, u32[]{:S(2)}) %collective-permute-start.27) | collective-permute-done | bytes 589856 | tf_op jit(solution)/shard_map/ppermute | solution.py:240
  870.3 32.0 %collective-permute-done.33 = bf16[768,384]{0,1:T(8,128)(2,1)S(1)} collective-permute-done((bf16[768,384]{0,1:T(8,128)(2,1)S(1)}, bf16[768,384]{0,1:T(8,128)(2,1)S(1)}, u32[]{:S(2)}, u32[]{:S(2)}) %collective-permute-start.33) | collective-permute-done | bytes 589856 | tf_op jit(solution)/shard_map/ppermute | solution.py:240
  903.9 8.8 collective-permute-done.28
  (320 shorter events, 115.8 us)
Async XLA Ops:
  0.6 12.2 %copy-start = (s32[2,1,8]{2,1,0:T(1,128)S(1)}, s32[2,1,8]{2,1,0:T(1,128)}, u32[]{:S(2)}) copy-start(s32[2,1,8]{2,1,0:T(1,128)} %param.16) | copy-start | bytes 196
  0.7 65.1 %copy-start.38 = (bf16[192,384]{1,0:T(8,128)(2,1)S(1)}, bf16[192,384]{1,0:T(8,128)(2,1)}, u32[]{:S(2)}) copy-start(bf16[192,384]{1,0:T(8,128)(2,1)} %param.11) | copy-start | bytes 442372
  0.7 13.3 %copy-start.3 = (bf16[2,1024,768]{2,1,0:T(8,128)(2,1)S(1)}, bf16[2,1024,768]{2,1,0:T(8,128)(2,1)}, u32[]{:S(2)}) copy-start(bf16[2,1024,768]{2,1,0:T(8,128)(2,1)} %param.17) | copy-start | bytes 9437188
  2.9 73.0 %collective-permute-start.10 = (bf16[768,384]{0,1:T(8,128)(2,1)}, bf16[768,384]{0,1:T(8,128)(2,1)}, u32[]{:S(2)}, u32[]{:S(2)}) collective-permute-start(bf16[768,384]{0,1:T(8,128)(2,1)} %copy.57), channel_id=1, source_target_pairs={{0,1},{1,0},{2,3},{3,2},{4,5},{5,4},{6,7},{7,6},{8,9},{9,8},{10,11... | collective-permute-start | bytes 1769480 | tf_op jit(solution)/shard_map/ppermute | solution.py:240
  4.5 63.4 %collective-permute-start = (bf16[192,1152]{1,0:T(8,128)(2,1)}, bf16[192,1152]{1,0:T(8,128)(2,1)}, u32[]{:S(2)}, u32[]{:S(2)}) collective-permute-start(bf16[192,1152]{1,0:T(8,128)(2,1)} %param.10), channel_id=1, source_target_pairs={{0,1},{1,0},{2,3},{3,2},{4,5},{5,4},{6,7},{7,6},{8,9},{9,8},{10,11... | collective-permute-start | bytes 1327112 | tf_op jit(solution)/shard_map/ppermute | solution.py:240
  7.6 168.9 %collective-permute-start.3 = (bf16[2,512,768]{2,1,0:T(8,128)(2,1)}, bf16[2,512,768]{2,1,0:T(8,128)(2,1)}, u32[]{:S(2)}, u32[]{:S(2)}) collective-permute-start(bf16[2,512,768]{2,1,0:T(8,128)(2,1)} %slice.76), channel_id=1, source_target_pairs={{0,1},{1,0},{2,3},{3,2},{4,5},{5,4},{6,7},{7,6},{8,9},{9,8},{10,11... | collective-permute-start | bytes 4718600 | tf_op jit(solution)/shard_map/ppermute | solution.py:240
  9.1 56.6 %collective-permute-start.4 = (bf16[192,384]{1,0:T(8,128)(2,1)}, bf16[192,384]{1,0:T(8,128)(2,1)S(1)}, u32[]{:S(2)}, u32[]{:S(2)}) collective-permute-start(bf16[192,384]{1,0:T(8,128)(2,1)} %param.11), channel_id=1, source_target_pairs={{0,1},{1,0},{2,3},{3,2},{4,5},{5,4},{6,7},{7,6},{8,9},{9,8},{10,11... | collective-permute-start | bytes 442376 | tf_op jit(solution)/shard_map/ppermute | solution.py:240
  9.6 70.1 %collective-permute-start.7 = (bf16[192,1536]{1,0:T(8,128)(2,1)}, bf16[192,1536]{1,0:T(8,128)(2,1)}, u32[]{:S(2)}, u32[]{:S(2)}) collective-permute-start(bf16[192,1536]{1,0:T(8,128)(2,1)} %param.12), channel_id=1, source_target_pairs={{0,1},{1,0},{2,3},{3,2},{4,5},{5,4},{6,7},{7,6},{8,9},{9,8},{10,11... | collective-permute-start | bytes 1769480 | tf_op jit(solution)/shard_map/ppermute | solution.py:240
  12.9 56.3 %copy-start.40 = (f32[768]{0:T(1024)}, f32[768]{0:T(1024)S(1)}, u32[]{:S(2)}) copy-start(f32[768]{0:T(1024)S(1)} %get-tuple-element.40) | copy-start | bytes 9220
  12.9 333.8 %copy-start.42 = (f32[768]{0:T(1024)}, f32[768]{0:T(1024)S(1)}, u32[]{:S(2)}) copy-start(f32[768]{0:T(1024)S(1)} %get-tuple-element.42) | copy-start | bytes 9220
  66.3 9.6 %copy-start.29 = (bf16[768,384]{0,1:T(8,128)(2,1)S(1)}, bf16[768,384]{0,1:T(8,128)(2,1)}, u32[]{:S(2)}) copy-start(bf16[768,384]{0,1:T(8,128)(2,1)} %copy.57) | copy-start | bytes 1769476
  66.3 8.0 collective-permute-start.5
  70.1 9.6 %copy-start.36 = (bf16[192,1536]{1,0:T(8,128)(2,1)S(1)}, bf16[192,1536]{1,0:T(8,128)(2,1)}, u32[]{:S(2)}) copy-start(bf16[192,1536]{1,0:T(8,128)(2,1)} %param.12) | copy-start | bytes 1769476
  71.6 22.8 %collective-permute-start.1 = (bf16[1,192,2304]{2,1,0:T(8,128)(2,1)}, bf16[1,192,2304]{2,1,0:T(8,128)(2,1)}, u32[]{:S(2)}, u32[]{:S(2)}) collective-permute-start(bf16[1,192,2304]{2,1,0:T(8,128)(2,1)} %broadcast_in_dim_reshape.13), channel_id=1, source_target_pairs={{0,4},{2,6},{4,0},{6,2},{1,5},{3,7},{5,1},{7,3},{8,12},{10,14},{12... | collective-permute-start | bytes 2654216 | tf_op jit(solution)/shard_map/ppermute | solution.py:240
  75.9 7.5 collective-permute-start.6
  77.2 42.5 %collective-permute-start.11 = (bf16[1,768,768]{1,2,0:T(8,128)(2,1)S(1)}, bf16[1,768,768]{1,2,0:T(8,128)(2,1)}, u32[]{:S(2)}, u32[]{:S(2)}) collective-permute-start(bf16[1,768,768]{1,2,0:T(8,128)(2,1)S(1)} %bitcast.257), channel_id=1, source_target_pairs={{0,4},{2,6},{4,0},{6,2},{1,5},{3,7},{5,1},{7,3},{8,12},{10,14},{12... | collective-permute-start | bytes 3538952 | tf_op jit(solution)/shard_map/ppermute | solution.py:240
  83.3 59.3 %collective-permute-start.8 = (bf16[1,192,3072]{2,1,0:T(8,128)(2,1)S(1)}, bf16[1,192,3072]{2,1,0:T(8,128)(2,1)S(1)}, u32[]{:S(2)}, u32[]{:S(2)}) collective-permute-start(bf16[1,192,3072]{2,1,0:T(8,128)(2,1)S(1)} %broadcast_in_dim_reshape.15), channel_id=1, source_target_pairs={{0,4},{2,6},{4,0},{6,2},{1,5},{3,7},{5,1},{7,3},{8,12},{10,14},{12... | collective-permute-start | bytes 3538952 | tf_op jit(solution)/shard_map/ppermute | solution.py:240
  96.2 49.3 %collective-permute-start.2 = (bf16[2,192,2304]{2,1,0:T(8,128)(2,1)S(1)}, bf16[2,192,2304]{2,1,0:T(8,128)(2,1)S(1)}, u32[]{:S(2)}, u32[]{:S(2)}) collective-permute-start(bf16[2,192,2304]{2,1,0:T(8,128)(2,1)S(1)} %maximum_bitcast_fusion.3), channel_id=1, source_target_pairs={{0,2},{2,0},{4,6},{6,4},{1,3},{3,1},{5,7},{7,5},{8,10},{10,8},{12,... | collective-permute-start | bytes 5308424 | tf_op jit(solution)/shard_map/ppermute | solution.py:240
  122.9 136.1 %collective-permute-start.12 = (bf16[2,768,768]{1,2,0:T(8,128)(2,1)}, bf16[2,768,768]{1,2,0:T(8,128)(2,1)}, u32[]{:S(2)}, u32[]{:S(2)}) collective-permute-start(bf16[2,768,768]{1,2,0:T(8,128)(2,1)} %maximum_bitcast_fusion.2), channel_id=1, source_target_pairs={{0,2},{2,0},{4,6},{6,4},{1,3},{3,1},{5,7},{7,5},{8,10},{10,8},{12,... | collective-permute-start | bytes 7077896 | tf_op jit(solution)/shard_map/ppermute | solution.py:240
  145.4 125.0 %collective-permute-start.9 = (bf16[2,192,3072]{2,1,0:T(8,128)(2,1)}, bf16[2,192,3072]{2,1,0:T(8,128)(2,1)}, u32[]{:S(2)}, u32[]{:S(2)}) collective-permute-start(bf16[2,192,3072]{2,1,0:T(8,128)(2,1)} %maximum_bitcast_fusion.1), channel_id=1, source_target_pairs={{0,2},{2,0},{4,6},{6,4},{1,3},{3,1},{5,7},{7,5},{8,10},{10,8},{12,... | collective-permute-start | bytes 7077896 | tf_op jit(solution)/shard_map/ppermute | solution.py:240
  164.0 12.6 %copy-start.31 = (bf16[768,6,2,128]{0,3,2,1:T(8,128)(2,1)S(1)}, bf16[768,6,2,128]{0,3,2,1:T(8,128)(2,1)}, u32[]{:S(2)}) copy-start(bf16[768,6,2,128]{0,3,2,1:T(8,128)(2,1)} %copy.50) | copy-start | bytes 7077892
  164.0 12.6 %copy-start.51 = (f32[1536]{0:T(1024)S(1)}, f32[1536]{0:T(1024)}, u32[]{:S(2)}) copy-start(f32[1536]{0:T(1024)} %add.254) | copy-start | bytes 18436
  273.5 73.2 %copy-start.19 = (bf16[2,2,192,3072]{3,2,1,0:T(8,128)(2,1)}, bf16[2,2,192,3072]{3,2,1,0:T(8,128)(2,1)S(1)}, u32[]{:S(2)}) copy-start(bf16[2,2,192,3072]{3,2,1,0:T(8,128)(2,1)S(1)} %copy.55) | copy-start | bytes 14155780
  277.4 69.3 %copy-start.5 = (bf16[2,2,768,768]{3,2,1,0:T(8,128)(2,1)S(1)}, bf16[2,2,768,768]{3,2,1,0:T(8,128)(2,1)}, u32[]{:S(2)}) copy-start(bf16[2,2,768,768]{3,2,1,0:T(8,128)(2,1)} %copy.59) | copy-start | bytes 14155780
  277.4 69.3 %copy-start.52 = (f32[768]{0:T(1024)S(1)}, f32[768]{0:T(1024)}, u32[]{:S(2)}) copy-start(f32[768]{0:T(1024)} %get-tuple-element.41) | copy-start | bytes 9220
  515.8 66.3 %slice-start.2 = ((s8[6291456]{0:T(1024)(128)(4,1)}), s8[2097152]{0:T(1024)(128)(4,1)S(1)}, s32[]{:S(2)}) async-start(s8[6291456]{0:T(1024)(128)(4,1)} %bitcast.230), calls=%async_computation.2 | async-start | bytes 4194304
  564.8 17.3 %copy-start.37 = (f32[9216]{0:T(1024)}, f32[9216]{0:T(1024)S(1)}, u32[]{:S(2)}) copy-start(f32[9216]{0:T(1024)S(1)} %psum.7) | copy-start | bytes 110596
  564.8 17.3 %slice-start.3 = ((s8[6291456]{0:T(1024)(128)(4,1)}), s8[4194304]{0:T(1024)(128)(4,1)S(1)}, s32[]{:S(2)}) async-start(s8[6291456]{0:T(1024)(128)(4,1)} %bitcast.230), calls=%async_computation.3 | async-start | bytes 8388608
  564.9 17.3 %copy-start.43 = (f32[768]{0:T(1024)S(1)}, f32[768]{0:T(1024)}, u32[]{:S(2)}) copy-start(f32[768]{0:T(1024)} %copy-done.42) | copy-start | bytes 9220
  634.4 115.5 %collective-permute-start.29 = (bf16[2,768,768]{1,2,0:T(8,128)(2,1)}, bf16[2,768,768]{1,2,0:T(8,128)(2,1)}, u32[]{:S(2)}, u32[]{:S(2)}) collective-permute-start(bf16[2,768,768]{1,2,0:T(8,128)(2,1)} %bitcast.270), channel_id=1, source_target_pairs={{0,2},{2,0},{4,6},{6,4},{1,3},{3,1},{5,7},{7,5},{8,10},{10,8},{12,... | collective-permute-start | bytes 7077896 | tf_op jit(solution)/shard_map/ppermute | solution.py:240
  638.6 116.1 %collective-permute-start.24 = (bf16[2,192,3072]{2,1,0:T(8,128)(2,1)}, bf16[2,192,3072]{2,1,0:T(8,128)(2,1)}, u32[]{:S(2)}, u32[]{:S(2)}) collective-permute-start(bf16[2,192,3072]{2,1,0:T(8,128)(2,1)} %fusion.26), channel_id=1, source_target_pairs={{0,2},{2,0},{4,6},{6,4},{1,3},{3,1},{5,7},{7,5},{8,10},{10,8},{12,... | collective-permute-start | bytes 7077896 | tf_op jit(solution)/shard_map/ppermute | solution.py:240
  646.6 26.6 %collective-permute-start.19 = (bf16[2,192,768]{2,1,0:T(8,128)(2,1)}, bf16[2,192,768]{2,1,0:T(8,128)(2,1)}, u32[]{:S(2)}, u32[]{:S(2)}) collective-permute-start(bf16[2,192,768]{2,1,0:T(8,128)(2,1)} %fusion.37), channel_id=1, source_target_pairs={{0,2},{2,0},{4,6},{6,4},{1,3},{3,1},{5,7},{7,5},{8,10},{10,8},{12,... | collective-permute-start | bytes 1769480 | tf_op jit(solution)/shard_map/ppermute | solution.py:240
  675.6 16.3 %collective-permute-start.20 = (bf16[1,192,768]{2,1,0:T(8,128)(2,1)S(1)}, bf16[1,192,768]{2,1,0:T(8,128)(2,1)}, u32[]{:S(2)}, u32[]{:S(2)}) collective-permute-start(bf16[1,192,768]{2,1,0:T(8,128)(2,1)S(1)} %dynamic-slice_convert_fusion.8), channel_id=1, source_target_pairs={{0,4},{2,6},{4,0},{6,2},{1,5},{3,7},{5,1},{7,3},{8,12},{10,14},{12... | collective-permute-start | bytes 884744 | tf_op jit(solution)/shard_map/ppermute | solution.py:240
  682.4 9.5 %copy-start.21 = (f32[2,192,768]{2,1,0:T(8,128)S(1)}, f32[2,192,768]{2,1,0:T(8,128)}, u32[]{:S(2)}) copy-start(f32[2,192,768]{2,1,0:T(8,128)} %copy-done.20) | copy-start | bytes 3538948
  693.7 10.4 %copy-start.25 = (bf16[2,512,1536]{2,1,0:T(8,128)(2,1)S(1)}, bf16[2,512,1536]{2,1,0:T(8,128)(2,1)}, u32[]{:S(2)}) copy-start(bf16[2,512,1536]{2,1,0:T(8,128)(2,1)} %get-tuple-element.15) | copy-start | bytes 9437188
  696.1 8.1 copy-start.32
  697.6 5.9 collective-permute-start.21
  698.3 12.0 %slice-start.13 = ((s8[9437184]{0:T(1024)(128)(4,1)}), s8[4194304]{0:T(1024)(128)(4,1)S(1)}, s32[]{:S(2)}) async-start(s8[9437184]{0:T(1024)(128)(4,1)} %bitcast.246), calls=%async_computation.13 | async-start | bytes 8388608
  698.3 12.0 %slice-start.16 = ((s8[6291456]{0:T(1024)(128)(4,1)}), s8[4194304]{0:T(1024)(128)(4,1)S(1)}, s32[]{:S(2)}) async-start(s8[6291456]{0:T(1024)(128)(4,1)} %bitcast.253), calls=%async_computation.16 | async-start | bytes 8388608
  701.8 44.0 %collective-permute-start.14 = (bf16[2,192,2304]{2,1,0:T(8,128)(2,1)}, bf16[2,192,2304]{2,1,0:T(8,128)(2,1)}, u32[]{:S(2)}, u32[]{:S(2)}) collective-permute-start(bf16[2,192,2304]{2,1,0:T(8,128)(2,1)} %fusion.27), channel_id=1, source_target_pairs={{0,2},{2,0},{4,6},{6,4},{1,3},{3,1},{5,7},{7,5},{8,10},{10,8},{12,... | collective-permute-start | bytes 5308424 | tf_op jit(solution)/shard_map/ppermute | solution.py:240
  703.6 5.2 collective-permute-start.22
  708.0 35.5 %collective-permute-start.13 = (bf16[2,512,768]{2,1,0:T(8,128)(2,1)}, bf16[2,512,768]{2,1,0:T(8,128)(2,1)S(1)}, u32[]{:S(2)}, u32[]{:S(2)}) collective-permute-start(bf16[2,512,768]{2,1,0:T(8,128)(2,1)} %bitcast.52), channel_id=1, source_target_pairs={{0,1},{1,0},{2,3},{3,2},{4,5},{5,4},{6,7},{7,6},{8,9},{9,8},{10,11... | collective-permute-start | bytes 4718600 | tf_op jit(solution)/shard_map/ppermute | solution.py:240
  708.8 10.8 %collective-permute-start.23 = (bf16[192,384]{1,0:T(8,128)(2,1)S(1)}, bf16[192,384]{1,0:T(8,128)(2,1)S(1)}, u32[]{:S(2)}, u32[]{:S(2)}) collective-permute-start(bf16[192,384]{1,0:T(8,128)(2,1)S(1)} %add_convert_fusion.6), channel_id=1, source_target_pairs={{0,24},{8,16},{16,8},{24,0},{1,25},{9,17},{17,9},{25,1},{2,26},{10... | collective-permute-start | bytes 442376 | tf_op jit(solution)/shard_map/ppermute | solution.py:240
  710.3 7.9 slice-start.19
  719.6 26.3 %slice-start.7 = ((s8[7077888]{0:T(1024)(128)(4,1)}), s8[4194304]{0:T(1024)(128)(4,1)S(1)}, s32[]{:S(2)}) async-start(s8[7077888]{0:T(1024)(128)(4,1)} %bitcast.238), calls=%async_computation.7 | async-start | bytes 8388608
  720.3 25.5 %slice-start.8 = ((s8[7077888]{0:T(1024)(128)(4,1)}), s8[2883584]{0:T(1024)(128)(4,1)S(1)}, s32[]{:S(2)}) async-start(s8[7077888]{0:T(1024)(128)(4,1)} %bitcast.238), calls=%async_computation.8 | async-start | bytes 5767168
  745.9 8.8 slice-start.4
  745.9 8.8 slice-start.5
  748.4 22.6 %collective-permute-start.15 = (bf16[1,192,2304]{2,1,0:T(8,128)(2,1)S(1)}, bf16[1,192,2304]{2,1,0:T(8,128)(2,1)S(1)}, u32[]{:S(2)}, u32[]{:S(2)}) collective-permute-start(bf16[1,192,2304]{2,1,0:T(8,128)(2,1)S(1)} %dynamic-slice_convert_fusion.3), channel_id=1, source_target_pairs={{0,4},{2,6},{4,0},{6,2},{1,5},{3,7},{5,1},{7,3},{8,12},{10,14},{12... | collective-permute-start | bytes 2654216 | tf_op jit(solution)/shard_map/ppermute | solution.py:240
  753.4 43.0 %collective-permute-start.30 = (bf16[1,768,768]{1,2,0:T(8,128)(2,1)}, bf16[1,768,768]{1,2,0:T(8,128)(2,1)}, u32[]{:S(2)}, u32[]{:S(2)}) collective-permute-start(bf16[1,768,768]{1,2,0:T(8,128)(2,1)} %dynamic-slice_convert_fusion.1), channel_id=1, source_target_pairs={{0,4},{2,6},{4,0},{6,2},{1,5},{3,7},{5,1},{7,3},{8,12},{10,14},{12... | collective-permute-start | bytes 3538952 | tf_op jit(solution)/shard_map/ppermute | solution.py:240
  760.7 58.7 %collective-permute-start.25 = (bf16[1,192,3072]{2,1,0:T(8,128)(2,1)}, bf16[1,192,3072]{2,1,0:T(8,128)(2,1)}, u32[]{:S(2)}, u32[]{:S(2)}) collective-permute-start(bf16[1,192,3072]{2,1,0:T(8,128)(2,1)} %dynamic-slice_convert_fusion.2), channel_id=1, source_target_pairs={{0,4},{2,6},{4,0},{6,2},{1,5},{3,7},{5,1},{7,3},{8,12},{10,14},{12... | collective-permute-start | bytes 3538952 | tf_op jit(solution)/shard_map/ppermute | solution.py:240
  772.4 47.1 %slice-start.11 = ((s8[4718592]{0:T(1024)(128)(4,1)}), s8[524288]{0:T(1024)(128)(4,1)S(1)}, s32[]{:S(2)}) async-start(s8[4718592]{0:T(1024)(128)(4,1)} %bitcast.244), calls=%async_computation.11 | async-start | bytes 1048576
  776.6 42.8 %slice-start.12 = ((s8[4718592]{0:T(1024)(128)(4,1)}), s8[4194304]{0:T(1024)(128)(4,1)S(1)}, s32[]{:S(2)}) async-start(s8[4718592]{0:T(1024)(128)(4,1)} %bitcast.244), calls=%async_computation.12 | async-start | bytes 8388608
  776.6 51.7 %collective-permute-start.16 = (bf16[192,1152]{1,0:T(8,128)(2,1)}, bf16[192,1152]{1,0:T(8,128)(2,1)}, u32[]{:S(2)}, u32[]{:S(2)}) collective-permute-start(bf16[192,1152]{1,0:T(8,128)(2,1)} %bitcast.224), channel_id=1, source_target_pairs={{0,1},{1,0},{2,3},{3,2},{4,5},{5,4},{6,7},{7,6},{8,9},{9,8},{10,11... | collective-permute-start | bytes 1327112 | tf_op jit(solution)/shard_map/ppermute | solution.py:240
  798.6 20.8 %copy-start.16 = (f32[1,768,768]{1,2,0:T(8,128)}, f32[1,768,768]{1,2,0:T(8,128)S(1)}, u32[]{:S(2)}) copy-start(f32[1,768,768]{1,2,0:T(8,128)S(1)} %convert_add_fusion) | copy-start | bytes 7077892
  799.6 32.4 %collective-permute-start.31 = (bf16[768,384]{0,1:T(8,128)(2,1)}, bf16[768,384]{0,1:T(8,128)(2,1)}, u32[]{:S(2)}, u32[]{:S(2)}) collective-permute-start(bf16[768,384]{0,1:T(8,128)(2,1)} %fusion.38), channel_id=1, source_target_pairs={{0,1},{1,0},{2,3},{3,2},{4,5},{5,4},{6,7},{7,6},{8,9},{9,8},{10,11... | collective-permute-start | bytes 1769480 | tf_op jit(solution)/shard_map/ppermute | solution.py:240
  827.0 13.1 %collective-permute-start.26 = (bf16[192,1536]{1,0:T(8,128)(2,1)S(1)}, bf16[192,1536]{1,0:T(8,128)(2,1)S(1)}, u32[]{:S(2)}, u32[]{:S(2)}) collective-permute-start(bf16[192,1536]{1,0:T(8,128)(2,1)S(1)} %bitcast.277), channel_id=1, source_target_pairs={{0,1},{1,0},{2,3},{3,2},{4,5},{5,4},{6,7},{7,6},{8,9},{9,8},{10,11... | collective-permute-start | bytes 1769480 | tf_op jit(solution)/shard_map/ppermute | solution.py:240
  829.4 13.1 %collective-permute-start.17 = (bf16[192,1152]{1,0:T(8,128)(2,1)S(1)}, bf16[192,1152]{1,0:T(8,128)(2,1)S(1)}, u32[]{:S(2)}, u32[]{:S(2)}) collective-permute-start(bf16[192,1152]{1,0:T(8,128)(2,1)S(1)} %fusion.36), channel_id=1, source_target_pairs={{0,8},{8,0},{16,24},{24,16},{1,9},{9,1},{17,25},{25,17},{2,10},{10... | collective-permute-start | bytes 1327112 | tf_op jit(solution)/shard_map/ppermute | solution.py:240
  833.3 21.9 %collective-permute-start.32 = (bf16[768,384]{0,1:T(8,128)(2,1)S(1)}, bf16[768,384]{0,1:T(8,128)(2,1)S(1)}, u32[]{:S(2)}, u32[]{:S(2)}) collective-permute-start(bf16[768,384]{0,1:T(8,128)(2,1)S(1)} %fusion.35), channel_id=1, source_target_pairs={{0,8},{8,0},{16,24},{24,16},{1,9},{9,1},{17,25},{25,17},{2,10},{10... | collective-permute-start | bytes 1769480 | tf_op jit(solution)/shard_map/ppermute | solution.py:240
  840.2 27.6 %collective-permute-start.27 = (bf16[192,1536]{1,0:T(8,128)(2,1)S(1)}, bf16[192,1536]{1,0:T(8,128)(2,1)S(1)}, u32[]{:S(2)}, u32[]{:S(2)}) collective-permute-start(bf16[192,1536]{1,0:T(8,128)(2,1)S(1)} %fusion.34), channel_id=1, source_target_pairs={{0,8},{8,0},{16,24},{24,16},{1,9},{9,1},{17,25},{25,17},{2,10},{10... | collective-permute-start | bytes 1769480 | tf_op jit(solution)/shard_map/ppermute | solution.py:240
  842.6 26.7 %collective-permute-start.18 = (bf16[192,1152]{1,0:T(8,128)(2,1)S(1)}, bf16[192,1152]{1,0:T(8,128)(2,1)S(1)}, u32[]{:S(2)}, u32[]{:S(2)}) collective-permute-start(bf16[192,1152]{1,0:T(8,128)(2,1)S(1)} %add_convert_fusion.5), channel_id=1, source_target_pairs={{0,24},{8,16},{16,8},{24,0},{1,25},{9,17},{17,9},{25,1},{2,26},{10... | collective-permute-start | bytes 1327112 | tf_op jit(solution)/shard_map/ppermute | solution.py:240
  855.3 47.1 %collective-permute-start.33 = (bf16[768,384]{0,1:T(8,128)(2,1)S(1)}, bf16[768,384]{0,1:T(8,128)(2,1)S(1)}, u32[]{:S(2)}, u32[]{:S(2)}) collective-permute-start(bf16[768,384]{0,1:T(8,128)(2,1)S(1)} %add_convert_fusion.3), channel_id=1, source_target_pairs={{0,24},{8,16},{16,8},{24,0},{1,25},{9,17},{17,9},{25,1},{2,26},{10... | collective-permute-start | bytes 1769480 | tf_op jit(solution)/shard_map/ppermute | solution.py:240
  867.8 46.0 %copy-start.1 = (s32[2,1,8]{2,1,0:T(1,128)S(1)}, s32[2,1,8]{2,1,0:T(1,128)}, u32[]{:S(2)}) copy-start(s32[2,1,8]{2,1,0:T(1,128)} %param.16) | copy-start | bytes 196
  867.9 44.7 %collective-permute-start.28 = (bf16[192,1536]{1,0:T(8,128)(2,1)S(1)}, bf16[192,1536]{1,0:T(8,128)(2,1)S(1)}, u32[]{:S(2)}, u32[]{:S(2)}) collective-permute-start(bf16[192,1536]{1,0:T(8,128)(2,1)S(1)} %add_convert_fusion.4), channel_id=1, source_target_pairs={{0,24},{8,16},{16,8},{24,0},{1,25},{9,17},{17,9},{25,1},{2,26},{10... | collective-permute-start | bytes 1769480 | tf_op jit(solution)/shard_map/ppermute | solution.py:240
  (43 other events, 183.9 us)

commit v2 on v1

--- a/solution.py
+++ b/solution.py
@@ -34,16 +34,106 @@
     return jnp.where(pick, value, jnp.zeros_like(value))
 
 
-def attend_kernel(own_ref, other_ref, mask_ref, out_ref, lse_ref, *, head, scale):
-    rows = own_ref.shape[1]
+def spread(order):
+    listed = []
+    for stage in range(len(order)):
+        for code in range(1 << stage):
+            listed.append((stage, tuple(order[i] for i in range(stage) if code >> i & 1)))
+    return listed
+
+
+def flipped(position, axis, mask):
+    bit = position[axis] // mask % 2
+    return {**position, axis: position[axis] + mask * (1 - 2 * bit)}
+
+
+def place_of(position, crossed):
+    for axis, mask in crossed:
+        position = flipped(position, axis, mask)
+    return position
+
+
+def here(axes):
+    return {axis: lax.axis_index(axis) for axis in axes}
+
+
+def bits_of(axis, size):
+    return [(axis, 1 << bit) for bit in range(size.bit_length() - 1)]
+
+
+def greet(partners):
+    barrier = pltpu.get_barrier_semaphore()
+    for axis, mask in partners:
+        target = flipped(here((axis,)), axis, mask)
+        pl.semaphore_signal(barrier, inc=1, device_id=target, device_id_type=pl.DeviceIdType.MESH)
+    pl.semaphore_wait(barrier, len(partners))
+
+
+class Gather:
+    def __init__(self, own, whole, order, sends, arrivals, base):
+        self.own, self.whole, self.order = own, whole, order
+        self.sends, self.arrivals, self.base = sends, arrivals, base
+        self.copies = spread(order)
+        self.position = here(("row", "col"))
+
+    def slot(self, position):
+        depth, columns = self.own.shape
+        first = pl.multiple_of(position["row"] * depth, 16)
+        start = pl.multiple_of(position["col"] * columns, LANES)
+        return self.whole.at[pl.ds(first, depth), pl.ds(start, columns)]
+
+    def copy(self, index):
+        stage, crossed = self.copies[index]
+        axis, mask = self.order[stage]
+        slot = self.slot(place_of(self.position, crossed))
+        return pltpu.make_async_remote_copy(
+            src_ref=slot if crossed else self.own,
+            dst_ref=slot,
+            send_sem=self.sends.at[self.base + index],
+            recv_sem=self.arrivals.at[self.base + index],
+            device_id=flipped(here((axis,)), axis, mask),
+            device_id_type=pl.DeviceIdType.MESH,
+        )
+
+    def arrival(self, index):
+        stage, crossed = self.copies[index]
+        axis, mask = self.order[stage]
+        slot = self.slot(place_of(self.position, crossed + (self.order[stage],)))
+        return pltpu.make_async_remote_copy(
+            src_ref=slot,
+            dst_ref=slot,
+            send_sem=self.sends.at[self.base + index],
+            recv_sem=self.arrivals.at[self.base + index],
+            device_id=flipped(here((axis,)), axis, mask),
+            device_id_type=pl.DeviceIdType.MESH,
+        )
+
+    def placing(self, semaphore):
+        return pltpu.make_async_copy(self.own, self.slot(self.position), semaphore)
+
+    def source(self, index):
+        crossed = self.copies[index][1]
+        last = self.order.index(crossed[-1])
+        return self.copies.index((last, crossed[:-1]))
+
+    def first(self):
+        return [i for i, (stage, crossed) in enumerate(self.copies) if not crossed]
+
+    def later(self):
+        return [i for i, (stage, crossed) in enumerate(self.copies) if crossed]
+
+
+def attend_step(q_ref, k_ref, v_ref, ok_ref, ov_ref, mask_ref, out_ref, lse_ref, *, head, exact):
+    rows = q_ref.shape[1]
     half = rows // 2
     heads = LANES // head
-    queries = own_ref[0, :, :LANES]
-    own_keys = own_ref[0, :, LANES : 2 * LANES] * jnp.asarray(scale, LOW)
-    own_values = own_ref[0, :, 2 * LANES :]
-    keys = cat([own_keys[:half], other_ref[0, :, :LANES] * jnp.asarray(scale, LOW)], axis=0)
+    scale = jnp.asarray(head**-0.5, LOW)
+    queries = q_ref[0]
+    own_keys = k_ref[0] * scale
+    own_values = v_ref[0]
+    keys = cat([own_keys[:half], ok_ref[0] * scale], axis=0)
     near = own_keys[half:]
-    values_t = cat([own_values[:half], other_ref[0, :, LANES:]], axis=0).T
+    values_t = cat([own_values[:half], ov_ref[0]], axis=0).T
     near_values_t = own_values[half:].T
     lane = lax.broadcasted_iota(jnp.int32, (1, LANES), 1) // head
     spans = [(start, start + CLEN) for start in range(0, half, CLEN)]
@@ -56,100 +146,311 @@
     def squares(value):
         return nt(chooser, value * value)
 
-    def run(exact):
-        flags = []
-        if not exact:
-            largest = jnp.maximum(
-                jnp.max(squares(keys), axis=1, keepdims=True),
-                jnp.max(squares(near), axis=1, keepdims=True),
-            )
-            bound = jnp.sqrt(squares(queries) * largest) * LOG2E
-        for part in range(2):
-            span = slice(part * half, (part + 1) * half)
-            query = queries[span]
-            outs = []
-            for h in range(heads):
-                pick = lane == h
-                lines = slice(h * head, (h + 1) * head)
-                scores = nt(only(pick, keys), query)
+    flags = []
+    if not exact:
+        largest = jnp.maximum(
+            jnp.max(squares(keys), axis=1, keepdims=True),
+            jnp.max(squares(near), axis=1, keepdims=True),
+        )
+        bound = jnp.sqrt(squares(queries) * largest) * LOG2E
+    for part in range(2):
+        span = slice(part * half, (part + 1) * half)
+        query = queries[span]
+        outs = []
+        for h in range(heads):
+            pick = lane == h
+            lines = slice(h * head, (h + 1) * head)
+            scores = nt(only(pick, keys), query)
+            if part:
+                near_keys = only(pick, near)
+                local = cat([nt(near_keys[a:b], query[a:b]) for a, b in spans], axis=1)
+                local = local + mask_ref[0]
+            if exact:
+                top = jnp.max(scores, axis=0, keepdims=True)
                 if part:
-                    near_keys = only(pick, near)
-                    local = cat([nt(near_keys[a:b], query[a:b]) for a, b in spans], axis=1)
-                    local = local + mask_ref[0]
-                if exact:
-                    top = jnp.max(scores, axis=0, keepdims=True)
-                    if part:
-                        top = jnp.maximum(top, jnp.max(local, axis=0, keepdims=True))
-                    top = top * LOG2E
-                else:
-                    top = bound[h : h + 1, span]
-                weights = jnp.exp2(scores * LOG2E - top).astype(LOW)
-                mixed = nn(with_ones(values_t[lines]), weights)
-                if part:
-                    weights = jnp.exp2(local * LOG2E - top).astype(LOW)
-                    value = with_ones(near_values_t[lines])
-                    mixed = mixed + cat(
-                        [nn(value[:, a:b], weights[:, a:b]) for a, b in spans], axis=1
-                    )
-                total = mixed[head : head + 1]
-                fine = jnp.logical_and(total > 1e-25, total < 1e30)
-                flags.append(jnp.where(fine, 0.0, 1.0))
-                outs.append(mixed[:head] / total)
-                lse_ref[0, 0, h : h + 1, span] = top + jnp.log2(total)
-            out_ref[0, span] = cat(outs, axis=0).T.astype(LOW)
-        return jnp.max(sum(flags[1:], flags[0]))
-
-    bad = run(False)
-
-    @pl.when(bad > 0.5)
+                    top = jnp.maximum(top, jnp.max(local, axis=0, keepdims=True))
+                top = top * LOG2E
+            else:
+                top = bound[h : h + 1, span]
+            weights = jnp.exp2(scores * LOG2E - top).astype(LOW)
+            mixed = nn(with_ones(values_t[lines]), weights)
+            if part:
+                weights = jnp.exp2(local * LOG2E - top).astype(LOW)
+                value = with_ones(near_values_t[lines])
+                mixed = mixed + cat([nn(value[:, a:b], weights[:, a:b]) for a, b in spans], axis=1)
+            total = mixed[head : head + 1]
+            fine = jnp.logical_and(total > 1e-25, total < 1e30)
+            flags.append(jnp.where(fine, 0.0, 1.0))
+            outs.append(mixed[:head] / total)
+            lse_ref[0, 0, h : h + 1, span] = top + jnp.log2(total)
+        out_ref[0, span] = cat(outs, axis=0).T.astype(LOW)
+    return sum(flags[1:], flags[0])
+
+
+def attend_again_kernel(*refs, head):
+    attend_step(*refs, head=head, exact=True)
+
+
+def attend_kernel(
+    q_ref, k_ref, v_ref, ok_ref, ov_ref, mask_ref, out_block, up_block, down_block,
+    out_ref, lse_ref, flag_ref, out_whole, up_whole, down_whole,
+    sends, arrivals, placed, *, head, grid,
+):
+    rows, columns = grid
+    steps = pl.num_programs(1)
+    step = pl.program_id(0) * steps + pl.program_id(1)
+    final = 2 * steps - 1
+    row_bits, col_bits = bits_of("row", rows), bits_of("col", columns)
+    first_order = tuple(col_bits + row_bits[::-1])
+    second_order = tuple(row_bits[:0:-1] + col_bits + row_bits[:1])
+    per = len(spread(first_order))
+    parts = [
+        Gather(out_block, out_whole, first_order, sends, arrivals, 0),
+        Gather(down_block, down_whole, first_order, sends, arrivals, per),
+        Gather(up_block, up_whole, second_order, sends, arrivals, 2 * per),
+    ]
+
+    @pl.when(step == 0)
     def _():
-        run(True)
-
-
-def attend(own, other, mask, head):
+        greet(row_bits + col_bits)
+        for index in parts[0].first():
+            for part in parts:
+                part.copy(index).start()
+        for number, part in enumerate(parts):
+            part.placing(placed.at[number]).start()
+
+    last = len(first_order) - 1
+    events = {}
+    for number, part in enumerate(parts):
+        for index in part.later():
+            stage, crossed = part.copies[index]
+            if len(crossed) > 1 and number:
+                when = final
+            elif stage == last:
+                when = (5, 8, 9)[number] + 2 * (len(crossed) > 1)
+            else:
+                when = (2, 6, 7)[number]
+            events.setdefault(min(when, final), []).append((part, index))
+    waited = set()
+    for when in sorted(events):
+        if when == final:
+            continue
+
+        @pl.when(step == when)
+        def _(batch=events[when]):
+            for part, index in batch:
+                origin = part.source(index)
+                if (part.base, origin) not in waited:
+                    waited.add((part.base, origin))
+                    part.arrival(origin).wait_recv()
+                part.copy(index).start()
+
+    flags = attend_step(
+        q_ref, k_ref, v_ref, ok_ref, ov_ref, mask_ref, out_ref, lse_ref, head=head, exact=False
+    )
+    flag_ref[0, 0] = jnp.broadcast_to(flags, flag_ref.shape[2:])
+
+    @pl.when(step == final)
+    def _():
+        for part, index in events.get(final, []):
+            origin = part.source(index)
+            if (part.base, origin) not in waited:
+                waited.add((part.base, origin))
+                part.arrival(origin).wait_recv()
+            part.copy(index).start()
+        for number, part in enumerate(parts):
+            part.placing(placed.at[number]).wait()
+            for index in range(per):
+                if (part.base, index) not in waited:
+                    part.arrival(index).wait_recv()
+                part.copy(index).wait_send()
+
+
+def attend_specs(own, other, mask):
     batch, rows, columns = own.shape
     steps = columns // (3 * LANES)
+
+    def spec(count, offset):
+        return pl.BlockSpec((1, count, LANES), lambda m, p: (m, 0, offset * steps + p))
+
+    ins = [
+        spec(rows, 0),
+        spec(rows, 1),
+        spec(rows, 2),
+        spec(rows // 2, 0),
+        spec(rows // 2, 1),
+        pl.BlockSpec((1,) + mask.shape[1:], lambda m, p: (m, 0, 0)),
+    ]
+    return batch, rows, steps, spec, ins
+
+
+def attend_again(own, other, mask, head):
+    batch, rows, steps, spec, ins = attend_specs(own, other, mask)
     heads = LANES // head
-    work = batch * rows * (rows + CLEN) * steps * LANES
-
-    def spec(count, width):
-        return pl.BlockSpec((1, count, width), lambda m, p: (m, 0, p))
-
     return pl.pallas_call(
-        functools.partial(attend_kernel, head=head, scale=head**-0.5),
+        functools.partial(attend_again_kernel, head=head),
         grid=(batch, steps),
-        in_specs=[
-            spec(rows, 3 * LANES),
-            spec(rows // 2, 2 * LANES),
-            pl.BlockSpec((1,) + mask.shape[1:], lambda m, p: (m, 0, 0)),
-        ],
-        out_specs=[
-            spec(rows, LANES),
-            pl.BlockSpec((1, 1, heads, rows), lambda m, p: (m, p, 0, 0)),
-        ],
+        in_specs=ins,
+        out_specs=[spec(rows, 0), pl.BlockSpec((1, 1, heads, rows), lambda m, p: (m, p, 0, 0))],
         out_shape=[
             jax.ShapeDtypeStruct((batch, rows, steps * LANES), LOW),
             jax.ShapeDtypeStruct((batch, steps, heads, rows), FULL),
         ],
+        name="attend_again",
+    )(own, own, own, other, other, mask)
+
+
+def attend(own, other, mask, blocks, grid, head):
+    batch, rows, steps, spec, ins = attend_specs(own, other, mask)
+    heads = LANES // head
+    half = rows // 2
+    anywhere = pl.BlockSpec(memory_space=pl.ANY)
+    copies = 3 * (grid[0] * grid[1] - 1)
+    work = batch * rows * (rows + CLEN) * steps * LANES
+    wholes = [
+        jax.ShapeDtypeStruct((block.shape[0] * grid[0], block.shape[1] * grid[1]), LOW)
+        for block in blocks
+    ]
+    out, lse, flags, *wholes = pl.pallas_call(
+        functools.partial(attend_kernel, head=head, grid=grid),
+        grid=(batch, steps),
+        in_specs=ins + [anywhere] * 3,
+        out_specs=[
+            spec(rows, 0),
+            pl.BlockSpec((1, 1, heads, rows), lambda m, p: (m, p, 0, 0)),
+            pl.BlockSpec((1, 1, 8, half), lambda m, p: (m, p, 0, 0)),
+        ]
+        + [anywhere] * 3,
+        out_shape=[
+            jax.ShapeDtypeStruct((batch, rows, steps * LANES), LOW),
+            jax.ShapeDtypeStruct((batch, steps, heads, rows), FULL),
+            jax.ShapeDtypeStruct((batch, steps, 8, half), FULL),
+        ]
+        + wholes,
+        scratch_shapes=[
+            pltpu.SemaphoreType.DMA((copies,)),
+            pltpu.SemaphoreType.DMA((copies,)),
+            pltpu.SemaphoreType.DMA((3,)),
+        ],
+        compiler_params=pltpu.CompilerParams(collective_id=1, has_side_effects=True),
         cost_estimate=pl.CostEstimate(
             flops=16 * work, bytes_accessed=own.size * 4, transcendentals=work // head
         ),
         name="attend",
-    )(own, other, mask)
+    )(own, own, own, other, other, mask, *blocks)
+    out, lse = lax.cond(
+        jnp.max(flags) > 0.5,
+        lambda: tuple(attend_again(own, other, mask, head)),
+        lambda: (out, lse),
+    )
+    return out, lse, wholes
+
+
+def begin_kernel(tokens_ref, block_ref, other_ref, whole_ref, sends, arrivals, placed, *, grid):
+    rows, columns = grid
+    row_bits, col_bits = bits_of("row", rows), bits_of("col", columns)
+    order = tuple(col_bits + row_bits[::-1])
+    part = Gather(block_ref, whole_ref, order, sends, arrivals, 0)
+    per = len(part.copies)
+    half = other_ref.shape[1]
+    partner = flipped(here(("col",)), "col", 1)
+    exchanges = [
+        pltpu.make_async_remote_copy(
+            src_ref=tokens_ref.at[m, pl.ds(0, half)],
+            dst_ref=other_ref.at[m],
+            send_sem=sends.at[per + m],
+            recv_sem=arrivals.at[per + m],
+            device_id=partner,
+            device_id_type=pl.DeviceIdType.MESH,
+        )
+        for m in range(other_ref.shape[0])
+    ]
+    greet(row_bits + col_bits)
+    for index in part.first():
+        part.copy(index).start()
+    for exchange in exchanges:
+        exchange.start()
+    part.placing(placed.at[0]).start()
+    waited = set()
+    for index in part.later():
+        origin = part.source(index)
+        if origin not in waited:
+            waited.add(origin)
+            part.arrival(origin).wait_recv()
+        part.copy(index).start()
+    for index in range(per):
+        if index not in waited:
+            part.arrival(index).wait_recv()
+        part.copy(index).wait_send()
+    part.placing(placed.at[0]).wait()
+    for exchange in exchanges:
+        exchange.wait()
+
+
+def begin(tokens, block, grid):
+    batch, rows, width = tokens.shape
+    copies = grid[0] * grid[1] - 1 + batch
+    anywhere = pl.BlockSpec(memory_space=pl.ANY)
+    return pl.pallas_call(
+        functools.partial(begin_kernel, grid=grid),
+        in_specs=[anywhere] * 2,
+        out_specs=[anywhere] * 2,
+        out_shape=[
+            jax.ShapeDtypeStruct((batch, rows // 2, width), LOW),
+            jax.ShapeDtypeStruct((block.shape[0] * grid[0], block.shape[1] * grid[1]), LOW),
+        ],
+        scratch_shapes=[
+            pltpu.SemaphoreType.DMA((copies,)),
+            pltpu.SemaphoreType.DMA((copies,)),
+            pltpu.SemaphoreType.DMA((1,)),
+        ],
+        compiler_params=pltpu.CompilerParams(collective_id=0, has_side_effects=True),
+        name="begin",
+    )(tokens, block)
 
 
 def attend_back_kernel(
-    own_ref, other_ref, mask_ref, out_ref, grad_ref, lse_ref, own_grad_ref, other_grad_ref,
-    *, head, scale,
+    q_ref, k_ref, v_ref, ok_ref, ov_ref, mask_ref, out_ref, grad_ref, lse_ref,
+    own_grad_ref, other_grad_ref, own_scratch, other_scratch, stored, *, head, scale,
 ):
-    rows = own_ref.shape[1]
+    rows = q_ref.shape[1]
     half = rows // 2
     heads = LANES // head
-    own_keys = own_ref[0, :, LANES : 2 * LANES] * jnp.asarray(scale, LOW)
-    own_values = own_ref[0, :, 2 * LANES :]
-    keys = cat([own_keys[:half], other_ref[0, :, :LANES] * jnp.asarray(scale, LOW)], axis=0)
+    steps = pl.num_programs(1)
+    group, tile = pl.program_id(0), pl.program_id(1)
+    step = group * steps + tile
+    slot = step % 2
+
+    def stores(group, tile, slot):
+        copies = []
+        for part in range(3):
+            lanes = pl.ds(pl.multiple_of((part * steps + tile) * LANES, LANES), LANES)
+            copies.append(
+                pltpu.make_async_copy(
+                    own_scratch.at[slot, part], own_grad_ref.at[group, :, lanes], stored.at[slot, part]
+                )
+            )
+        for part in range(2):
+            lanes = pl.ds(pl.multiple_of((part * steps + tile) * LANES, LANES), LANES)
+            copies.append(
+                pltpu.make_async_copy(
+                    other_scratch.at[slot, part],
+                    other_grad_ref.at[group, :, lanes],
+                    stored.at[slot, 3 + part],
+                )
+            )
+        return copies
+
+    @pl.when(step >= 2)
+    def _():
+        for copy in stores((step - 2) // steps, (step - 2) % steps, slot):
+            copy.wait()
+
+    own_keys = k_ref[0] * jnp.asarray(scale, LOW)
+    own_values = v_ref[0]
+    keys = cat([own_keys[:half], ok_ref[0] * jnp.asarray(scale, LOW)], axis=0)
     near = own_keys[half:]
-    values = cat([own_values[:half], other_ref[0, :, LANES:]], axis=0)
+    values = cat([own_values[:half], ov_ref[0]], axis=0)
     near_values = own_values[half:]
     keys_t = keys.T
     near_t = near.T
@@ -162,7 +463,7 @@
 
     for part in range(2):
         span = slice(part * half, (part + 1) * half)
-        query = own_ref[0, span, :LANES]
+        query = q_ref[0, span]
         grad = grad_ref[0, span]
         dots = (grad.astype(FULL) * out_ref[0, span].astype(FULL)).T
         query_grads = []
@@ -193,46 +494,54 @@
                 add(2, cat([nn(slopes[:, a:b], query_h[a:b]) for a, b in spans], axis=0))
                 add(3, cat([nn(probs[:, a:b], grad_h[a:b]) for a, b in spans], axis=0))
             query_grads.append(query_grad)
-        own_grad_ref[0, span, :LANES] = cat(query_grads, axis=0).T.astype(LOW)
+        own_scratch[slot, 0, span] = cat(query_grads, axis=0).T.astype(LOW)
     key_grad = (totals[0] * scale).astype(LOW)
     value_grad = totals[1].astype(LOW)
-    own_grad_ref[0, :half, LANES : 2 * LANES] = key_grad[:half]
-    own_grad_ref[0, :half, 2 * LANES :] = value_grad[:half]
-    other_grad_ref[0, :, :LANES] = key_grad[half:]
-    other_grad_ref[0, :, LANES:] = value_grad[half:]
-    own_grad_ref[0, half:, LANES : 2 * LANES] = (totals[2] * scale).astype(LOW)
-    own_grad_ref[0, half:, 2 * LANES :] = totals[3].astype(LOW)
+    own_scratch[slot, 1, :half] = key_grad[:half]
+    own_scratch[slot, 2, :half] = value_grad[:half]
+    own_scratch[slot, 1, half:] = (totals[2] * scale).astype(LOW)
+    own_scratch[slot, 2, half:] = totals[3].astype(LOW)
+    other_scratch[slot, 0] = key_grad[half:]
+    other_scratch[slot, 1] = value_grad[half:]
+    for copy in stores(group, tile, slot):
+        copy.start()
+
+    @pl.when(step == pl.num_programs(0) * steps - 1)
+    def _():
+        for copy in stores((step - 1) // steps, (step - 1) % steps, 1 - slot):
+            copy.wait()
+        for copy in stores(group, tile, slot):
+            copy.wait()
 
 
 def attend_back(own, other, mask, out, grad, lse, head):
-    batch, rows, columns = own.shape
-    steps = columns // (3 * LANES)
+    batch, rows, steps, spec, ins = attend_specs(own, other, mask)
     work = batch * rows * (rows + CLEN) * steps * LANES
-
-    def spec(count, width):
-        return pl.BlockSpec((1, count, width), lambda m, p: (m, 0, p))
-
+    anywhere = pl.BlockSpec(memory_space=pl.ANY)
     return pl.pallas_call(
         functools.partial(attend_back_kernel, head=head, scale=head**-0.5),
         grid=(batch, steps),
-        in_specs=[
-            spec(rows, 3 * LANES),
-            spec(rows // 2, 2 * LANES),
-            pl.BlockSpec((1,) + mask.shape[1:], lambda m, p: (m, 0, 0)),
-            spec(rows, LANES),
-            spec(rows, LANES),
+        in_specs=ins
+        + [
+            spec(rows, 0),
+            spec(rows, 0),
             pl.BlockSpec((1, 1) + lse.shape[2:], lambda m, p: (m, p, 0, 0)),
         ],
-        out_specs=[spec(rows, 3 * LANES), spec(rows // 2, 2 * LANES)],
+        out_specs=[anywhere] * 2,
         out_shape=[
             jax.ShapeDtypeStruct(own.shape, LOW),
             jax.ShapeDtypeStruct(other.shape, LOW),
+        ],
+        scratch_shapes=[
+            pltpu.VMEM((2, 3, rows, LANES), LOW),
+            pltpu.VMEM((2, 2, rows // 2, LANES), LOW),
+            pltpu.SemaphoreType.DMA((2, 5)),
         ],
         cost_estimate=pl.CostEstimate(
             flops=40 * work, bytes_accessed=own.size * 10, transcendentals=work // head
         ),
         name="attend_back",
-    )(own, other, mask, out, grad, lse)
+    )(own, own, own, other, other, mask, out, grad, lse)
 
 
 def swapped(value, axis, mask):
@@ -328,43 +637,41 @@
     batch, rows, width = inputs.shape
     half = rows // 2
     head = width // H
-    steps = width // LANES
     half_conts = cont_lengths.shape[2] // 2
     group_lengths = lax.dynamic_index_in_dim(cont_lengths, place // 2, 1, keepdims=False)
     lengths = lax.dynamic_slice_in_dim(group_lengths, side * half_conts, half_conts, 1)
     mask = near_mask(lengths, half)
 
-    other_tokens = swapped(inputs[:, :half], "col", 1).reshape(batch * half, width)
+    grid = (grid_rows, grid_cols)
+    direct = out_weight.shape[1] % LANES == 0 and qkv_weight.shape[1] % LANES == 0
+    blocks = (out_weight, up_weight, down_weight)
     tokens = inputs.reshape(batch * rows, width)
-
-    def by_step(matrix):
-        lead = matrix.shape[0]
-        shaped = matrix.reshape(lead, 3, steps, LANES)
-        return shaped.transpose(0, 2, 1, 3)
-
-    qkv_matrix = by_step(gathered(qkv_weight))
-    pair_matrix = qkv_matrix[:, :, 1:].reshape(width, 2 * width)
-    qkv_matrix = qkv_matrix.reshape(width, 3 * width)
-    shift = by_step(
-        cat([vectors[:, 0], jnp.zeros((width,), FULL), vectors[:, 1]])[None]
-    )
-    pair_shift = shift[:, :, 1:].reshape(1, 2 * width)
-    shift = shift.reshape(1, 3 * width)
+    if direct:
+        other_tokens, qkv_matrix = begin(inputs, qkv_weight, grid)
+    else:
+        other_tokens = swapped(inputs[:, :half], "col", 1)
+        qkv_matrix = gathered(qkv_weight)
+    other_tokens = other_tokens.reshape(batch * half, width)
+    pair_matrix = qkv_matrix[:, width:]
+    shift = cat([vectors[:, 0], jnp.zeros((width,), FULL), vectors[:, 1]])
+    pair_shift = shift[width:]
     own = (nn(tokens, qkv_matrix) + shift).astype(LOW).reshape(batch, rows, 3 * width)
     other = (nn(other_tokens, pair_matrix) + pair_shift).astype(LOW)
     other = other.reshape(batch, half, 2 * width)
-    attended, lse = attend(own, other, mask, head)
-
-    out_matrix = gathered(out_weight)
-    up_matrix = gathered(up_weight)
-    down_matrix = gathered(down_weight)
+    if direct:
+        attended, lse, (out_matrix, up_matrix, down_matrix) = attend(
+            own, other, mask, blocks, grid, head
+        )
+    else:
+        attended, lse = attend_again(own, other, mask, head)
+        out_matrix, up_matrix, down_matrix = (gathered(block) for block in blocks)
     attended = attended.reshape(batch * rows, width)
     first_sum = tokens.astype(FULL) + nn(attended, out_matrix) + vectors[:, 2]
     first_normed, first_inverse = normalize(first_sum)
     hidden = first_normed * vectors[:, 3] + vectors[:, 4]
     hidden_low = hidden.astype(LOW)
     pre_act = nn(hidden_low, up_matrix) + up_bias
-    phi = 0.5 * lax.erfc(pre_act * (-(0.5**0.5)))
+    phi = 0.5 + 0.5 * lax.erf(pre_act * (0.5**0.5))
     slope = phi + pre_act * (jnp.exp(-0.5 * pre_act * pre_act) * ((2 * math.pi) ** -0.5))
     act_low = (pre_act * phi).astype(LOW)
     slope_low = slope.astype(LOW)
@@ -401,17 +708,16 @@
     grad_tokens = (grad_first + nt(own_grad, qkv_matrix)).reshape(batch, rows, width)
     grad_tokens = cat([grad_tokens[:, :half] + received, grad_tokens[:, half:]], axis=1)
     grad_tokens = grad_tokens.astype(LOW)
-    qkv_total = tn(tokens, own_grad).reshape(width, steps, 3, LANES)
-    pair_total = tn(other_tokens, other_grad).reshape(width, steps, 2, LANES)
-    qkv_total = cat([qkv_total[:, :, :1], qkv_total[:, :, 1:] + pair_total], axis=2)
-    qkv_total = qkv_total.transpose(0, 2, 1, 3).reshape(width, 3 * width)
+    qkv_total = tn(tokens, own_grad)
+    pair_total = tn(other_tokens, other_grad)
+    qkv_total = cat([qkv_total[:, :width], qkv_total[:, width:] + pair_total], axis=1)
     qkv_grad = scattered(qkv_total, qkv_weight.shape)
 
-    own_sum = jnp.sum(own_grad.astype(FULL), axis=0).reshape(steps, 3, LANES)
-    other_sum = jnp.sum(other_grad.astype(FULL), axis=0).reshape(steps, 2, LANES)
+    own_sum = jnp.sum(own_grad.astype(FULL), axis=0)
+    other_sum = jnp.sum(other_grad.astype(FULL), axis=0)
     sums = [
-        own_sum[:, 0].reshape(width),
-        (own_sum[:, 2] + other_sum[:, 1]).reshape(width),
+        own_sum[:width],
+        own_sum[2 * width :] + other_sum[width:],
         jnp.sum(grad_first, axis=0),
         jnp.sum(grad_hidden * first_normed, axis=0),
         jnp.sum(grad_hidden, axis=0),

time: 921 us -> 756 us (0.82)
  waiting for transfers between devices: 242 us -> 129 us
  Pallas kernels: 140 us -> 233 us
  local copies, waits for them, and re-layouts: 134 us -> 70.2 us
  matrix products: 241 us -> 182 us
  other arithmetic: 81.2 us -> 58.1 us
  loops' own time: 0 us -> 11.3 us
  starting transfers between devices: 32.1 us -> 21.5 us
    ppermute x34 -> x21, waiting for transfers between devices: 242 us -> 129 us  [swapped(): return lax.ppermute(value, axis, pairs)]
    pallas_call x1 -> x3, Pallas kernels: 63.1 us -> 155 us  [the longest x1 55.9 us: attend(): pl.pallas_call(functools.partial(attend_kernel, head=head, grid=grid), gr...]
    dot_general x5, matrix products: 106 us -> 53.3 us  [nn(): lax.dot_general(left, right, (((1,), (0,)), ((), ())), preferred_element_...]
    another operation x13 -> x0, local copies, waits for them, and re-layouts: 28.7 us -> none  [the longest x7 11 us: joined(): jnp.stack([jnp.where(first, value, other), jnp.where(first, other, value)...]
    another operation x21 -> x1, other arithmetic: 16.7 us -> 3.17 us  [the longest x20 16.3 us: joined(): jnp.stack([jnp.where(first, value, other), jnp.where(first, other, value)...]
    dot_general x5, matrix products: 60.6 us -> 47.6 us  [tn(): lax.dot_general(left, right, (((0,), (0,)), ((), ())), preferred_element_...]
    slice x7 -> x1, local copies, waits for them, and re-layouts: 12.4 us -> 0.15 us  [local(): qkv_total[:, :width]]
    another operation x0 -> x1, loops' own time: none -> 11.3 us  [attend(): lax.cond(jnp.max(flags) > 0.5, lambda: tuple(attend_again(own, other, mas...]
  transfers between devices with their start and end apart: 34 -> 21, of which waited for: 16 -> 12; matrix products, arithmetic and copies ran while one was open for 22% -> 27% of each run, Pallas kernels for 7% -> 10%
where the time goes in v2:
time: 756 us; the launch traced here: 748 us
  Pallas kernels  233 us (31%)
  matrix products  182 us (24%)
  waiting for transfers between devices  129 us (17%)
  local copies, waits for them, and re-layouts  70.2 us (9%)
  other arithmetic  58.1 us (8%)
  blocking collectives  40 us (5%)
  starting transfers between devices  21.5 us (3%)
  loops' own time  11.3 us (1%)
    ppermute x21, waiting for transfers between devices, swapped(): return lax.ppermute(value, axis, pairs)  129 us
    dot_general x5, matrix products, nt(): lax.dot_general(left, right, (((1,), (1,)), ((), ())), preferred_element_...  81.3 us
    pallas_call x1, Pallas kernels, attend_back(): pl.pallas_call(functools.partial(attend_back_kernel, head=head, scale=hea...  78.5 us
    pallas_call x1, Pallas kernels, attend(): pl.pallas_call(functools.partial(attend_kernel, head=head, grid=grid), gr...  55.9 us
    dot_general x5, matrix products, nn(): lax.dot_general(left, right, (((1,), (0,)), ((), ())), preferred_element_...  53.3 us
    pallas_call x1, Pallas kernels, attend_again(): pl.pallas_call(functools.partial(attend_again_kernel, head=head), grid=(b...  51.8 us
    dot_general x5, matrix products, tn(): lax.dot_general(left, right, (((0,), (0,)), ((), ())), preferred_element_...  47.6 us
    pallas_call x1, Pallas kernels, begin(): pl.pallas_call(functools.partial(begin_kernel, grid=grid), in_specs=[anyw...  47.1 us
  transfers between devices with their start and end apart: 21, of which 12 were waited for; matrix products, arithmetic and copies ran while one was open for 27% of the time, Pallas kernels for 10%

profile of v2, /device:TPU:8, one launch (start us, length us, event | category | flops | bytes accessed | tf_op | source)
XLA Modules:
  0.0 747.9 jit_solution(6278130359822789081)
XLA Ops:
  2.6 3.9 convert_reduce_fusion.1
  7.5 47.1 %begin.1 = (bf16[2,512,768]{2,1,0:T(8,128)(2,1)}, bf16[768,2304]{1,0:T(8,128)(2,1)}) custom-call(bf16[2,1024,768]{2,1,0:T(8,128)(2,1)} %tokens_ref.1, bf16[192,1152]{1,0:T(8,128)(2,1)} %block_ref.1), custom_call_target="tpu_custom_call" | custom-call | tf_op jit(solution)/shard_map/begin/pallas_call | solution.py:394
  54.6 4.9 add_convert_fusion.2
  59.5 9.9 %add_convert_fusion = bf16[2304,2048]{0,1:T(8,128)(2,1)} fusion(bf16[2048,768]{1,0:T(8,128)(2,1)S(1)} %bitcast.166, bf16[768,2304]{1,0:T(8,128)(2,1)S(1)} %copy-done.30, f32[2304]{0:T(1024)S(1)} %pad_maximum_fusion.2), kind=kOutput, calls=%fused_computation.10 | convolution fusion | flops 7257194496 | bytes 16131072 | tf_op jit(solution)/shard_map/dot_general | solution.py:26
  69.4 55.9 %attend.1 = (bf16[2,1024,768]{2,1,0:T(8,128)(2,1)}, f32[2,6,2,1024]{3,2,1,0:T(2,128)}, f32[2,6,8,512]{3,2,1,0:T(8,128)}, bf16[768,768]{1,0:T(8,128)(2,1)}, bf16[...) custom-call(bf16[2,1024,2304]{2,1,0:T(8,128)(2,1)} %bitcast.129, bf16[2,1024,2304]{2,1,0:T(8,128)(2,1)} %bitcast.130, ...), custom_call_target="tpu_custom_call" | custom-call | flops 28991029248 | bytes 18874368 | tf_op jit(solution)/shard_map/attend/pallas_call | solution.py:314
  127.6 65.2 %conditional.1 = (bf16[2,1024,768]{2,1,0:T(8,128)(2,1)}, f32[2,6,2,1024]{3,2,1,0:T(2,128)}, bf16[2048,768]{1,0:T(8,128)(2,1)S(1)}) conditional(s32[]{:T(128)} %convert_element_type.247, (bf16[2,1024,768]{2,1,0:T(8,128)(2,1)}, f32[2,6,2,1024]{3,2,1,0:T(2,128)}) %tuple.32, (bf16[2,1024,2304]{2,1,0:T(8,128)(2,1)}, bf16[2,512,1536]{2,1,0:T(8,128)(2,1)S(1)}, ...), branch_computations={%region_1.2_spmd, %region_2.3_spmd} | conditional | bytes 12582936 | solution.py:341
  138.9 51.8 %attend_again.3 = (bf16[2,1024,768]{2,1,0:T(8,128)(2,1)}, f32[2,6,2,1024]{3,2,1,0:T(2,128)}) custom-call(bf16[2,1024,2304]{2,1,0:T(8,128)(2,1)} %get-tuple-element.42.refs_0_.refs_1_.refs_2_, bf16[2,1024,2304]{2,1,0:T(8,128)(2,1)} %get-tuple-element.42.refs_0_.refs_1_.refs_2_, bf16[2,1024,2304]{2,1,0:T(8,128)(2,1)} %get-tuple-element.42.refs_0_.refs_1_.refs_2_, ...), custom_call_target="tpu_custom_call" | custom-call | tf_op jit(solution)/shard_map/cond/branch_1_fun/attend_again/pallas_call | solution.py:290
  192.9 6.5 fusion.56
  200.2 18.4 %multiply_convert_fusion = (bf16[2048,3072]{1,0:T(8,128)(2,1)}, f32[2048,3072]{1,0:T(8,128)}) fusion(f32[3072]{0:T(1024)S(1)} %copy-done.32, bf16[768,3072]{1,0:T(8,128)(2,1)S(1)} %bitcast.178, f32[2048,768]{1,0:T(8,128)S(1)} %get-tuple-element.122, f32[768]{0:T(1024)S(1)} %get-tuple-element.108, f32[768]{0:T(1024)S(1)} %get-tuple-element.109, ...), kind=kOutput, calls=%fused_computation.7 | convolution fusion | flops 9709289472 | bytes 48793600 | tf_op jit(solution)/shard_map/dot_general | solution.py:26
  218.7 13.6 %fusion.57 = (f32[2048]{0:T(1024)S(1)}, f32[2048,768]{1,0:T(8,128)S(1)}) fusion(f32[768]{0:T(1024)S(1)} %get-tuple-element.107, bf16[2048,3072]{1,0:T(8,128)(2,1)} %get-tuple-element.123, bf16[3072,768]{1,0:T(8,128)(2,1)S(1)} %bitcast.180, f32[768]{0:T(1024)S(1)} %get-tuple-element.108, f32[768]{0:T(1024)S(1)} %get-tuple-element.109, ...), kind=kOutput, calls=%fused_computation.157 | convolution fusion | flops 9674684416 | bytes 29918208 | tf_op jit(solution)/shard_map/dot_general | solution.py:26
  234.2 2.9 fusion.13
  237.1 4.4 fusion.53
  241.6 2.6 copy-done.14
  244.2 15.6 %fusion.28 = f32[3072,768]{1,0:T(8,128)} fusion(bf16[2048,3072]{1,0:T(8,128)(2,1)} %get-tuple-element.123, f32[2048,768]{1,0:T(8,128)S(1)} %get-tuple-element.117), kind=kOutput, calls=%fused_computation.71 | convolution fusion | flops 9665249280 | bytes 28311552 | tf_op jit(solution)/shard_map/dot_general | solution.py:30
  259.8 2.6 constant_dynamic-slice_fusion.1
  262.4 2.5 copy.54
  264.9 4.9 copy.36
  269.7 31.9 %fusion.5 = (f32[3072]{0:T(1024)}, bf16[2048,3072]{1,0:T(8,128)(2,1)}, f32[2048,3072]{1,0:T(8,128)}) fusion(f32[2048,3072]{1,0:T(8,128)} %get-tuple-element.124, f32[3072]{0:T(1024)S(1)} %copy-done.32, bf16[3072,768]{1,0:T(8,128)(2,1)} %get-tuple-element.73, f32[2048,768]{1,0:T(8,128)} %copy-done.14), kind=kOutput, calls=%fused_computation.11 | convolution fusion | flops 9747035136 | bytes 73949184 | tf_op jit(solution)/shard_map/dot_general | solution.py:22
  301.7 25.0 %multiply_reduce_fusion = (f32[768]{0:T(1024)}, f32[2048]{0:T(1024)S(1)}, f32[2048]{0:T(1024)S(1)}, f32[768]{0:T(1024)}, f32[2048,768]{1,0:T(8,128)}) fusion(f32[2048,768]{1,0:T(8,128)S(1)} %bitcast.137, f32[2048]{0:T(1024)S(1)} %add_rsqrt_fusion.1, f32[2048]{0:T(1024)S(1)} %broadcast_multiply_fusion.4, f32[768]{0:T(1024)S(1)} %get-tuple-element.109, ...), kind=kOutput, calls=%fused_computation.25 | convolution fusion | flops 9698273280 | bytes 61383680 | tf_op jit(solution)/shard_map/dot_general | solution.py:22
  326.6 5.3 fusion.55
  331.9 2.6 fusion.16
  337.4 4.1 convolution_convert_fusion
  341.5 78.5 %attend_back.1 = (bf16[2,1024,2304]{2,1,0:T(8,128)(2,1)}, bf16[2,512,1536]{2,1,0:T(8,128)(2,1)}) custom-call(bf16[2,1024,2304]{2,1,0:T(8,128)(2,1)} %bitcast.133, bf16[2,1024,2304]{2,1,0:T(8,128)(2,1)} %bitcast.134, bf16[2,1024,2304]{2,1,0:T(8,128)(2,1)} %bitcast.135, bf16[2,512,1536]{2,1,0:T(8,128)(2,1)S(1)} %bitcast.153, ...), custom_call_target="tpu_custom_call" | custom-call | flops 72477573120 | bytes 47185920 | tf_op jit(solution)/shard_map/attend_back/pallas_call | solution.py:521
  420.0 6.6 fusion.23
  427.5 7.6 %convolution_bitcast_fusion = f32[768,2304]{0,1:T(8,128)S(1)} fusion(bf16[2,1024,2304]{2,1,0:T(8,128)(2,1)S(1)} %copy-done.10, bf16[2,1024,768]{2,1,0:T(8,128)(2,1)S(1)} %copy-done.16), kind=kOutput, calls=%fused_computation.38 | convolution fusion | flops 7247757312 | bytes 19660800 | tf_op jit(solution)/shard_map/dot_general | solution.py:30
  435.1 2.7 slice_add_fusion
  438.0 3.8 pad_maximum_fusion
  441.8 8.0 %copy.35 = f32[768,2304]{1,0:T(8,128)} copy(f32[768,2304]{0,1:T(8,128)} %pad_maximum_fusion) | data formatting | bytes 14155776 | tf_op jit(solution)/shard_map/concatenate | solution.py:713
  449.8 3.4 fusion.22
  453.2 19.1 %fusion.46 = f32[768,3072]{1,0:T(8,128)S(1)} fusion(f32[2048,3072]{1,0:T(8,128)} %get-tuple-element.127, bf16[2048,3072]{1,0:T(8,128)(2,1)} %get-tuple-element.115, f32[2048,768]{1,0:T(8,128)} %copy-done.2, f32[768]{0:T(1024)S(1)} %copy-done.22, f32[768]{0:T(1024)S(1)} %get-tuple-element.109, f32[2048]{0:T(1024)S(1)} %add_rsqrt_fusion.1, ...), kind=kOutput, calls=%fused_computation.152 | convolution fusion | flops 9690415104 | bytes 53499904 | tf_op jit(solution)/shard_map/dot_general | solution.py:30
  472.3 3.7 copy-done.3
  478.2 2.4 convert_reduce_fusion.2
  480.6 5.0 convert_reduce_fusion
  485.7 13.8 %convolution_add_fusion.1 = f32[2048,768]{1,0:T(8,128)} fusion(f32[2048,768]{1,0:T(8,128)} %copy-done.13, bf16[2048,2304]{1,0:T(8,128)(2,1)} %bitcast.157, bf16[768,2304]{1,0:T(8,128)(2,1)} %get-tuple-element.65), kind=kOutput, calls=%fused_computation.49 | convolution fusion | flops 7249330176 | bytes 25559040 | tf_op jit(solution)/shard_map/dot_general | solution.py:22
  502.0 4.8 constant_dynamic-slice_fusion.2
  506.8 3.0 collective-permute-done.7
  511.9 3.8 collective-permute-done.8
  516.4 4.6 collective-permute-done.9
  521.0 2.3 collective-permute-start.10
  523.3 40.0 %psum.7 = f32[9216]{0:T(1024)S(1)} all-reduce(f32[9216]{0:T(1024)S(1)} %constant_dynamic-update-slice_fusion), channel_id=1, replica_groups=mesh['dp'=4,'row'=4,'col'=2] {'dp','row','col'}, use_global_device_ids=true, to_apply=%region_20.21 | all-reduce | flops 9216 | bytes 73728 | tf_op jit(solution)/shard_map/psum | solution.py:729
  563.4 6.0 copy.39
  569.4 2.0 slice.121
  573.5 3.2 fusion.15
  578.6 2.3 bitcast_add_fusion.2
  581.1 2.2 collective-permute-start.2
  583.3 2.2 bitcast_add_fusion
  588.1 2.6 bitcast_add_fusion.1
  590.8 2.1 copy-done.5
  594.9 8.9 %collective-permute-done.2 = bf16[1,192,2304]{2,1,0:T(8,128)(2,1)S(1)} collective-permute-done((bf16[1,192,2304]{2,1,0:T(8,128)(2,1)S(1)}, bf16[1,192,2304]{2,1,0:T(8,128)(2,1)S(1)}, u32[]{:S(2)}, u32[]{:S(2)}) %collective-permute-start.2) | collective-permute-done | bytes 884768 | tf_op jit(solution)/shard_map/ppermute | solution.py:549
  605.2 2.4 reshape_reshape.23
  609.3 2.1 collective-permute-start.3
  612.2 17.0 %collective-permute-done.17 = bf16[1,768,768]{1,2,0:T(8,128)(2,1)} collective-permute-done((bf16[1,768,768]{1,2,0:T(8,128)(2,1)}, bf16[1,768,768]{1,2,0:T(8,128)(2,1)}, u32[]{:S(2)}, u32[]{:S(2)}) %collective-permute-start.17) | collective-permute-done | bytes 1179680 | tf_op jit(solution)/shard_map/ppermute | solution.py:549
  629.2 2.3 convert_add_fusion
  632.4 2.1 collective-permute-start.18
  634.6 18.0 %collective-permute-done.12 = bf16[1,192,3072]{2,1,0:T(8,128)(2,1)} collective-permute-done((bf16[1,192,3072]{2,1,0:T(8,128)(2,1)}, bf16[1,192,3072]{2,1,0:T(8,128)(2,1)}, u32[]{:S(2)}, u32[]{:S(2)}) %collective-permute-start.12) | collective-permute-done | bytes 1179680 | tf_op jit(solution)/shard_map/ppermute | solution.py:549
  652.6 3.0 convert_add_fusion.1
  655.6 3.6 reshape_reshape.26
  665.7 2.0 collective-permute-start.19
  667.7 6.2 collective-permute-done.13
  674.1 2.3 collective-permute-done.4
  677.2 11.8 %collective-permute-done.19 = bf16[768,384]{0,1:T(8,128)(2,1)S(1)} collective-permute-done((bf16[768,384]{0,1:T(8,128)(2,1)S(1)}, bf16[768,384]{0,1:T(8,128)(2,1)S(1)}, u32[]{:S(2)}, u32[]{:S(2)}) %collective-permute-start.19) | collective-permute-done | bytes 589856 | tf_op jit(solution)/shard_map/ppermute | solution.py:549
  689.9 11.8 %collective-permute-done.14 = bf16[192,1536]{1,0:T(8,128)(2,1)S(1)} collective-permute-done((bf16[192,1536]{1,0:T(8,128)(2,1)S(1)}, bf16[192,1536]{1,0:T(8,128)(2,1)S(1)}, u32[]{:S(2)}, u32[]{:S(2)}) %collective-permute-start.14) | collective-permute-done | bytes 589856 | tf_op jit(solution)/shard_map/ppermute | solution.py:549
  703.5 33.0 %collective-permute-done.20 = bf16[768,384]{0,1:T(8,128)(2,1)S(1)} collective-permute-done((bf16[768,384]{0,1:T(8,128)(2,1)S(1)}, bf16[768,384]{0,1:T(8,128)(2,1)S(1)}, u32[]{:S(2)}, u32[]{:S(2)}) %collective-permute-start.20) | collective-permute-done | bytes 589856 | tf_op jit(solution)/shard_map/ppermute | solution.py:549
  738.1 8.4 %collective-permute-done.15 = bf16[192,1536]{1,0:T(8,128)(2,1)S(1)} collective-permute-done((bf16[192,1536]{1,0:T(8,128)(2,1)S(1)}, bf16[192,1536]{1,0:T(8,128)(2,1)S(1)}, u32[]{:S(2)}, u32[]{:S(2)}) %collective-permute-start.15) | collective-permute-done | bytes 589856 | tf_op jit(solution)/shard_map/ppermute | solution.py:549
  (202 shorter events, 47.1 us)
Async XLA Ops:
  2.6 216.1 %copy-start.21 = (f32[768]{0:T(1024)}, f32[768]{0:T(1024)S(1)}, u32[]{:S(2)}) copy-start(f32[768]{0:T(1024)S(1)} %get-tuple-element.108) | copy-start | bytes 9220
  54.6 4.9 copy-start.15
  54.6 4.9 copy-start.30
  59.5 68.1 %copy-start.7 = (bf16[1024,1536]{1,0:T(8,128)(2,1)}, bf16[1024,1536]{1,0:T(8,128)(2,1)S(1)}, u32[]{:S(2)}) copy-start(bf16[1024,1536]{1,0:T(8,128)(2,1)S(1)} %add_convert_fusion.2) | copy-start | bytes 9437188
  192.8 6.5 copy-start.9
  192.8 7.3 slice-start.11
  192.8 7.3 slice-start.12
  199.3 19.4 %copy-start.2 = (f32[2048,768]{1,0:T(8,128)}, f32[2048,768]{1,0:T(8,128)S(1)}, u32[]{:S(2)}) copy-start(f32[2048,768]{1,0:T(8,128)S(1)} %get-tuple-element.122) | copy-start | bytes 18874372
  199.4 19.3 %slice-start.13 = ((s8[4718592]{0:T(1024)(128)(4,1)}), s8[4194304]{0:T(1024)(128)(4,1)S(1)}, s32[]{:S(2)}) async-start(s8[4718592]{0:T(1024)(128)(4,1)} %bitcast.179), calls=%async_computation.13 | async-start | bytes 8388608
  200.2 18.5 %slice-start.14 = ((s8[4718592]{0:T(1024)(128)(4,1)}), s8[524288]{0:T(1024)(128)(4,1)S(1)}, s32[]{:S(2)}) async-start(s8[4718592]{0:T(1024)(128)(4,1)} %bitcast.179), calls=%async_computation.14 | async-start | bytes 1048576
  264.9 318.5 %collective-permute-start.16 = (bf16[2,768,768]{1,2,0:T(8,128)(2,1)}, bf16[2,768,768]{1,2,0:T(8,128)(2,1)}, u32[]{:S(2)}, u32[]{:S(2)}) collective-permute-start(bf16[2,768,768]{1,2,0:T(8,128)(2,1)} %bitcast.169), channel_id=1, source_target_pairs={{0,2},{2,0},{4,6},{6,4},{1,3},{3,1},{5,7},{7,5},{8,10},{10,8},{12,... | collective-permute-start | bytes 7077896 | tf_op jit(solution)/shard_map/ppermute | solution.py:549
  264.9 36.8 %slice-start = ((s8[6291456]{0:T(1024)(128)(4,1)}), s8[2097152]{0:T(1024)(128)(4,1)S(1)}, s32[]{:S(2)}) async-start(s8[6291456]{0:T(1024)(128)(4,1)} %bitcast.136), calls=%async_computation | async-start | bytes 4194304
  269.7 31.9 %slice-start.1 = ((s8[6291456]{0:T(1024)(128)(4,1)}), s8[4194304]{0:T(1024)(128)(4,1)S(1)}, s32[]{:S(2)}) async-start(s8[6291456]{0:T(1024)(128)(4,1)} %bitcast.136), calls=%async_computation.1 | async-start | bytes 8388608
  326.6 5.3 copy-start.18
  331.9 5.5 copy-start.13
  331.9 5.5 copy-start.34
  336.9 4.6 copy-start.8
  336.9 4.6 copy-start.33
  336.9 162.6 %collective-permute-start.6 = (bf16[2,192,768]{2,1,0:T(8,128)(2,1)}, bf16[2,192,768]{2,1,0:T(8,128)(2,1)}, u32[]{:S(2)}, u32[]{:S(2)}) collective-permute-start(bf16[2,192,768]{2,1,0:T(8,128)(2,1)} %fusion.35), channel_id=1, source_target_pairs={{0,2},{2,0},{4,6},{6,4},{1,3},{3,1},{5,7},{7,5},{8,10},{10,8},{12,... | collective-permute-start | bytes 1769480 | tf_op jit(solution)/shard_map/ppermute | solution.py:549
  420.0 7.5 %copy-start.10 = (bf16[2,1024,2304]{2,1,0:T(8,128)(2,1)S(1)}, bf16[2,1024,2304]{2,1,0:T(8,128)(2,1)}, u32[]{:S(2)}) copy-start(bf16[2,1024,2304]{2,1,0:T(8,128)(2,1)} %get-tuple-element.75) | copy-start | bytes 28311556
  420.0 7.5 %copy-start.16 = (bf16[2,1024,768]{2,1,0:T(8,128)(2,1)S(1)}, bf16[2,1024,768]{2,1,0:T(8,128)(2,1)}, u32[]{:S(2)}) copy-start(bf16[2,1024,768]{2,1,0:T(8,128)(2,1)} %tokens_ref.1) | copy-start | bytes 9437188
  426.5 147.0 %collective-permute-start = (bf16[2,512,768]{2,1,0:T(8,128)(2,1)}, bf16[2,512,768]{2,1,0:T(8,128)(2,1)}, u32[]{:S(2)}, u32[]{:S(2)}) collective-permute-start(bf16[2,512,768]{2,1,0:T(8,128)(2,1)} %bitcast.15), channel_id=1, source_target_pairs={{0,1},{1,0},{2,3},{3,2},{4,5},{5,4},{6,7},{7,6},{8,9},{9,8},{10,11... | collective-permute-start | bytes 4718600 | tf_op jit(solution)/shard_map/ppermute | solution.py:549
  427.5 7.6 %copy-start.17 = (bf16[2,512,1536]{2,1,0:T(8,128)(2,1)S(1)}, bf16[2,512,1536]{2,1,0:T(8,128)(2,1)}, u32[]{:S(2)}) copy-start(bf16[2,512,1536]{2,1,0:T(8,128)(2,1)} %get-tuple-element.76) | copy-start | bytes 9437188
  427.5 7.6 %copy-start.31 = (bf16[2,512,768]{2,1,0:T(8,128)(2,1)S(1)}, bf16[2,512,768]{2,1,0:T(8,128)(2,1)}, u32[]{:S(2)}) copy-start(bf16[2,512,768]{2,1,0:T(8,128)(2,1)} %get-tuple-element.66) | copy-start | bytes 4718596
  441.8 11.4 %copy-start.22 = (f32[768]{0:T(1024)S(1)}, f32[768]{0:T(1024)}, u32[]{:S(2)}) copy-start(f32[768]{0:T(1024)} %copy-done.21) | copy-start | bytes 9220
  453.2 125.4 %collective-permute-start.1 = (bf16[2,192,2304]{2,1,0:T(8,128)(2,1)}, bf16[2,192,2304]{2,1,0:T(8,128)(2,1)}, u32[]{:S(2)}, u32[]{:S(2)}) collective-permute-start(bf16[2,192,2304]{2,1,0:T(8,128)(2,1)} %fusion.22), channel_id=1, source_target_pairs={{0,2},{2,0},{4,6},{6,4},{1,3},{3,1},{5,7},{7,5},{8,10},{10,8},{12,... | collective-permute-start | bytes 5308424 | tf_op jit(solution)/shard_map/ppermute | solution.py:549
  472.3 3.7 copy-start.3
  477.7 110.4 %collective-permute-start.11 = (bf16[2,192,3072]{2,1,0:T(8,128)(2,1)}, bf16[2,192,3072]{2,1,0:T(8,128)(2,1)}, u32[]{:S(2)}, u32[]{:S(2)}) collective-permute-start(bf16[2,192,3072]{2,1,0:T(8,128)(2,1)} %fusion.18), channel_id=1, source_target_pairs={{0,2},{2,0},{4,6},{6,4},{1,3},{3,1},{5,7},{7,5},{8,10},{10,8},{12,... | collective-permute-start | bytes 7077896 | tf_op jit(solution)/shard_map/ppermute | solution.py:549
  485.6 13.9 %copy-start.26 = (f32[768]{0:T(1024)S(1)}, f32[768]{0:T(1024)}, u32[]{:S(2)}) copy-start(f32[768]{0:T(1024)} %get-tuple-element.118) | copy-start | bytes 9220
  485.6 13.9 %copy-start.29 = (f32[768]{0:T(1024)S(1)}, f32[768]{0:T(1024)}, u32[]{:S(2)}) copy-start(f32[768]{0:T(1024)} %get-tuple-element.98) | copy-start | bytes 9220
  485.6 13.9 %copy-start.20 = (f32[2,2,192,768]{3,2,1,0:T(8,128)S(1)}, f32[2,2,192,768]{3,2,1,0:T(8,128)}, u32[]{:S(2)}) copy-start(f32[2,2,192,768]{3,2,1,0:T(8,128)} %copy-done.19) | copy-start | bytes 7077892
  485.7 16.3 %copy-start.28 = (f32[768]{0:T(1024)S(1)}, f32[768]{0:T(1024)}, u32[]{:S(2)}) copy-start(f32[768]{0:T(1024)} %get-tuple-element.103) | copy-start | bytes 9220
  500.8 9.0 %collective-permute-start.7 = (bf16[1,192,768]{2,1,0:T(8,128)(2,1)S(1)}, bf16[1,192,768]{2,1,0:T(8,128)(2,1)S(1)}, u32[]{:S(2)}, u32[]{:S(2)}) collective-permute-start(bf16[1,192,768]{2,1,0:T(8,128)(2,1)S(1)} %dynamic-slice_convert_fusion.8), channel_id=1, source_target_pairs={{0,4},{2,6},{4,0},{6,2},{1,5},{3,7},{5,1},{7,3},{8,12},{10,14},{12... | collective-permute-start | bytes 884744 | tf_op jit(solution)/shard_map/ppermute | solution.py:549
  502.0 9.7 %copy-start.25 = (f32[768]{0:T(1024)S(1)}, f32[768]{0:T(1024)}, u32[]{:S(2)}) copy-start(f32[768]{0:T(1024)} %get-tuple-element.116) | copy-start | bytes 9220
  502.0 14.4 %copy-start.24 = (f32[768]{0:T(1024)S(1)}, f32[768]{0:T(1024)}, u32[]{:S(2)}) copy-start(f32[768]{0:T(1024)} %get-tuple-element.100) | copy-start | bytes 9220
  502.0 14.4 %copy-start.23 = (f32[768]{0:T(1024)S(1)}, f32[768]{0:T(1024)}, u32[]{:S(2)}) copy-start(f32[768]{0:T(1024)} %get-tuple-element.104) | copy-start | bytes 9220
  502.0 21.3 %copy-start.27 = (f32[3072]{0:T(1024)S(1)}, f32[3072]{0:T(1024)}, u32[]{:S(2)}) copy-start(f32[3072]{0:T(1024)} %get-tuple-element.114) | copy-start | bytes 36868
  510.5 5.2 collective-permute-start.8
  515.7 5.2 collective-permute-start.9
  521.0 51.8 %collective-permute-start.10 = (bf16[192,384]{1,0:T(8,128)(2,1)S(1)}, bf16[192,384]{1,0:T(8,128)(2,1)S(1)}, u32[]{:S(2)}, u32[]{:S(2)}) collective-permute-start(bf16[192,384]{1,0:T(8,128)(2,1)S(1)} %add_convert_fusion.6), channel_id=1, source_target_pairs={{0,24},{8,16},{16,8},{24,0},{1,25},{9,17},{17,9},{25,1},{2,26},{10... | collective-permute-start | bytes 442376 | tf_op jit(solution)/shard_map/ppermute | solution.py:549
  572.8 5.8 slice-start.5
  573.5 5.1 slice-start.6
  576.7 6.6 slice-start.7
  578.6 4.7 slice-start.8
  578.6 9.5 %slice-start.2 = ((s8[9437184]{0:T(1024)(128)(4,1)}), s8[4194304]{0:T(1024)(128)(4,1)S(1)}, s32[]{:S(2)}) async-start(s8[9437184]{0:T(1024)(128)(4,1)} %bitcast.139), calls=%async_computation.2 | async-start | bytes 8388608
  578.6 9.5 %slice-start.3 = ((s8[9437184]{0:T(1024)(128)(4,1)}), s8[4194304]{0:T(1024)(128)(4,1)S(1)}, s32[]{:S(2)}) async-start(s8[9437184]{0:T(1024)(128)(4,1)} %bitcast.139), calls=%async_computation.3 | async-start | bytes 8388608
  581.1 7.1 slice-start.4
  581.1 22.7 %collective-permute-start.2 = (bf16[1,192,2304]{2,1,0:T(8,128)(2,1)S(1)}, bf16[1,192,2304]{2,1,0:T(8,128)(2,1)S(1)}, u32[]{:S(2)}, u32[]{:S(2)}) collective-permute-start(bf16[1,192,2304]{2,1,0:T(8,128)(2,1)S(1)} %dynamic-slice_convert_fusion.3), channel_id=1, source_target_pairs={{0,4},{2,6},{4,0},{6,2},{1,5},{3,7},{5,1},{7,3},{8,12},{10,14},{12... | collective-permute-start | bytes 2654216 | tf_op jit(solution)/shard_map/ppermute | solution.py:549
  586.8 42.4 %collective-permute-start.17 = (bf16[1,768,768]{1,2,0:T(8,128)(2,1)}, bf16[1,768,768]{1,2,0:T(8,128)(2,1)}, u32[]{:S(2)}, u32[]{:S(2)}) collective-permute-start(bf16[1,768,768]{1,2,0:T(8,128)(2,1)} %dynamic-slice_convert_fusion.1), channel_id=1, source_target_pairs={{0,4},{2,6},{4,0},{6,2},{1,5},{3,7},{5,1},{7,3},{8,12},{10,14},{12... | collective-permute-start | bytes 3538952 | tf_op jit(solution)/shard_map/ppermute | solution.py:549
  594.1 58.5 %collective-permute-start.12 = (bf16[1,192,3072]{2,1,0:T(8,128)(2,1)}, bf16[1,192,3072]{2,1,0:T(8,128)(2,1)}, u32[]{:S(2)}, u32[]{:S(2)}) collective-permute-start(bf16[1,192,3072]{2,1,0:T(8,128)(2,1)} %dynamic-slice_convert_fusion.2), channel_id=1, source_target_pairs={{0,4},{2,6},{4,0},{6,2},{1,5},{3,7},{5,1},{7,3},{8,12},{10,14},{12... | collective-permute-start | bytes 3538952 | tf_op jit(solution)/shard_map/ppermute | solution.py:549
  605.2 47.4 %slice-start.9 = ((s8[4718592]{0:T(1024)(128)(4,1)}), s8[524288]{0:T(1024)(128)(4,1)S(1)}, s32[]{:S(2)}) async-start(s8[4718592]{0:T(1024)(128)(4,1)} %bitcast.148), calls=%async_computation.9 | async-start | bytes 1048576
  609.3 43.3 %slice-start.10 = ((s8[4718592]{0:T(1024)(128)(4,1)}), s8[4194304]{0:T(1024)(128)(4,1)S(1)}, s32[]{:S(2)}) async-start(s8[4718592]{0:T(1024)(128)(4,1)} %bitcast.148), calls=%async_computation.10 | async-start | bytes 8388608
  609.3 52.9 %collective-permute-start.3 = (bf16[192,1152]{1,0:T(8,128)(2,1)}, bf16[192,1152]{1,0:T(8,128)(2,1)}, u32[]{:S(2)}, u32[]{:S(2)}) collective-permute-start(bf16[192,1152]{1,0:T(8,128)(2,1)} %bitcast.125), channel_id=1, source_target_pairs={{0,1},{1,0},{2,3},{3,2},{4,5},{5,4},{6,7},{7,6},{8,9},{9,8},{10,11... | collective-permute-start | bytes 1327112 | tf_op jit(solution)/shard_map/ppermute | solution.py:549
  631.5 21.1 %copy-start.11 = (f32[1,768,768]{1,2,0:T(8,128)}, f32[1,768,768]{1,2,0:T(8,128)S(1)}, u32[]{:S(2)}) copy-start(f32[1,768,768]{1,2,0:T(8,128)S(1)} %convert_add_fusion) | copy-start | bytes 7077892
  632.4 32.0 %collective-permute-start.18 = (bf16[768,384]{0,1:T(8,128)(2,1)}, bf16[768,384]{0,1:T(8,128)(2,1)}, u32[]{:S(2)}, u32[]{:S(2)}) collective-permute-start(bf16[768,384]{0,1:T(8,128)(2,1)} %fusion.36), channel_id=1, source_target_pairs={{0,1},{1,0},{2,3},{3,2},{4,5},{5,4},{6,7},{7,6},{8,9},{9,8},{10,11... | collective-permute-start | bytes 1769480 | tf_op jit(solution)/shard_map/ppermute | solution.py:549
  659.2 5.3 copy-start.12
  660.4 13.5 %collective-permute-start.13 = (bf16[192,1536]{1,0:T(8,128)(2,1)S(1)}, bf16[192,1536]{1,0:T(8,128)(2,1)S(1)}, u32[]{:S(2)}, u32[]{:S(2)}) collective-permute-start(bf16[192,1536]{1,0:T(8,128)(2,1)S(1)} %bitcast.170), channel_id=1, source_target_pairs={{0,1},{1,0},{2,3},{3,2},{4,5},{5,4},{6,7},{7,6},{8,9},{9,8},{10,11... | collective-permute-start | bytes 1769480 | tf_op jit(solution)/shard_map/ppermute | solution.py:549
  663.3 13.1 %collective-permute-start.4 = (bf16[192,1152]{1,0:T(8,128)(2,1)S(1)}, bf16[192,1152]{1,0:T(8,128)(2,1)S(1)}, u32[]{:S(2)}, u32[]{:S(2)}) collective-permute-start(bf16[192,1152]{1,0:T(8,128)(2,1)S(1)} %fusion.34), channel_id=1, source_target_pairs={{0,8},{8,0},{16,24},{24,16},{1,9},{9,1},{17,25},{25,17},{2,10},{10... | collective-permute-start | bytes 1327112 | tf_op jit(solution)/shard_map/ppermute | solution.py:549
  665.7 23.3 %collective-permute-start.19 = (bf16[768,384]{0,1:T(8,128)(2,1)S(1)}, bf16[768,384]{0,1:T(8,128)(2,1)S(1)}, u32[]{:S(2)}, u32[]{:S(2)}) collective-permute-start(bf16[768,384]{0,1:T(8,128)(2,1)S(1)} %fusion.33), channel_id=1, source_target_pairs={{0,8},{8,0},{16,24},{24,16},{1,9},{9,1},{17,25},{25,17},{2,10},{10... | collective-permute-start | bytes 1769480 | tf_op jit(solution)/shard_map/ppermute | solution.py:549
  674.0 27.7 %collective-permute-start.14 = (bf16[192,1536]{1,0:T(8,128)(2,1)S(1)}, bf16[192,1536]{1,0:T(8,128)(2,1)S(1)}, u32[]{:S(2)}, u32[]{:S(2)}) collective-permute-start(bf16[192,1536]{1,0:T(8,128)(2,1)S(1)} %fusion.32), channel_id=1, source_target_pairs={{0,8},{8,0},{16,24},{24,16},{1,9},{9,1},{17,25},{25,17},{2,10},{10... | collective-permute-start | bytes 1769480 | tf_op jit(solution)/shard_map/ppermute | solution.py:549
  676.4 71.3 %copy-start.1 = (s32[2,1,8]{2,1,0:T(1,128)S(1)}, s32[2,1,8]{2,1,0:T(1,128)}, u32[]{:S(2)}) copy-start(s32[2,1,8]{2,1,0:T(1,128)} %param.18) | copy-start | bytes 196
  676.5 26.0 %collective-permute-start.5 = (bf16[192,1152]{1,0:T(8,128)(2,1)S(1)}, bf16[192,1152]{1,0:T(8,128)(2,1)S(1)}, u32[]{:S(2)}, u32[]{:S(2)}) collective-permute-start(bf16[192,1152]{1,0:T(8,128)(2,1)S(1)} %add_convert_fusion.5), channel_id=1, source_target_pairs={{0,24},{8,16},{16,8},{24,0},{1,25},{9,17},{17,9},{25,1},{2,26},{10... | collective-permute-start | bytes 1327112 | tf_op jit(solution)/shard_map/ppermute | solution.py:549
  689.2 47.4 %collective-permute-start.20 = (bf16[768,384]{0,1:T(8,128)(2,1)S(1)}, bf16[768,384]{0,1:T(8,128)(2,1)S(1)}, u32[]{:S(2)}, u32[]{:S(2)}) collective-permute-start(bf16[768,384]{0,1:T(8,128)(2,1)S(1)} %add_convert_fusion.3), channel_id=1, source_target_pairs={{0,24},{8,16},{16,8},{24,0},{1,25},{9,17},{17,9},{25,1},{2,26},{10... | collective-permute-start | bytes 1769480 | tf_op jit(solution)/shard_map/ppermute | solution.py:549
  701.8 44.7 %collective-permute-start.15 = (bf16[192,1536]{1,0:T(8,128)(2,1)S(1)}, bf16[192,1536]{1,0:T(8,128)(2,1)S(1)}, u32[]{:S(2)}, u32[]{:S(2)}) collective-permute-start(bf16[192,1536]{1,0:T(8,128)(2,1)S(1)} %add_convert_fusion.4), channel_id=1, source_target_pairs={{0,24},{8,16},{16,8},{24,0},{1,25},{9,17},{17,9},{25,1},{2,26},{10... | collective-permute-start | bytes 1769480 | tf_op jit(solution)/shard_map/ppermute | solution.py:549
  (7 other events, 12.3 us)

commit v3 on v2

--- a/solution.py
+++ b/solution.py
@@ -121,6 +121,234 @@
 
     def later(self):
         return [i for i, (stage, crossed) in enumerate(self.copies) if crossed]
+
+
+class Reduce:
+    def __init__(self, total, low, acc, arrived, chain, sends, arrivals, loads, order, across):
+        self.total, self.low, self.acc, self.arrived, self.chain = total, low, acc, arrived, chain
+        self.sends, self.arrivals, self.loads = sends, arrivals, loads
+        self.order, self.across = order, across
+        self.position = here(("row", "col"))
+        self.settled = set()
+
+    def slot(self, crossed, size):
+        position = place_of(self.position, crossed)
+        depth, columns = self.acc.shape[1:]
+        first = pl.multiple_of(position["row"] * size + self.low, 16)
+        start = pl.multiple_of(position["col"] * columns, LANES)
+        return self.total.at[pl.ds(first, depth), pl.ds(start, columns)]
+
+    def crossed(self, code):
+        return tuple(bit for i, bit in enumerate(self.order[1:]) if code >> i & 1)
+
+    def number(self, stage, code):
+        count = len(self.order)
+        return sum(1 << (count - 1 - s) for s in range(stage)) + code
+
+    def copy(self, stage, code, source):
+        axis, mask = self.order[stage]
+        number = self.number(stage, code)
+        return pltpu.make_async_remote_copy(
+            src_ref=source,
+            dst_ref=self.arrived.at[number],
+            send_sem=self.sends.at[number],
+            recv_sem=self.arrivals.at[number],
+            device_id=flipped(here((axis,)), axis, mask),
+            device_id_type=pl.DeviceIdType.MESH,
+        )
+
+    def load(self, code, size):
+        return pltpu.make_async_copy(
+            self.slot(self.crossed(code), size), self.acc.at[code], self.loads.at[code]
+        )
+
+    def outgoing(self, stage, code, size):
+        if stage == 0:
+            return self.copy(0, code, self.slot((self.order[0],) + self.crossed(code), size))
+        return self.copy(stage, code, self.acc.at[code << stage | 1 << (stage - 1)])
+
+    def begin(self, size):
+        self.size = size
+        for code in range(1 << (len(self.order) - 1))[::-1]:
+            self.outgoing(0, code, size).start()
+        for code in range(1 << (len(self.order) - 1))[::-1]:
+            self.load(code, size).start()
+
+    def settle(self, stage, code):
+        if (stage, code) in self.settled:
+            return
+        self.settled.add((stage, code))
+        entry = code << stage
+        if stage == 0:
+            self.load(code, self.size).wait()
+        else:
+            self.settle(stage - 1, 2 * code)
+        self.outgoing(stage, code, self.size).wait_recv()
+        number = self.number(stage, code)
+        value = self.acc[entry].astype(FULL) + self.arrived[number].astype(FULL)
+        self.acc[entry] = value.astype(LOW)
+
+    def codes(self, stage):
+        return range(1 << (len(self.order) - 1 - stage))[::-1]
+
+    def prepare(self, stage):
+        count = len(self.order)
+        if stage < count:
+            for code in self.codes(stage):
+                self.settle(stage - 1, 2 * code + 1)
+        elif stage == count:
+            self.settle(count - 1, 0)
+        else:
+            hop = stage - count - 1
+            self.hop(hop).wait_recv()
+            before = self.acc[0] if hop == 0 else self.chain[len(self.across) + hop - 1]
+            value = before.astype(FULL) + self.chain[hop].astype(FULL)
+            self.chain[len(self.across) + hop] = value.astype(LOW)
+
+    def hop(self, hop):
+        axis, mask = self.across[hop]
+        number = (1 << len(self.order)) - 1 + hop
+        target = self.target(axis, mask)
+        source = self.acc.at[0] if hop == 0 else self.chain.at[len(self.across) + hop - 1]
+        return pltpu.make_async_remote_copy(
+            src_ref=source,
+            dst_ref=self.chain.at[hop],
+            send_sem=self.sends.at[number],
+            recv_sem=self.arrivals.at[number],
+            device_id=target,
+            device_id_type=pl.DeviceIdType.MESH,
+        )
+
+    @staticmethod
+    def target(axis, mask):
+        return across_target(axis, mask)
+
+    def launch(self, stage):
+        if stage < len(self.order):
+            for code in self.codes(stage):
+                self.outgoing(stage, code, self.size).start()
+        else:
+            self.hop(stage - len(self.order)).start()
+
+    def stages(self):
+        return len(self.order) + len(self.across)
+
+    def finish(self, out):
+        hops = len(self.across)
+        self.hop(hops - 1).wait_recv()
+        before = self.acc[0] if hops == 1 else self.chain[2 * hops - 2]
+        out[...] = before.astype(FULL) + self.chain[hops - 1].astype(FULL)
+        for stage in range(len(self.order)):
+            for code in self.codes(stage):
+                self.outgoing(stage, code, self.size).wait_send()
+        for hop in range(hops):
+            self.hop(hop).wait_send()
+
+
+def across_target(axis, mask):
+    index = lax.axis_index(axis)
+    return {axis: index // (mask + 1) * (mask + 1) + mask - index % (mask + 1)}
+
+
+def across_bits(axis, size):
+    return [(axis, (2 << bit) - 1) for bit in range(size.bit_length() - 1)]
+
+
+def reduce_scratch(blocks, grid, hops):
+    count = grid[0] * grid[1]
+    shapes = []
+    for depth, columns in blocks:
+        shapes += [
+            pltpu.VMEM((count // 2, depth, columns), LOW),
+            pltpu.VMEM((count - 1, depth, columns), LOW),
+            pltpu.VMEM((2 * hops, depth, columns), LOW),
+            pltpu.SemaphoreType.DMA((count - 1 + hops,)),
+            pltpu.SemaphoreType.DMA((count - 1 + hops,)),
+            pltpu.SemaphoreType.DMA((count // 2,)),
+        ]
+    return shapes
+
+
+def greet_all(row_bits, col_bits, across):
+    barrier = pltpu.get_barrier_semaphore()
+    targets = [flipped(here((axis,)), axis, mask) for axis, mask in row_bits + col_bits]
+    targets += [across_target(axis, mask) for axis, mask in across]
+    for target in targets:
+        pl.semaphore_signal(barrier, inc=1, device_id=target, device_id_type=pl.DeviceIdType.MESH)
+    pl.semaphore_wait(barrier, len(targets))
+
+
+def end_kernel(total_ref, sums_ref, out_ref, all_ref, *scratch, grid, dp):
+    rows, columns = grid
+    row_bits, col_bits = bits_of("row", rows), bits_of("col", columns)
+    across = across_bits("dp", dp)
+    greet_all(row_bits, col_bits, across)
+    depth = out_ref.shape[0]
+    orders = [
+        (tuple(row_bits + col_bits[::-1]), tuple(across)),
+        (tuple(row_bits[:1] + col_bits[::-1] + row_bits[1:]), tuple(across[::-1])),
+    ]
+    parts = []
+    for number, (order, hops) in enumerate(orders):
+        buffers = scratch[6 * number : 6 * number + 6]
+        acc, arrived, chain, sends, arrivals, loads = buffers
+        part = Reduce(
+            total_ref, number * depth // 2, acc, arrived, chain, sends, arrivals, loads, order, hops
+        )
+        parts.append(part)
+    running, came, small_sends, small_arrivals = scratch[12:]
+    targets = [flipped(here((axis,)), axis, mask) for axis, mask in row_bits + col_bits]
+    targets += [across_target(axis, mask) for axis, mask in across]
+
+    def small(stage):
+        return pltpu.make_async_remote_copy(
+            src_ref=running.at[stage],
+            dst_ref=came.at[stage],
+            send_sem=small_sends.at[stage],
+            recv_sem=small_arrivals.at[stage],
+            device_id=targets[stage],
+            device_id_type=pl.DeviceIdType.MESH,
+        )
+
+    running[0] = sums_ref[...]
+    for part in parts:
+        part.begin(depth)
+    small(0).start()
+    stages = len(targets)
+    for stage in range(1, stages):
+        for part in parts:
+            part.prepare(stage)
+            part.launch(stage)
+        small(stage - 1).wait_recv()
+        running[stage] = running[stage - 1] + came[stage - 1]
+        small(stage).start()
+    for number, part in enumerate(parts):
+        part.finish(out_ref.at[pl.ds(number * depth // 2, depth // 2)])
+    small(stages - 1).wait_recv()
+    all_ref[...] = running[stages - 1] + came[stages - 1]
+    for stage in range(stages):
+        small(stage).wait_send()
+
+
+def end(total, sums, shape, grid, dp):
+    hops = dp.bit_length() - 1
+    stages = (grid[0] * grid[1] * dp).bit_length() - 1
+    inside = pl.BlockSpec(memory_space=pltpu.VMEM)
+    return pl.pallas_call(
+        functools.partial(end_kernel, grid=grid, dp=dp),
+        in_specs=[pl.BlockSpec(memory_space=pl.ANY), inside],
+        out_specs=[inside, inside],
+        out_shape=[jax.ShapeDtypeStruct(shape, FULL), jax.ShapeDtypeStruct(sums.shape, FULL)],
+        scratch_shapes=reduce_scratch([(shape[0] // 2, shape[1])] * 2, grid, hops)
+        + [
+            pltpu.VMEM((stages,) + sums.shape, FULL),
+            pltpu.VMEM((stages,) + sums.shape, FULL),
+            pltpu.SemaphoreType.DMA((stages,)),
+            pltpu.SemaphoreType.DMA((stages,)),
+        ],
+        compiler_params=pltpu.CompilerParams(collective_id=3, has_side_effects=True),
+        name="end",
+    )(total, sums)
 
 
 def attend_step(q_ref, k_ref, v_ref, ok_ref, ov_ref, mask_ref, out_ref, lse_ref, *, head, exact):
@@ -338,10 +566,10 @@
         ),
         name="attend",
     )(own, own, own, other, other, mask, *blocks)
-    out, lse = lax.cond(
-        jnp.max(flags) > 0.5,
-        lambda: tuple(attend_again(own, other, mask, head)),
-        lambda: (out, lse),
+    _, out, lse = lax.while_loop(
+        lambda state: state[0] > 0.5,
+        lambda state: (jnp.zeros((), FULL), *attend_again(own, other, mask, head)),
+        (jnp.max(flags), out, lse),
     )
     return out, lse, wholes
 
@@ -411,8 +639,14 @@
 
 def attend_back_kernel(
     q_ref, k_ref, v_ref, ok_ref, ov_ref, mask_ref, out_ref, grad_ref, lse_ref,
-    own_grad_ref, other_grad_ref, own_scratch, other_scratch, stored, *, head, scale,
+    *rest, head, scale, grid, dp,
 ):
+    if grid is not None:
+        totals_in, rest = rest[:3], rest[3:]
+    own_grad_ref, other_grad_ref, *rest = rest
+    if grid is not None:
+        blocks_out, rest = rest[:3], rest[3:]
+    own_scratch, other_scratch, stored, *scratch = rest
     rows = q_ref.shape[1]
     half = rows // 2
     heads = LANES // head
@@ -445,6 +679,44 @@
     def _():
         for copy in stores((step - 2) // steps, (step - 2) % steps, slot):
             copy.wait()
+
+    launches = {}
+    if grid is not None:
+        final = pl.num_programs(0) * steps - 1
+        row_bits, col_bits = bits_of("row", grid[0]), bits_of("col", grid[1])
+        across = across_bits("dp", dp)
+        by_row = tuple(row_bits + col_bits[::-1])
+        by_col = tuple(row_bits[:1] + col_bits[::-1] + row_bits[1:])
+        plans = [
+            (by_row, tuple(across), (0, 1, 4, 8, 10)),
+            (by_col, tuple(across[::-1]), (0, 1, 4, 8, 10)),
+            (by_row, tuple(across), (0, 1, 6, 8, 10)),
+        ]
+        parts = []
+        for number, (order, hops, _) in enumerate(plans):
+            buffers = scratch[6 * number : 6 * number + 6]
+            acc, arrived, chain, sends, arrivals, loads = buffers
+            part = Reduce(
+                totals_in[number], 0, acc, arrived, chain, sends, arrivals, loads, order, hops
+            )
+            part.size = blocks_out[number].shape[0]
+            parts.append(part)
+
+        @pl.when(step == 0)
+        def _():
+            greet_all(row_bits, col_bits, across)
+            for part in parts:
+                part.begin(part.size)
+
+        for number, part in enumerate(parts):
+            for stage in range(1, part.stages()):
+                launches.setdefault(plans[number][2][stage], []).append((part, stage))
+        for when in sorted(launches):
+
+            @pl.when(step == when)
+            def _(batch=launches[when]):
+                for part, stage in batch:
+                    part.prepare(stage)
 
     own_keys = k_ref[0] * jnp.asarray(scale, LOW)
     own_values = v_ref[0]
@@ -505,6 +777,19 @@
     other_scratch[slot, 1] = value_grad[half:]
     for copy in stores(group, tile, slot):
         copy.start()
+    for when in sorted(launches):
+
+        @pl.when(step == when)
+        def _(batch=launches[when]):
+            for part, stage in batch:
+                part.launch(stage)
+
+    if grid is not None:
+
+        @pl.when(step == final)
+        def _():
+            for part, block in zip(parts, blocks_out):
+                part.finish(block)
 
     @pl.when(step == pl.num_programs(0) * steps - 1)
     def _():
@@ -514,34 +799,47 @@
             copy.wait()
 
 
-def attend_back(own, other, mask, out, grad, lse, head):
+def attend_back(own, other, mask, out, grad, lse, head, sums=None, shapes=None, grid=None, dp=1):
     batch, rows, steps, spec, ins = attend_specs(own, other, mask)
     work = batch * rows * (rows + CLEN) * steps * LANES
     anywhere = pl.BlockSpec(memory_space=pl.ANY)
+    more_in, more_out, more_shapes, more_scratch, operands = [], [], [], [], []
+    params = None
+    if grid is not None:
+        more_in = [anywhere] * 3
+        more_out = [pl.BlockSpec(shape, lambda m, p: (0, 0)) for shape in shapes]
+        more_shapes = [jax.ShapeDtypeStruct(shape, FULL) for shape in shapes]
+        more_scratch = reduce_scratch(shapes, grid, dp.bit_length() - 1)
+        operands = list(sums)
+        params = pltpu.CompilerParams(collective_id=2, has_side_effects=True)
     return pl.pallas_call(
-        functools.partial(attend_back_kernel, head=head, scale=head**-0.5),
+        functools.partial(attend_back_kernel, head=head, scale=head**-0.5, grid=grid, dp=dp),
         grid=(batch, steps),
         in_specs=ins
         + [
             spec(rows, 0),
             spec(rows, 0),
             pl.BlockSpec((1, 1) + lse.shape[2:], lambda m, p: (m, p, 0, 0)),
-        ],
-        out_specs=[anywhere] * 2,
+        ]
+        + more_in,
+        out_specs=[anywhere] * 2 + more_out,
         out_shape=[
             jax.ShapeDtypeStruct(own.shape, LOW),
             jax.ShapeDtypeStruct(other.shape, LOW),
-        ],
+        ]
+        + more_shapes,
         scratch_shapes=[
             pltpu.VMEM((2, 3, rows, LANES), LOW),
             pltpu.VMEM((2, 2, rows // 2, LANES), LOW),
             pltpu.SemaphoreType.DMA((2, 5)),
-        ],
+        ]
+        + more_scratch,
+        compiler_params=params,
         cost_estimate=pl.CostEstimate(
             flops=40 * work, bytes_accessed=own.size * 10, transcendentals=work // head
         ),
         name="attend_back",
-    )(own, own, own, other, other, mask, out, grad, lse)
+    )(own, own, own, other, other, mask, out, grad, lse, *operands)
 
 
 def swapped(value, axis, mask):
@@ -688,11 +986,11 @@
     grad_first = normalize_back(grad_hidden * vectors[:, 3], first_normed, first_inverse)
     grad_first_low = grad_first.astype(LOW)
     grad_attended = nt(grad_first_low, out_matrix).astype(LOW)
-    down_grad = scattered(tn(act_low, grad_second_low), down_weight.shape)
-    up_grad = scattered(tn(hidden_low, grad_pre_low), up_weight.shape)
-    out_grad = scattered(tn(attended, grad_first_low), out_weight.shape)
-
-    own_grad, other_grad = attend_back(
+    shapes = (down_weight.shape, up_weight.shape, out_weight.shape)
+    totals = (
+        tn(act_low, grad_second_low), tn(hidden_low, grad_pre_low), tn(attended, grad_first_low),
+    )
+    operands = (
         own,
         other,
         mask,
@@ -701,6 +999,16 @@
         lse,
         head,
     )
+    if direct:
+        totals = [total.astype(LOW) for total in totals]
+        own_grad, other_grad, down_grad, up_grad, out_grad = attend_back(
+            *operands, totals, shapes, grid, lax.axis_size("dp")
+        )
+    else:
+        own_grad, other_grad = attend_back(*operands)
+        down_grad, up_grad, out_grad = (
+            scattered(total, shape) for total, shape in zip(totals, shapes)
+        )
     own_grad = own_grad.reshape(batch * rows, 3 * width)
     other_grad = other_grad.reshape(batch * half, 2 * width)
     sent = nt(other_grad, pair_matrix).astype(LOW).reshape(batch, half, width)
@@ -711,7 +1019,6 @@
     qkv_total = tn(tokens, own_grad)
     pair_total = tn(other_tokens, other_grad)
     qkv_total = cat([qkv_total[:, :width], qkv_total[:, width:] + pair_total], axis=1)
-    qkv_grad = scattered(qkv_total, qkv_weight.shape)
 
     own_sum = jnp.sum(own_grad.astype(FULL), axis=0)
     other_sum = jnp.sum(other_grad.astype(FULL), axis=0)
@@ -726,7 +1033,17 @@
         jnp.sum(grad_out, axis=0),
         jnp.sum(grad_pre, axis=0),
     ]
-    sums = lax.psum(cat(sums), ("dp", "row", "col"))
+    sums = cat(sums)
+    if direct:
+        lines = sums.reshape(-1, width)
+        lines = jnp.pad(lines, ((0, -lines.shape[0] % 8), (0, 0)))
+        qkv_grad, lines = end(
+            qkv_total.astype(LOW), lines, qkv_weight.shape, grid, lax.axis_size("dp")
+        )
+        sums = lines.reshape(-1)[: sums.shape[0]]
+    else:
+        qkv_grad = scattered(qkv_total, qkv_weight.shape)
+        sums = lax.psum(sums, ("dp", "row", "col"))
     index = lax.axis_index("row") * grid_cols + place
     devices = grid_rows * grid_cols
     split = sums[: 8 * width].reshape(8, width)

time: 756 us -> 592 us (0.78)
  waiting for transfers between devices: 129 us -> 0.01 us
  Pallas kernels: 233 us -> 345 us
  local copies, waits for them, and re-layouts: 70.2 us -> 15.9 us
  blocking collectives: 40 us -> 0 us
  other arithmetic: 58.1 us -> 35.3 us
  starting transfers between devices: 21.5 us -> 6.06 us
  loops' own time: 11.3 us -> 0.86 us
    ppermute x21 -> x1, waiting for transfers between devices: 129 us -> 0.01 us  [swapped(): return lax.ppermute(value, axis, pairs)]
    pallas_call x1, Pallas kernels: 78.5 us -> 192 us  [attend_back(): pl.pallas_call(functools.partial(attend_back_kernel, head=head, scale=hea...]
    psum x1 -> x0, blocking collectives: 40 us -> none  [local(): sums = lax.psum(cat(sums), ('dp', 'row', 'col'))]
    add x12 -> x0, other arithmetic: 18.1 us -> none  [the longest x8 15.1 us: parted(): return keep + swapped(send.astype(LOW), axis, mask).astype(FULL)]
    dynamic_slice x7 -> x0, local copies, waits for them, and re-layouts: 15.7 us -> none  [the longest x5 12.9 us: parted(): keep = lax.dynamic_index_in_dim(value, bit, dim, keepdims=False)]
    ppermute x21 -> x1, starting transfers between devices: 21.5 us -> 6.06 us  [swapped(): return lax.ppermute(value, axis, pairs)]
    unnamed x116 -> x86, local copies, waits for them, and re-layouts: 22.1 us -> 10.4 us
    dot_general x5, matrix products: 81.3 us -> 69.8 us  [nt(): lax.dot_general(left, right, (((1,), (1,)), ((), ())), preferred_element_...]
  transfers between devices with their start and end apart: 21 -> 1, of which waited for: 12 -> 0; matrix products, arithmetic and copies ran while one was open for 27% -> 7% of each run, Pallas kernels for 10% -> 9%
where the time goes in v3:
time: 592 us; the launch traced here: 584 us
  Pallas kernels  345 us (58%)
  matrix products  179 us (30%)
  other arithmetic  35.3 us (6%)
  local copies, waits for them, and re-layouts  15.9 us (3%)
  starting transfers between devices  6.06 us (1%)
    pallas_call x1, Pallas kernels, attend_back(): pl.pallas_call(functools.partial(attend_back_kernel, head=head, scale=hea...  192 us
    dot_general x5, matrix products, nt(): lax.dot_general(left, right, (((1,), (1,)), ((), ())), preferred_element_...  69.8 us
    pallas_call x1, Pallas kernels, attend(): pl.pallas_call(functools.partial(attend_kernel, head=head, grid=grid), gr...  56 us
    dot_general x5, matrix products, tn(): lax.dot_general(left, right, (((0,), (0,)), ((), ())), preferred_element_...  55.1 us
    dot_general x5, matrix products, nn(): lax.dot_general(left, right, (((1,), (0,)), ((), ())), preferred_element_...  53.8 us
    pallas_call x1, Pallas kernels, end(): pl.pallas_call(functools.partial(end_kernel, grid=grid, dp=dp), in_specs=...  49.9 us
    pallas_call x1, Pallas kernels, begin(): pl.pallas_call(functools.partial(begin_kernel, grid=grid), in_specs=[anyw...  47.1 us
  transfers between devices with their start and end apart: 1, of which 0 were waited for; matrix products, arithmetic and copies ran while one was open for 7% of the time, Pallas kernels for 9%

profile of v3, /device:TPU:8, one launch (start us, length us, event | category | flops | bytes accessed | tf_op | source)
XLA Modules:
  0.0 583.7 jit_solution(11970002107670820787)
XLA Ops:
  0.6 0.0 copy-start
  0.7 0.6 copy-done
  1.3 0.1 constant_dynamic-slice_fusion
  1.4 0.1 broadcast_bitcast_fusion
  1.5 1.7 slice_reduce_fusion.1
  3.2 3.9 convert_reduce_fusion.1
  7.1 0.6 copy.28
  7.8 0.9 fusion.37.mask_ref
  8.7 47.1 %begin.1 = (bf16[2,512,768]{2,1,0:T(8,128)(2,1)}, bf16[768,2304]{1,0:T(8,128)(2,1)}) custom-call(bf16[2,1024,768]{2,1,0:T(8,128)(2,1)} %tokens_ref.1, bf16[192,1152]{1,0:T(8,128)(2,1)} %block_ref.1), custom_call_target="tpu_custom_call" | custom-call | tf_op jit(solution)/shard_map/begin/pallas_call | solution.py:622
  55.7 0.0 copy-start.9
  55.8 4.9 add_convert_fusion.2
  60.7 9.9 %add_convert_fusion = bf16[2304,2048]{0,1:T(8,128)(2,1)} fusion(bf16[2048,768]{1,0:T(8,128)(2,1)S(1)} %bitcast.80, bf16[768,2304]{1,0:T(8,128)(2,1)S(1)} %copy-done.24, f32[2304]{0:T(1024)S(1)} %pad_maximum_fusion.2), kind=kOutput, calls=%fused_computation.14 | convolution fusion | flops 7257194496 | bytes 16131072 | tf_op jit(solution)/shard_map/dot_general | solution.py:26
  70.6 56.0 %attend.1 = (bf16[2,1024,768]{2,1,0:T(8,128)(2,1)}, f32[2,6,2,1024]{3,2,1,0:T(2,128)}, f32[2,6,8,512]{3,2,1,0:T(8,128)}, bf16[768,768]{1,0:T(8,128)(2,1)}, bf16[...) custom-call(bf16[2,1024,2304]{2,1,0:T(8,128)(2,1)} %bitcast.68, bf16[2,1024,2304]{2,1,0:T(8,128)(2,1)} %bitcast.69, ...), custom_call_target="tpu_custom_call" | custom-call | flops 28991029248 | bytes 18874368 | tf_op jit(solution)/shard_map/attend/pallas_call | solution.py:542
  126.6 1.6 reduce_max.9
  128.2 0.9 while.12
  129.0 0.0 copy-start.2
  129.1 7.3 %fusion.51 = (f32[2048]{0:T(1024)S(1)}, f32[2048,768]{1,0:T(8,128)S(1)}) fusion(f32[768]{0:T(1024)S(1)} %get-tuple-element.101, bf16[2048,768]{1,0:T(8,128)(2,1)} %bitcast.88, bf16[768,768]{1,0:T(8,128)(2,1)} %get-tuple-element.61, bf16[2048,768]{1,0:T(8,128)(2,1)} %bitcast.79), kind=kOutput, calls=%fused_computation.112 | convolution fusion | flops 2422208512 | bytes 13773824 | tf_op jit(solution)/shard_map/dot_general | solution.py:26
  136.4 0.0 copy-start.26
  136.4 0.8 multiply_reduce_fusion.3
  137.3 18.3 %multiply_convert_fusion = (bf16[2048,3072]{1,0:T(8,128)(2,1)}, f32[2048,3072]{1,0:T(8,128)}) fusion(f32[3072]{0:T(1024)S(1)} %copy-done.26, bf16[768,3072]{1,0:T(8,128)(2,1)S(1)} %bitcast.91, f32[2048,768]{1,0:T(8,128)S(1)} %get-tuple-element.127, f32[768]{0:T(1024)S(1)} %get-tuple-element.99, f32[768]{0:T(1024)S(1)} %get-tuple-element.100, ...), kind=kOutput, calls=%fused_computation.11 | convolution fusion | flops 9709289472 | bytes 48793600 | tf_op jit(solution)/shard_map/dot_general | solution.py:26
  155.5 13.5 %fusion.52 = (f32[2048]{0:T(1024)S(1)}, f32[2048,768]{1,0:T(8,128)S(1)}) fusion(f32[768]{0:T(1024)S(1)} %get-tuple-element.98, bf16[2048,3072]{1,0:T(8,128)(2,1)} %get-tuple-element.128, bf16[3072,768]{1,0:T(8,128)(2,1)S(1)} %bitcast.93, f32[768]{0:T(1024)S(1)} %get-tuple-element.99, f32[768]{0:T(1024)S(1)} %get-tuple-element.100, ...), kind=kOutput, calls=%fused_computation.113 | convolution fusion | flops 9674684416 | bytes 29918208 | tf_op jit(solution)/shard_map/dot_general | solution.py:26
  169.0 0.0 copy-start.4
  169.0 0.0 copy-start.17
  169.1 0.8 multiply_reduce_fusion.2
  169.9 0.0 copy-start.18
  169.9 0.0 copy-start.19
  169.9 1.0 copy-done.4
  170.9 2.9 fusion.17
  173.8 5.5 fusion.48
  179.4 18.4 %convolution_convert_fusion.1.rest_0_ = bf16[3072,768]{1,0:T(8,128)(2,1)} fusion(bf16[2048,3072]{1,0:T(8,128)(2,1)} %get-tuple-element.128, f32[2048,768]{1,0:T(8,128)} %get-tuple-element.122), kind=kOutput, calls=%fused_computation.45 | convolution fusion | flops 9667608576 | bytes 23592960 | tf_op jit(solution)/shard_map/dot_general | solution.py:30
  197.8 22.9 %fusion.9 = (f32[3072]{0:T(1024)}, bf16[2048,3072]{1,0:T(8,128)(2,1)}, f32[2048,3072]{1,0:T(8,128)}) fusion(f32[2048,3072]{1,0:T(8,128)} %get-tuple-element.129, f32[3072]{0:T(1024)S(1)} %copy-done.26, bf16[3072,768]{1,0:T(8,128)(2,1)S(1)} %bitcast.95, f32[2048,768]{1,0:T(8,128)S(1)} %copy-done.7), kind=kOutput, calls=%fused_computation.15 | convolution fusion | flops 9747035136 | bytes 73949184 | tf_op jit(solution)/shard_map/dot_general | solution.py:22
  220.6 24.2 %multiply_reduce_fusion = (f32[768]{0:T(1024)S(1)}, f32[2048]{0:T(1024)S(1)}, f32[2048]{0:T(1024)S(1)}, f32[768]{0:T(1024)S(1)}, f32[2048,768]{1,0:T(8,128)}) fusion(f32[2048,768]{1,0:T(8,128)S(1)} %get-tuple-element.127, f32[2048]{0:T(1024)S(1)} %add_rsqrt_fusion.1, f32[2048]{0:T(1024)S(1)} %broadcast_multiply_fusion.4, f32[768]{0:T(1024)S(1)} %get-tuple-element.100, ...), kind=kOutput, calls=%fused_computation.28 | convolution fusion | flops 9698273280 | bytes 61383680 | tf_op jit(solution)/shard_map/dot_general | solution.py:22
  244.9 20.2 %convolution_convert_fusion.rest_1_ = bf16[768,3072]{1,0:T(8,128)(2,1)} fusion(f32[2048,3072]{1,0:T(8,128)} %get-tuple-element.132, bf16[2048,3072]{1,0:T(8,128)(2,1)} %get-tuple-element.120, f32[2048,768]{1,0:T(8,128)S(1)} %get-tuple-element.127, f32[768]{0:T(1024)S(1)} %get-tuple-element.99, f32[768]{0:T(1024)S(1)} %get-tuple-element.100, ...), kind=kOutput, calls=%fused_computation.44 | convolution fusion | flops 9692774400 | bytes 48781312 | tf_op jit(solution)/shard_map/dot_general | solution.py:30
  265.1 4.7 fusion.50
  269.8 3.8 fusion.33.rest_2_
  273.6 4.0 convolution_convert_fusion.2
  277.7 192.1 %attend_back.1 = (bf16[2,1024,2304]{2,1,0:T(8,128)(2,1)}, bf16[2,512,1536]{2,1,0:T(8,128)(2,1)}, f32[768,384]{1,0:T(8,128)}, f32[192,1536]{1,0:T(8,128)}, f32[192,384]{1,0:T(8,128)}) custom-call(bf16[2,1024,2304]{2,1,0:T(8,128)(2,1)} %get-tuple-element.180, bf16[2,1024,2304]{2,1,0:T(8,128)(2,1)} %get-tuple-element.180, ...), custom_call_target="tpu_custom_call" | custom-call | flops 72477573120 | bytes 47185920 | tf_op jit(solution)/shard_map/attend_back/pallas_call | solution.py:815
  469.8 6.6 %fusion.24 = bf16[1024,768]{1,0:T(8,128)(2,1)} fusion(bf16[1024,1536]{1,0:T(8,128)(2,1)} %bitcast.81, bf16[768,2304]{1,0:T(8,128)(2,1)} %get-tuple-element.55), kind=kOutput, calls=%fused_computation.60 | convolution fusion | flops 2416705536 | bytes 7077888 | tf_op jit(solution)/shard_map/dot_general | solution.py:22
  476.4 6.1 %collective-permute-start = (bf16[2,512,768]{2,1,0:T(8,128)(2,1)}, bf16[2,512,768]{2,1,0:T(8,128)(2,1)}, u32[]{:S(2)}, u32[]{:S(2)}) collective-permute-start(bf16[2,512,768]{2,1,0:T(8,128)(2,1)} %bitcast.14), channel_id=1, source_target_pairs={{0,1},{1,0},{2,3},{3,2},{4,5},{5,4},{6,7},{7,6},{8,9},{9,8},{10,11... | collective-permute-start | bytes 4718600 | tf_op jit(solution)/shard_map/ppermute | solution.py:847
  482.4 0.5 convert_reduce_fusion.2
  482.9 5.2 convert_reduce_fusion
  488.2 0.6 copy-done.5
  488.8 0.9 copy-done.10
  489.7 8.4 %convolution_bitcast_fusion = f32[768,2304]{1,0:T(8,128)S(1)} fusion(bf16[2,1024,2304]{2,1,0:T(8,128)(2,1)S(1)} %copy-done.5, bf16[2,1024,768]{2,1,0:T(8,128)(2,1)S(1)} %copy-done.10), kind=kOutput, calls=%fused_computation.41 | convolution fusion | flops 7247757312 | bytes 19660800 | tf_op jit(solution)/shard_map/dot_general | solution.py:30
  498.1 0.0 copy-start.22
  498.1 0.0 copy-start.23
  498.2 4.4 fusion.19
  502.5 0.1 slice.122
  502.8 0.6 pad.5.sums_ref
  503.5 3.7 pad_maximum_fusion.total_ref
  507.1 49.9 %end.1 = (f32[192,1152]{1,0:T(8,128)}, f32[16,768]{1,0:T(8,128)}) custom-call(bf16[768,2304]{1,0:T(8,128)(2,1)} %pad_maximum_fusion.total_ref, f32[16,768]{1,0:T(8,128)} %pad.5.sums_ref), custom_call_target="tpu_custom_call" | custom-call | tf_op jit(solution)/shard_map/end/pallas_call | solution.py:337
  557.1 0.7 slice.85
  557.8 0.7 slice.84
  558.6 12.1 %convolution_add_fusion.1 = f32[2048,768]{1,0:T(8,128)S(1)} fusion(f32[2048,768]{1,0:T(8,128)} %copy-done.6, bf16[2048,2304]{1,0:T(8,128)(2,1)} %bitcast.75, bf16[768,2304]{1,0:T(8,128)(2,1)} %get-tuple-element.55), kind=kOutput, calls=%fused_computation.51 | convolution fusion | flops 7249330176 | bytes 25559040 | tf_op jit(solution)/shard_map/dot_general | solution.py:22
  570.7 2.7 copy-done.8
  573.3 0.2 slice.121
  573.5 0.7 dynamic_slice.16
  574.1 0.7 dynamic-slice_bitcast_fusion
  574.8 2.8 fusion.20
  577.7 1.9 pad_maximum_fusion.1
  579.5 0.9 copy.54
  580.5 0.7 copy.55
  581.2 1.0 copy.56
  582.2 1.0 copy.57
  (86 shorter events, 0.3 us)
Async XLA Ops:
  0.6 0.7 copy-start
  3.2 3.9 copy-start.16
  55.7 4.9 copy-start.9
  55.8 4.9 copy-start.24
  129.0 7.3 %copy-start.2 = (bf16[2,512,1536]{2,1,0:T(8,128)(2,1)}, bf16[2,512,1536]{2,1,0:T(8,128)(2,1)S(1)}, u32[]{:S(2)}) copy-start(bf16[2,512,1536]{2,1,0:T(8,128)(2,1)S(1)} %get-tuple-element.181) | copy-start | bytes 9437188
  129.1 8.2 %slice-start = ((s8[4718592]{0:T(1024)(128)(4,1)}), s8[4194304]{0:T(1024)(128)(4,1)S(1)}, s32[]{:S(2)}) async-start(s8[4718592]{0:T(1024)(128)(4,1)} %bitcast.90), calls=%async_computation | async-start | bytes 8388608
  129.1 8.2 %slice-start.1 = ((s8[4718592]{0:T(1024)(128)(4,1)}), s8[524288]{0:T(1024)(128)(4,1)S(1)}, s32[]{:S(2)}) async-start(s8[4718592]{0:T(1024)(128)(4,1)} %bitcast.90), calls=%async_computation.1 | async-start | bytes 1048576
  136.4 0.9 copy-start.26
  136.4 19.1 %slice-start.2 = ((s8[4718592]{0:T(1024)(128)(4,1)}), s8[4194304]{0:T(1024)(128)(4,1)S(1)}, s32[]{:S(2)}) async-start(s8[4718592]{0:T(1024)(128)(4,1)} %bitcast.92), calls=%async_computation.2 | async-start | bytes 8388608
  137.3 18.3 %slice-start.3 = ((s8[4718592]{0:T(1024)(128)(4,1)}), s8[524288]{0:T(1024)(128)(4,1)S(1)}, s32[]{:S(2)}) async-start(s8[4718592]{0:T(1024)(128)(4,1)} %bitcast.92), calls=%async_computation.3 | async-start | bytes 1048576
  169.0 1.9 copy-start.4
  169.0 1.9 copy-start.17
  169.9 4.0 copy-start.18
  169.9 4.0 copy-start.19
  173.8 23.9 %slice-start.4 = ((s8[4718592]{0:T(1024)(128)(4,1)}), s8[524288]{0:T(1024)(128)(4,1)S(1)}, s32[]{:S(2)}) async-start(s8[4718592]{0:T(1024)(128)(4,1)} %bitcast.94), calls=%async_computation.4 | async-start | bytes 1048576
  179.4 18.4 %copy-start.7 = (f32[2048,768]{1,0:T(8,128)S(1)}, f32[2048,768]{1,0:T(8,128)}, u32[]{:S(2)}) copy-start(f32[2048,768]{1,0:T(8,128)} %get-tuple-element.122) | copy-start | bytes 18874372
  179.4 18.4 %slice-start.5 = ((s8[4718592]{0:T(1024)(128)(4,1)}), s8[4194304]{0:T(1024)(128)(4,1)S(1)}, s32[]{:S(2)}) async-start(s8[4718592]{0:T(1024)(128)(4,1)} %bitcast.94), calls=%async_computation.5 | async-start | bytes 8388608
  265.1 4.7 copy-start.27
  269.8 3.8 copy-start.6
  269.8 3.8 copy-start.29
  273.6 4.1 copy-start.3
  273.6 4.1 copy-start.28
  469.8 12.7 %copy-start.11 = (bf16[2,512,1536]{2,1,0:T(8,128)(2,1)S(1)}, bf16[2,512,1536]{2,1,0:T(8,128)(2,1)}, u32[]{:S(2)}) copy-start(bf16[2,512,1536]{2,1,0:T(8,128)(2,1)} %get-tuple-element.66) | copy-start | bytes 9437188
  476.4 98.4 %collective-permute-start = (bf16[2,512,768]{2,1,0:T(8,128)(2,1)}, bf16[2,512,768]{2,1,0:T(8,128)(2,1)}, u32[]{:S(2)}, u32[]{:S(2)}) collective-permute-start(bf16[2,512,768]{2,1,0:T(8,128)(2,1)} %bitcast.14), channel_id=1, source_target_pairs={{0,1},{1,0},{2,3},{3,2},{4,5},{5,4},{6,7},{7,6},{8,9},{9,8},{10,11... | collective-permute-start | bytes 4718600 | tf_op jit(solution)/shard_map/ppermute | solution.py:847
  482.4 6.4 %copy-start.5 = (bf16[2,1024,2304]{2,1,0:T(8,128)(2,1)S(1)}, bf16[2,1024,2304]{2,1,0:T(8,128)(2,1)}, u32[]{:S(2)}) copy-start(bf16[2,1024,2304]{2,1,0:T(8,128)(2,1)} %get-tuple-element.65) | copy-start | bytes 28311556
  482.4 7.3 %copy-start.10 = (bf16[2,1024,768]{2,1,0:T(8,128)(2,1)S(1)}, bf16[2,1024,768]{2,1,0:T(8,128)(2,1)}, u32[]{:S(2)}) copy-start(bf16[2,1024,768]{2,1,0:T(8,128)(2,1)} %tokens_ref.1) | copy-start | bytes 9437188
  489.7 8.4 %copy-start.25 = (bf16[2,512,768]{2,1,0:T(8,128)(2,1)S(1)}, bf16[2,512,768]{2,1,0:T(8,128)(2,1)}, u32[]{:S(2)}) copy-start(bf16[2,512,768]{2,1,0:T(8,128)(2,1)} %get-tuple-element.56) | copy-start | bytes 4718596
  498.1 4.6 copy-start.22
  498.1 4.6 copy-start.21
  498.1 4.6 copy-start.20
  498.1 4.7 copy-start.23
  570.6 2.7 copy-start.8
  574.8 4.8 copy-start.14
  574.8 5.7 copy-start.15
  574.8 6.4 %copy-start.13 = (f32[192,1536]{1,0:T(8,128)S(1)}, f32[192,1536]{1,0:T(8,128)}, u32[]{:S(2)}) copy-start(f32[192,1536]{1,0:T(8,128)} %get-tuple-element.176) | copy-start | bytes 3538948
  574.8 8.4 %copy-start.1 = (s32[2,1,8]{2,1,0:T(1,128)S(1)}, s32[2,1,8]{2,1,0:T(1,128)}, u32[]{:S(2)}) copy-start(s32[2,1,8]{2,1,0:T(1,128)} %param.18) | copy-start | bytes 196
  577.7 4.5 copy-start.12

commit v4 on v3

--- a/solution.py
+++ b/solution.py
@@ -28,6 +28,10 @@
 
 def tn(left, right):
     return lax.dot_general(left, right, (((0,), (0,)), ((), ())), preferred_element_type=FULL)
+
+
+def folded(value):
+    return jnp.sum(value.reshape(-1, 8, value.shape[1]), axis=0)
 
 
 def only(pick, value):
@@ -108,8 +112,11 @@
             device_id_type=pl.DeviceIdType.MESH,
         )
 
-    def placing(self, semaphore):
-        return pltpu.make_async_copy(self.own, self.slot(self.position), semaphore)
+    def loading(self, held, semaphores):
+        return pltpu.make_async_copy(self.own, held, semaphores.at[0])
+
+    def placing(self, held, semaphores):
+        return pltpu.make_async_copy(held, self.slot(self.position), semaphores.at[1])
 
     def source(self, index):
         crossed = self.copies[index][1]
@@ -233,14 +240,22 @@
     def stages(self):
         return len(self.order) + len(self.across)
 
+    def close(self, out):
+        self.settle(len(self.order) - 1, 0)
+        out[...] = self.acc[0]
+        self.sent()
+
+    def sent(self):
+        for stage in range(len(self.order)):
+            for code in self.codes(stage):
+                self.outgoing(stage, code, self.size).wait_send()
+
     def finish(self, out):
         hops = len(self.across)
         self.hop(hops - 1).wait_recv()
         before = self.acc[0] if hops == 1 else self.chain[2 * hops - 2]
         out[...] = before.astype(FULL) + self.chain[hops - 1].astype(FULL)
-        for stage in range(len(self.order)):
-            for code in self.codes(stage):
-                self.outgoing(stage, code, self.size).wait_send()
+        self.sent()
         for hop in range(hops):
             self.hop(hop).wait_send()
 
@@ -252,6 +267,249 @@
 
 def across_bits(axis, size):
     return [(axis, (2 << bit) - 1) for bit in range(size.bit_length() - 1)]
+
+
+class Chain:
+    def __init__(self, start, buffers, sends, arrivals, across):
+        self.start, self.buffers, self.across = start, buffers, across
+        self.sends, self.arrivals = sends, arrivals
+
+    def before(self, hop):
+        return self.start if hop == 0 else self.buffers.at[len(self.across) + hop - 1]
+
+    def hop(self, hop):
+        axis, mask = self.across[hop]
+        return pltpu.make_async_remote_copy(
+            src_ref=self.before(hop),
+            dst_ref=self.buffers.at[hop],
+            send_sem=self.sends.at[hop],
+            recv_sem=self.arrivals.at[hop],
+            device_id=across_target(axis, mask),
+            device_id_type=pl.DeviceIdType.MESH,
+        )
+
+    def total(self, hop):
+        self.hop(hop).wait_recv()
+        return self.before(hop)[...].astype(FULL) + self.buffers[hop].astype(FULL)
+
+    def prepare(self, hop):
+        self.buffers[len(self.across) + hop - 1] = self.total(hop - 1).astype(LOW)
+
+    def launch(self, hop):
+        self.hop(hop).start()
+
+    def finish(self, out):
+        out[...] = self.total(len(self.across) - 1)
+        for hop in range(len(self.across)):
+            self.hop(hop).wait_send()
+
+
+def chain_scratch(blocks, hops):
+    shapes = []
+    for depth, columns in blocks:
+        shapes += [
+            pltpu.VMEM((2 * hops, depth, columns), LOW),
+            pltpu.SemaphoreType.DMA((hops,)),
+            pltpu.SemaphoreType.DMA((hops,)),
+        ]
+    return shapes
+
+
+def halve_scratch(shape, grid):
+    count = grid[0] * grid[1]
+    depth, columns = shape
+    return [
+        pltpu.VMEM((count // 2, depth // 2, columns), LOW),
+        pltpu.VMEM((count - 1, depth // 2, columns), LOW),
+        pltpu.SemaphoreType.DMA((count - 1,)),
+        pltpu.SemaphoreType.DMA((count - 1,)),
+        pltpu.SemaphoreType.DMA((count // 2,)),
+    ] * 2
+
+
+class Halving:
+    def __init__(self, total, out, scratch, grid, whens):
+        self.row_bits, self.col_bits = bits_of("row", grid[0]), bits_of("col", grid[1])
+        self.out, self.whens = out, whens
+        self.depth = out.shape[0]
+        first, later = tuple(self.row_bits[:1]), tuple(self.row_bits[1:])
+        orders = [first + later + tuple(self.col_bits[::-1]), first + tuple(self.col_bits[::-1]) + later]
+        self.parts = []
+        for number, order in enumerate(orders):
+            acc, arrived, sends, arrivals, loads = scratch[5 * number : 5 * number + 5]
+            low = number * self.depth // 2
+            self.parts.append(
+                Reduce(total, low, acc, arrived, None, sends, arrivals, loads, order, ())
+            )
+
+    def before(self, step):
+        @pl.when(step == 0)
+        def _():
+            greet(self.row_bits + self.col_bits)
+            for part in self.parts:
+                part.begin(self.depth)
+
+        for part in self.parts:
+            part.size = self.depth
+        for stage in range(1, self.parts[0].stages()):
+
+            @pl.when(step == self.whens[stage])
+            def _(stage=stage):
+                for part in self.parts:
+                    part.prepare(stage)
+                    part.launch(stage)
+
+    def after(self, step, final):
+        @pl.when(step == final)
+        def _():
+            half = self.depth // 2
+            for number, part in enumerate(self.parts):
+                part.close(self.out.at[pl.ds(number * half, half)])
+
+
+def widen_kernel(
+    second_ref, hidden_ref, down_ref, slope_ref, total_ref,
+    grad_ref, up_ref, sums_ref, block_ref, turned, *scratch, grid, whens, chunk,
+):
+    step = pl.program_id(0)
+    carried = Halving(total_ref, block_ref, scratch, grid, whens)
+    carried.before(step)
+
+    @pl.when(step == 0)
+    def _():
+        turned[...] = hidden_ref[...].T
+
+    rows = grad_ref.shape[0]
+
+    def part(index, total):
+        span = pl.ds(pl.multiple_of(index * chunk, chunk), chunk)
+        grad = nt(second_ref[span], down_ref[...]) * slope_ref[span].astype(FULL)
+        grad_ref[span] = grad.astype(LOW)
+        return total + jnp.sum(grad.reshape(chunk // 8, 8, grad.shape[1]), axis=0)
+
+    sums_ref[...] = lax.fori_loop(0, rows // chunk, part, jnp.zeros(sums_ref.shape, FULL))
+    up_ref[...] = nn(turned[...], grad_ref[...]).astype(LOW)
+    carried.after(step, pl.num_programs(0) - 1)
+
+
+def widen(second, hidden, down_matrix, slope, down_total, shape, grid):
+    rows, width = second.shape
+    hidden_units = down_matrix.shape[0]
+    tile = 512
+    steps = hidden_units // tile
+    once = pl.Buffered(buffer_count=1)
+    return pl.pallas_call(
+        functools.partial(widen_kernel, grid=grid, whens=(0, 1, 4), chunk=min(rows, 1024)),
+        grid=(steps,),
+        in_specs=[
+            pl.BlockSpec((rows, width), lambda i: (0, 0), pipeline_mode=once),
+            pl.BlockSpec((rows, width), lambda i: (0, 0), pipeline_mode=once),
+            pl.BlockSpec((tile, width), lambda i: (i, 0)),
+            pl.BlockSpec((rows, tile), lambda i: (0, i)),
+            pl.BlockSpec(memory_space=pl.ANY),
+        ],
+        out_specs=[
+            pl.BlockSpec((rows, tile), lambda i: (0, i)),
+            pl.BlockSpec((width, tile), lambda i: (0, i)),
+            pl.BlockSpec((8, tile), lambda i: (0, i)),
+            pl.BlockSpec(shape, lambda i: (0, 0)),
+        ],
+        out_shape=[
+            jax.ShapeDtypeStruct((rows, hidden_units), LOW),
+            jax.ShapeDtypeStruct((width, hidden_units), LOW),
+            jax.ShapeDtypeStruct((8, hidden_units), FULL),
+            jax.ShapeDtypeStruct(shape, LOW),
+        ],
+        scratch_shapes=[pltpu.VMEM((width, rows), LOW)] + halve_scratch(shape, grid),
+        compiler_params=pltpu.CompilerParams(
+            collective_id=4, has_side_effects=True, vmem_limit_bytes=56 * 2**20
+        ),
+        cost_estimate=pl.CostEstimate(
+            flops=4 * rows * width * hidden_units, bytes_accessed=6 * rows * hidden_units, transcendentals=0
+        ),
+        name="widen",
+    )(second, hidden, down_matrix, slope, down_total)
+
+
+def narrow_kernel(
+    grad_ref, second_ref, normed_ref, inverse_ref, attended_ref, up_ref, out_ref, gain_ref, total_ref,
+    first_ref, back_ref, out_total_ref, sums_ref, block_ref, held, *scratch, grid, whens,
+):
+    step = pl.program_id(0)
+    final = pl.num_programs(0) - 1
+    carried = Halving(total_ref, block_ref, scratch, grid, whens)
+    carried.before(step)
+
+    @pl.when(step == 0)
+    def _():
+        held[...] = jnp.zeros(held.shape, FULL)
+        sums_ref[...] = jnp.zeros(sums_ref.shape, FULL)
+
+    grad_hidden = nt(grad_ref[...], up_ref[...]) + second_ref[...].astype(FULL)
+    normed = normed_ref[...].astype(FULL)
+    grad_first = normalize_back(grad_hidden * gain_ref[...], normed, inverse_ref[...])
+    low = grad_first.astype(LOW)
+    first_ref[...] = low
+    back_ref[...] = nt(low, out_ref[...]).astype(LOW)
+    held[...] += tn(attended_ref[...], low)
+
+    sums_ref[0:8] += folded(grad_first)
+    sums_ref[8:16] += folded(grad_hidden * normed)
+    sums_ref[16:24] += folded(grad_hidden)
+    carried.after(step, final)
+
+    @pl.when(step == final)
+    def _():
+        out_total_ref[...] = held[...].astype(LOW)
+
+
+def narrow(grad, second, normed, inverse, attended, up_matrix, out_matrix, gain, up_total, shape, grid):
+    rows, width = second.shape
+    hidden_units = grad.shape[1]
+    tile = 256
+    once = pl.Buffered(buffer_count=1)
+
+    def block(columns):
+        return pl.BlockSpec((tile, columns), lambda i: (i, 0))
+
+    def whole(shape, **more):
+        return pl.BlockSpec(shape, lambda i: (0, 0), **more)
+
+    return pl.pallas_call(
+        functools.partial(narrow_kernel, grid=grid, whens=(0, 1, 5)),
+        grid=(rows // tile,),
+        in_specs=[
+            block(hidden_units),
+            block(width),
+            block(width),
+            block(1),
+            block(width),
+            whole(up_matrix.shape, pipeline_mode=once),
+            whole(out_matrix.shape, pipeline_mode=once),
+            whole(gain.shape),
+            pl.BlockSpec(memory_space=pl.ANY),
+        ],
+        out_specs=[
+            block(width), block(width), whole(out_matrix.shape), whole((24, width)), whole(shape),
+        ],
+        out_shape=[
+            jax.ShapeDtypeStruct((rows, width), LOW),
+            jax.ShapeDtypeStruct((rows, width), LOW),
+            jax.ShapeDtypeStruct(out_matrix.shape, LOW),
+            jax.ShapeDtypeStruct((24, width), FULL),
+            jax.ShapeDtypeStruct(shape, LOW),
+        ],
+        scratch_shapes=[pltpu.VMEM(out_matrix.shape, FULL)] + halve_scratch(shape, grid),
+        compiler_params=pltpu.CompilerParams(
+            collective_id=5, has_side_effects=True, vmem_limit_bytes=56 * 2**20
+        ),
+        cost_estimate=pl.CostEstimate(
+            flops=2 * rows * width * (hidden_units + 2 * width),
+            bytes_accessed=2 * rows * hidden_units,
+            transcendentals=0,
+        ),
+        name="narrow",
+    )(grad, second, normed, inverse, attended, up_matrix, out_matrix, gain, up_total)
 
 
 def reduce_scratch(blocks, grid, hops):
@@ -278,25 +536,29 @@
     pl.semaphore_wait(barrier, len(targets))
 
 
-def end_kernel(total_ref, sums_ref, out_ref, all_ref, *scratch, grid, dp):
+def end_kernel(
+    own_ref, matrix_ref, first_ref, total_ref, pair_ref, norm_ref, bias_ref, last_ref,
+    tokens_ref, out_ref, all_ref, *scratch, grid, dp,
+):
+    step = pl.program_id(0)
+    final = pl.num_programs(0) - 1
     rows, columns = grid
     row_bits, col_bits = bits_of("row", rows), bits_of("col", columns)
     across = across_bits("dp", dp)
-    greet_all(row_bits, col_bits, across)
+    first, later = tuple(row_bits[:1]), tuple(row_bits[1:])
+    orders = [first + later + tuple(col_bits[::-1]), first + tuple(col_bits[::-1]) + later]
     depth = out_ref.shape[0]
-    orders = [
-        (tuple(row_bits + col_bits[::-1]), tuple(across)),
-        (tuple(row_bits[:1] + col_bits[::-1] + row_bits[1:]), tuple(across[::-1])),
-    ]
+    part_depth = depth // 4
     parts = []
-    for number, (order, hops) in enumerate(orders):
-        buffers = scratch[6 * number : 6 * number + 6]
-        acc, arrived, chain, sends, arrivals, loads = buffers
+    for number in range(4):
+        acc, arrived, chain, sends, arrivals, loads = scratch[6 * number : 6 * number + 6]
         part = Reduce(
-            total_ref, number * depth // 2, acc, arrived, chain, sends, arrivals, loads, order, hops
-        )
+            total_ref, number * part_depth, acc, arrived, chain, sends, arrivals, loads,
+            orders[number % 2], tuple(across),
+        )
+        part.size = depth
         parts.append(part)
-    running, came, small_sends, small_arrivals = scratch[12:]
+    running, came, small_sends, small_arrivals = scratch[24:]
     targets = [flipped(here((axis,)), axis, mask) for axis, mask in row_bits + col_bits]
     targets += [across_target(axis, mask) for axis, mask in across]
 
@@ -310,45 +572,115 @@
             device_id_type=pl.DeviceIdType.MESH,
         )
 
-    running[0] = sums_ref[...]
-    for part in parts:
-        part.begin(depth)
-    small(0).start()
     stages = len(targets)
-    for stage in range(1, stages):
+    events = []
+    for number, part in enumerate(parts):
+        for stage in range(1, stages):
+            late = 0 if number < 2 else (1.1 if stage == 1 else 2.1)
+            events.append((stage + late, number, stage))
+    whens = {1: 2, 2: 5, 3: 5}
+    batches = {}
+    for key, number, stage in sorted(events):
+        batches.setdefault(min(whens.get(int(key), final), final), []).append((number, stage))
+
+    def advance(batch):
+        for number, stage in batch:
+            parts[number].prepare(stage)
+            parts[number].launch(stage)
+            if number == 1:
+                small(stage - 1).wait_recv()
+                running[stage] = running[stage - 1] + came[stage - 1]
+                small(stage).start()
+
+    @pl.when(step == 0)
+    def _():
+        greet_all(row_bits, col_bits, across)
         for part in parts:
-            part.prepare(stage)
-            part.launch(stage)
-        small(stage - 1).wait_recv()
-        running[stage] = running[stage - 1] + came[stage - 1]
-        small(stage).start()
-    for number, part in enumerate(parts):
-        part.finish(out_ref.at[pl.ds(number * depth // 2, depth // 2)])
-    small(stages - 1).wait_recv()
-    all_ref[...] = running[stages - 1] + came[stages - 1]
-    for stage in range(stages):
-        small(stage).wait_send()
-
-
-def end(total, sums, shape, grid, dp):
+            part.begin(depth)
+        running[0] = jnp.zeros(running.shape[1:], FULL)
+
+        def column_sums(value):
+            return jnp.sum(value, axis=0, keepdims=True)
+
+        width = running.shape[2]
+        tiles = pair_ref.shape[1]
+        for kind in range(2):
+            lines = slice(8 * kind, 8 * kind + 8)
+            for tile in range(tiles):
+                value = sum(pair_ref[m, tile, lines] for m in range(pair_ref.shape[0]))
+                running[0, kind : kind + 1, tile * LANES : (tile + 1) * LANES] = column_sums(value)
+        for number in range(3):
+            running[0, 2 + number : 3 + number] = column_sums(norm_ref[8 * number : 8 * number + 8])
+            running[0, 5 + number : 6 + number] = last_ref[number : number + 1]
+        for number in range(bias_ref.shape[1] // width):
+            value = bias_ref[:, number * width : (number + 1) * width]
+            running[0, 8 + number : 9 + number] = column_sums(value)
+        small(0).start()
+
+    for when in sorted(batches):
+        if when < final:
+            pl.when(step == when)(functools.partial(advance, batches[when]))
+
+    grad = nt(own_ref[...], matrix_ref[...]) + first_ref[...].astype(FULL)
+    tokens_ref[...] = grad.astype(LOW)
+
+    @pl.when(step == final)
+    def _():
+        advance(batches.get(final, []))
+        for number, part in enumerate(parts):
+            part.finish(out_ref.at[pl.ds(number * part_depth, part_depth)])
+        small(stages - 1).wait_recv()
+        all_ref[...] = running[stages - 1] + came[stages - 1]
+        for stage in range(stages):
+            small(stage).wait_send()
+
+
+def end(own, matrix, first, total, sums, shape, grid, dp):
+    lines = 8 + sums[2].shape[1] // first.shape[1]
+    lines = (lines + -lines % 8, first.shape[1])
     hops = dp.bit_length() - 1
     stages = (grid[0] * grid[1] * dp).bit_length() - 1
-    inside = pl.BlockSpec(memory_space=pltpu.VMEM)
+    rows, width = first.shape
+    tile = 256
+
+    def block(columns):
+        return pl.BlockSpec((tile, columns), lambda i: (i, 0))
+
+    def whole(shape, **more):
+        return pl.BlockSpec(shape, lambda i: (0, 0), **more)
+
     return pl.pallas_call(
         functools.partial(end_kernel, grid=grid, dp=dp),
-        in_specs=[pl.BlockSpec(memory_space=pl.ANY), inside],
-        out_specs=[inside, inside],
-        out_shape=[jax.ShapeDtypeStruct(shape, FULL), jax.ShapeDtypeStruct(sums.shape, FULL)],
-        scratch_shapes=reduce_scratch([(shape[0] // 2, shape[1])] * 2, grid, hops)
+        grid=(rows // tile,),
+        in_specs=[
+            block(own.shape[1]),
+            whole(matrix.shape, pipeline_mode=pl.Buffered(buffer_count=1)),
+            block(width),
+            pl.BlockSpec(memory_space=pl.ANY),
+            pl.BlockSpec(sums[0].shape, lambda i: (0, 0, 0, 0)),
+            *(whole(value.shape) for value in sums[1:]),
+        ],
+        out_specs=[block(width), whole(shape), whole(lines)],
+        out_shape=[
+            jax.ShapeDtypeStruct((rows, width), LOW),
+            jax.ShapeDtypeStruct(shape, FULL),
+            jax.ShapeDtypeStruct(lines, FULL),
+        ],
+        scratch_shapes=reduce_scratch([(shape[0] // 4, shape[1])] * 4, grid, hops)
         + [
-            pltpu.VMEM((stages,) + sums.shape, FULL),
-            pltpu.VMEM((stages,) + sums.shape, FULL),
+            pltpu.VMEM((stages,) + lines, FULL),
+            pltpu.VMEM((stages,) + lines, FULL),
             pltpu.SemaphoreType.DMA((stages,)),
             pltpu.SemaphoreType.DMA((stages,)),
         ],
-        compiler_params=pltpu.CompilerParams(collective_id=3, has_side_effects=True),
+        compiler_params=pltpu.CompilerParams(
+            collective_id=3, has_side_effects=True, vmem_limit_bytes=56 * 2**20
+        ),
+        cost_estimate=pl.CostEstimate(
+            flops=2 * rows * width * own.shape[1], bytes_accessed=8 * own.size, transcendentals=0
+        ),
         name="end",
-    )(total, sums)
+    )(own, matrix, first, total, *sums)
 
 
 def attend_step(q_ref, k_ref, v_ref, ok_ref, ov_ref, mask_ref, out_ref, lse_ref, *, head, exact):
@@ -422,7 +754,7 @@
 def attend_kernel(
     q_ref, k_ref, v_ref, ok_ref, ov_ref, mask_ref, out_block, up_block, down_block,
     out_ref, lse_ref, flag_ref, out_whole, up_whole, down_whole,
-    sends, arrivals, placed, *, head, grid,
+    sends, arrivals, placed, *held, head, grid,
 ):
     rows, columns = grid
     steps = pl.num_programs(1)
@@ -445,7 +777,13 @@
             for part in parts:
                 part.copy(index).start()
         for number, part in enumerate(parts):
-            part.placing(placed.at[number]).start()
+            part.loading(held[number], placed.at[number]).start()
+
+    @pl.when(step == 1)
+    def _():
+        for number, part in enumerate(parts):
+            part.loading(held[number], placed.at[number]).wait()
+            part.placing(held[number], placed.at[number]).start()
 
     last = len(first_order) - 1
     events = {}
@@ -455,7 +793,7 @@
             if len(crossed) > 1 and number:
                 when = final
             elif stage == last:
-                when = (5, 8, 9)[number] + 2 * (len(crossed) > 1)
+                when = (5, 10, 10)[number] + 2 * (len(crossed) > 1)
             else:
                 when = (2, 6, 7)[number]
             events.setdefault(min(when, final), []).append((part, index))
@@ -487,7 +825,7 @@
                 part.arrival(origin).wait_recv()
             part.copy(index).start()
         for number, part in enumerate(parts):
-            part.placing(placed.at[number]).wait()
+            part.placing(held[number], placed.at[number]).wait()
             for index in range(per):
                 if (part.base, index) not in waited:
                     part.arrival(index).wait_recv()
@@ -558,8 +896,9 @@
         scratch_shapes=[
             pltpu.SemaphoreType.DMA((copies,)),
             pltpu.SemaphoreType.DMA((copies,)),
-            pltpu.SemaphoreType.DMA((3,)),
-        ],
+            pltpu.SemaphoreType.DMA((3, 2)),
+        ]
+        + [pltpu.VMEM(blocks[i].shape, LOW) for i in (0, 2, 1)],
         compiler_params=pltpu.CompilerParams(collective_id=1, has_side_effects=True),
         cost_estimate=pl.CostEstimate(
             flops=16 * work, bytes_accessed=own.size * 4, transcendentals=work // head
@@ -574,31 +913,27 @@
     return out, lse, wholes
 
 
-def begin_kernel(tokens_ref, block_ref, other_ref, whole_ref, sends, arrivals, placed, *, grid):
+def begin_kernel(tokens_ref, block_ref, other_ref, whole_ref, sends, arrivals, placed, held, *, grid):
     rows, columns = grid
     row_bits, col_bits = bits_of("row", rows), bits_of("col", columns)
     order = tuple(col_bits + row_bits[::-1])
     part = Gather(block_ref, whole_ref, order, sends, arrivals, 0)
     per = len(part.copies)
-    half = other_ref.shape[1]
-    partner = flipped(here(("col",)), "col", 1)
-    exchanges = [
-        pltpu.make_async_remote_copy(
-            src_ref=tokens_ref.at[m, pl.ds(0, half)],
-            dst_ref=other_ref.at[m],
-            send_sem=sends.at[per + m],
-            recv_sem=arrivals.at[per + m],
-            device_id=partner,
-            device_id_type=pl.DeviceIdType.MESH,
-        )
-        for m in range(other_ref.shape[0])
-    ]
+    exchange = pltpu.make_async_remote_copy(
+        src_ref=tokens_ref.at[0, pl.ds(0, other_ref.shape[0])],
+        dst_ref=other_ref,
+        send_sem=sends.at[per],
+        recv_sem=arrivals.at[per],
+        device_id=flipped(here(("col",)), "col", 1),
+        device_id_type=pl.DeviceIdType.MESH,
+    )
     greet(row_bits + col_bits)
     for index in part.first():
         part.copy(index).start()
-    for exchange in exchanges:
-        exchange.start()
-    part.placing(placed.at[0]).start()
+    exchange.start()
+    part.loading(held, placed).start()
+    part.loading(held, placed).wait()
+    part.placing(held, placed).start()
     waited = set()
     for index in part.later():
         origin = part.source(index)
@@ -610,29 +945,32 @@
         if index not in waited:
             part.arrival(index).wait_recv()
         part.copy(index).wait_send()
-    part.placing(placed.at[0]).wait()
-    for exchange in exchanges:
-        exchange.wait()
+    part.placing(held, placed).wait()
+    exchange.wait()
 
 
 def begin(tokens, block, grid):
     batch, rows, width = tokens.shape
-    copies = grid[0] * grid[1] - 1 + batch
+    copies = grid[0] * grid[1]
     anywhere = pl.BlockSpec(memory_space=pl.ANY)
     return pl.pallas_call(
         functools.partial(begin_kernel, grid=grid),
         in_specs=[anywhere] * 2,
         out_specs=[anywhere] * 2,
         out_shape=[
-            jax.ShapeDtypeStruct((batch, rows // 2, width), LOW),
+            jax.ShapeDtypeStruct((rows // 2, width), LOW),
             jax.ShapeDtypeStruct((block.shape[0] * grid[0], block.shape[1] * grid[1]), LOW),
         ],
         scratch_shapes=[
             pltpu.SemaphoreType.DMA((copies,)),
             pltpu.SemaphoreType.DMA((copies,)),
-            pltpu.SemaphoreType.DMA((1,)),
+            pltpu.SemaphoreType.DMA((2,)),
+            pltpu.VMEM(block.shape, LOW),
         ],
         compiler_params=pltpu.CompilerParams(collective_id=0, has_side_effects=True),
+        cost_estimate=pl.CostEstimate(
+            flops=0, bytes_accessed=block.size * copies * 16, transcendentals=0
+        ),
         name="begin",
     )(tokens, block)
 
@@ -642,10 +980,10 @@
     *rest, head, scale, grid, dp,
 ):
     if grid is not None:
-        totals_in, rest = rest[:3], rest[3:]
-    own_grad_ref, other_grad_ref, *rest = rest
+        totals_in, matrices_in, rest = rest[:3], rest[3:5], rest[5:]
+    own_grad_ref, other_grad_ref, sums_ref, *rest = rest
     if grid is not None:
-        blocks_out, rest = rest[:3], rest[3:]
+        blocks_out, early_ref, rest = rest[:3], rest[3], rest[4:]
     own_scratch, other_scratch, stored, *scratch = rest
     rows = q_ref.shape[1]
     half = rows // 2
@@ -686,31 +1024,47 @@
         row_bits, col_bits = bits_of("row", grid[0]), bits_of("col", grid[1])
         across = across_bits("dp", dp)
         by_row = tuple(row_bits + col_bits[::-1])
-        by_col = tuple(row_bits[:1] + col_bits[::-1] + row_bits[1:])
-        plans = [
-            (by_row, tuple(across), (0, 1, 4, 8, 10)),
-            (by_col, tuple(across[::-1]), (0, 1, 4, 8, 10)),
-            (by_row, tuple(across), (0, 1, 6, 8, 10)),
-        ]
         parts = []
-        for number, (order, hops, _) in enumerate(plans):
-            buffers = scratch[6 * number : 6 * number + 6]
-            acc, arrived, chain, sends, arrivals, loads = buffers
-            part = Reduce(
-                totals_in[number], 0, acc, arrived, chain, sends, arrivals, loads, order, hops
-            )
-            part.size = blocks_out[number].shape[0]
-            parts.append(part)
+        for number, hops in enumerate((tuple(across), tuple(across))):
+            buffers, sends, arrivals = scratch[3 * number : 3 * number + 3]
+            parts.append(Chain(totals_in[number], buffers, sends, arrivals, hops))
+        acc, arrived, chain, sends, arrivals, loads = scratch[6:12]
+        last = Reduce(
+            totals_in[2], 0, acc, arrived, chain, sends, arrivals, loads, by_row, tuple(across)
+        )
+        last.size = blocks_out[2].shape[0]
+        parts.append(last)
 
         @pl.when(step == 0)
         def _():
             greet_all(row_bits, col_bits, across)
-            for part in parts:
-                part.begin(part.size)
-
-        for number, part in enumerate(parts):
-            for stage in range(1, part.stages()):
-                launches.setdefault(plans[number][2][stage], []).append((part, stage))
+            for part in parts[:2]:
+                part.launch(0)
+            last.begin(last.size)
+
+        kept, sent, sent_sem, early_sem = scratch[12:]
+        exchange = pltpu.make_async_remote_copy(
+            src_ref=sent,
+            dst_ref=early_ref,
+            send_sem=sent_sem,
+            recv_sem=early_sem,
+            device_id=flipped(here(("col",)), "col", 1),
+            device_id_type=pl.DeviceIdType.MESH,
+        )
+
+        @pl.when(step == steps)
+        def _():
+            width = kept.shape[1] // 2
+            value = nt(kept[:, :width], matrices_in[0][...]) + nt(kept[:, width:], matrices_in[1][...])
+            sent[...] = value.astype(LOW)
+            exchange.start()
+
+        for hop in range(1, len(across)):
+            launches.setdefault(min(2 * hop, final), []).append((parts[0], hop))
+            launches.setdefault(min(2 * hop + 2, final), []).append((parts[1], hop))
+        for stage in range(1, last.stages()):
+            when = min((0, 1, 3, 5, 9)[stage] if stage < 5 else final, final)
+            launches.setdefault(when, []).append((last, stage))
         for when in sorted(launches):
 
             @pl.when(step == when)
@@ -729,6 +1083,7 @@
     lane = lax.broadcasted_iota(jnp.int32, (1, LANES), 1) // head
     spans = [(start, start + CLEN) for start in range(0, half, CLEN)]
     totals = [None, None, None, None]
+    query_sums = []
 
     def add(place, value):
         totals[place] = value if totals[place] is None else totals[place] + value
@@ -766,7 +1121,9 @@
                 add(2, cat([nn(slopes[:, a:b], query_h[a:b]) for a, b in spans], axis=0))
                 add(3, cat([nn(probs[:, a:b], grad_h[a:b]) for a, b in spans], axis=0))
             query_grads.append(query_grad)
-        own_scratch[slot, 0, span] = cat(query_grads, axis=0).T.astype(LOW)
+        query_grad = cat(query_grads, axis=0).T
+        query_sums.append(folded(query_grad))
+        own_scratch[slot, 0, span] = query_grad.astype(LOW)
     key_grad = (totals[0] * scale).astype(LOW)
     value_grad = totals[1].astype(LOW)
     own_scratch[slot, 1, :half] = key_grad[:half]
@@ -775,6 +1132,12 @@
     own_scratch[slot, 2, half:] = totals[3].astype(LOW)
     other_scratch[slot, 0] = key_grad[half:]
     other_scratch[slot, 1] = value_grad[half:]
+    if grid is not None:
+        for part in range(2):
+            lanes = pl.ds(pl.multiple_of((part * steps + tile) * LANES, LANES), LANES)
+            kept[:, lanes] = other_scratch[slot, part]
+    sums_ref[0, 0, 0:8] = query_sums[0] + query_sums[1]
+    sums_ref[0, 0, 8:16] = folded(totals[1]) + folded(totals[3])
     for copy in stores(group, tile, slot):
         copy.start()
     for when in sorted(launches):
@@ -790,6 +1153,7 @@
         def _():
             for part, block in zip(parts, blocks_out):
                 part.finish(block)
+            exchange.wait()
 
     @pl.when(step == pl.num_programs(0) * steps - 1)
     def _():
@@ -799,19 +1163,37 @@
             copy.wait()
 
 
-def attend_back(own, other, mask, out, grad, lse, head, sums=None, shapes=None, grid=None, dp=1):
+def attend_back(
+    own, other, mask, out, grad, lse, head, sums=None, matrix=None, shapes=None, grid=None, dp=1
+):
     batch, rows, steps, spec, ins = attend_specs(own, other, mask)
     work = batch * rows * (rows + CLEN) * steps * LANES
     anywhere = pl.BlockSpec(memory_space=pl.ANY)
     more_in, more_out, more_shapes, more_scratch, operands = [], [], [], [], []
     params = None
     if grid is not None:
-        more_in = [anywhere] * 3
-        more_out = [pl.BlockSpec(shape, lambda m, p: (0, 0)) for shape in shapes]
+        width = steps * LANES
+        once = pl.Buffered(buffer_count=1)
+        more_in = [pl.BlockSpec(shape, lambda m, p: (0, 0)) for shape in shapes[:2]] + [anywhere]
+        more_in += [
+            pl.BlockSpec((width, width), lambda m, p: (0, 1), pipeline_mode=once),
+            pl.BlockSpec((width, width), lambda m, p: (0, 2), pipeline_mode=once),
+        ]
+        more_out = [pl.BlockSpec(shape, lambda m, p: (0, 0)) for shape in shapes] + [anywhere]
         more_shapes = [jax.ShapeDtypeStruct(shape, FULL) for shape in shapes]
-        more_scratch = reduce_scratch(shapes, grid, dp.bit_length() - 1)
-        operands = list(sums)
-        params = pltpu.CompilerParams(collective_id=2, has_side_effects=True)
+        more_shapes += [jax.ShapeDtypeStruct((rows // 2, width), LOW)]
+        hops = dp.bit_length() - 1
+        more_scratch = chain_scratch(shapes[:2], hops) + reduce_scratch(shapes[2:], grid, hops)
+        more_scratch += [
+            pltpu.VMEM((rows // 2, 2 * width), LOW),
+            pltpu.VMEM((rows // 2, width), LOW),
+            pltpu.SemaphoreType.DMA,
+            pltpu.SemaphoreType.DMA,
+        ]
+        operands = list(sums) + [matrix, matrix]
+        params = pltpu.CompilerParams(
+            collective_id=2, has_side_effects=True, vmem_limit_bytes=60 * 2**20
+        )
     return pl.pallas_call(
         functools.partial(attend_back_kernel, head=head, scale=head**-0.5, grid=grid, dp=dp),
         grid=(batch, steps),
@@ -822,10 +1204,13 @@
             pl.BlockSpec((1, 1) + lse.shape[2:], lambda m, p: (m, p, 0, 0)),
         ]
         + more_in,
-        out_specs=[anywhere] * 2 + more_out,
+        out_specs=[anywhere] * 2
+        + [pl.BlockSpec((1, 1, 16, LANES), lambda m, p: (m, p, 0, 0))]
+        + more_out,
         out_shape=[
             jax.ShapeDtypeStruct(own.shape, LOW),
             jax.ShapeDtypeStruct(other.shape, LOW),
+            jax.ShapeDtypeStruct((batch, steps, 16, LANES), FULL),
         ]
         + more_shapes,
         scratch_shapes=[
@@ -945,7 +1330,9 @@
     blocks = (out_weight, up_weight, down_weight)
     tokens = inputs.reshape(batch * rows, width)
     if direct:
-        other_tokens, qkv_matrix = begin(inputs, qkv_weight, grid)
+        early, qkv_matrix = begin(inputs, qkv_weight, grid)
+        late, qkv_matrix = lax.optimization_barrier((inputs[1:, :half], qkv_matrix))
+        other_tokens = cat([early[None], swapped(late, "col", 1)], axis=0)
     else:
         other_tokens = swapped(inputs[:, :half], "col", 1)
         qkv_matrix = gathered(qkv_weight)
@@ -980,16 +1367,31 @@
     grad_out = out_cotangent.reshape(batch * rows, width).astype(FULL)
     grad_second = normalize_back(grad_out * vectors[:, 6], second_normed, second_inverse)
     grad_second_low = grad_second.astype(LOW)
-    grad_pre = nt(grad_second_low, down_matrix) * slope_low.astype(FULL)
-    grad_pre_low = grad_pre.astype(LOW)
-    grad_hidden = grad_second + nt(grad_pre_low, up_matrix)
-    grad_first = normalize_back(grad_hidden * vectors[:, 3], first_normed, first_inverse)
-    grad_first_low = grad_first.astype(LOW)
-    grad_attended = nt(grad_first_low, out_matrix).astype(LOW)
     shapes = (down_weight.shape, up_weight.shape, out_weight.shape)
-    totals = (
-        tn(act_low, grad_second_low), tn(hidden_low, grad_pre_low), tn(attended, grad_first_low),
-    )
+    down_total = tn(act_low, grad_second_low)
+    if direct:
+        grad_pre_low, up_total, bias_sums, down_block = widen(
+            grad_second_low, hidden_low, down_matrix, slope_low, down_total.astype(LOW), shapes[0], grid
+        )
+        grad_first, grad_attended, out_total, norm_sums, up_block = narrow(
+            grad_pre_low, grad_second_low, first_normed.astype(LOW), first_inverse, attended,
+            up_matrix, out_matrix, vectors[:, 3][None], up_total, shapes[1], grid,
+        )
+        totals = [down_block, up_block, out_total]
+    else:
+        grad_pre = nt(grad_second_low, down_matrix) * slope_low.astype(FULL)
+        grad_pre_low = grad_pre.astype(LOW)
+        grad_hidden = grad_second + nt(grad_pre_low, up_matrix)
+        grad_first = normalize_back(grad_hidden * vectors[:, 3], first_normed, first_inverse)
+        grad_first_low = grad_first.astype(LOW)
+        grad_attended = nt(grad_first_low, out_matrix).astype(LOW)
+        totals = (down_total, tn(hidden_low, grad_pre_low), tn(attended, grad_first_low))
+        first_sums = [
+            jnp.sum(grad_first, axis=0),
+            jnp.sum(grad_hidden * first_normed, axis=0),
+            jnp.sum(grad_hidden, axis=0),
+        ]
+        bias_sum = jnp.sum(grad_pre, axis=0)
     operands = (
         own,
         other,
@@ -1000,50 +1402,49 @@
         head,
     )
     if direct:
-        totals = [total.astype(LOW) for total in totals]
-        own_grad, other_grad, down_grad, up_grad, out_grad = attend_back(
-            *operands, totals, shapes, grid, lax.axis_size("dp")
-        )
+        own_grad, other_grad, pair_sums, down_grad, up_grad, out_grad, received = attend_back(
+            *operands, totals, qkv_matrix, shapes, grid, lax.axis_size("dp")
+        )
+        sent = nt(other_grad[1:].reshape(-1, 2 * width), pair_matrix).astype(LOW)
+        sent, own_grad = lax.optimization_barrier((sent, own_grad))
+        late = swapped(sent.reshape(batch - 1, half, width), "col", 1)
+        received = cat([received[None], late], axis=0)
+        own_grad = own_grad.reshape(batch * rows, 3 * width)
+        other_grad = other_grad.reshape(batch * half, 2 * width)
     else:
-        own_grad, other_grad = attend_back(*operands)
+        own_grad, other_grad, pair_sums = attend_back(*operands)
         down_grad, up_grad, out_grad = (
             scattered(total, shape) for total, shape in zip(totals, shapes)
         )
-    own_grad = own_grad.reshape(batch * rows, 3 * width)
-    other_grad = other_grad.reshape(batch * half, 2 * width)
-    sent = nt(other_grad, pair_matrix).astype(LOW).reshape(batch, half, width)
-    received = swapped(sent, "col", 1).astype(FULL)
-    grad_tokens = (grad_first + nt(own_grad, qkv_matrix)).reshape(batch, rows, width)
-    grad_tokens = cat([grad_tokens[:, :half] + received, grad_tokens[:, half:]], axis=1)
-    grad_tokens = grad_tokens.astype(LOW)
+        own_grad = own_grad.reshape(batch * rows, 3 * width)
+        other_grad = other_grad.reshape(batch * half, 2 * width)
+        sent = nt(other_grad, pair_matrix).astype(LOW).reshape(batch, half, width)
+        received = swapped(sent, "col", 1).astype(FULL)
+        grad_tokens = (grad_first + nt(own_grad, qkv_matrix)).reshape(batch, rows, width)
+        grad_tokens = cat([grad_tokens[:, :half] + received, grad_tokens[:, half:]], axis=1)
+        grad_tokens = grad_tokens.astype(LOW)
     qkv_total = tn(tokens, own_grad)
     pair_total = tn(other_tokens, other_grad)
     qkv_total = cat([qkv_total[:, :width], qkv_total[:, width:] + pair_total], axis=1)
-
-    own_sum = jnp.sum(own_grad.astype(FULL), axis=0)
-    other_sum = jnp.sum(other_grad.astype(FULL), axis=0)
-    sums = [
-        own_sum[:width],
-        own_sum[2 * width :] + other_sum[width:],
-        jnp.sum(grad_first, axis=0),
-        jnp.sum(grad_hidden * first_normed, axis=0),
-        jnp.sum(grad_hidden, axis=0),
+    last_sums = [
         jnp.sum(grad_second, axis=0),
         jnp.sum(grad_out * second_normed, axis=0),
         jnp.sum(grad_out, axis=0),
-        jnp.sum(grad_pre, axis=0),
     ]
-    sums = cat(sums)
     if direct:
-        lines = sums.reshape(-1, width)
-        lines = jnp.pad(lines, ((0, -lines.shape[0] % 8), (0, 0)))
-        qkv_grad, lines = end(
-            qkv_total.astype(LOW), lines, qkv_weight.shape, grid, lax.axis_size("dp")
-        )
-        sums = lines.reshape(-1)[: sums.shape[0]]
+        grad_tokens, qkv_grad, sums = end(
+            own_grad, qkv_matrix, grad_first, qkv_total.astype(LOW),
+            (pair_sums, norm_sums, bias_sums, jnp.stack(last_sums)),
+            qkv_weight.shape, grid, lax.axis_size("dp"),
+        )
+        received = jnp.pad(received, ((0, 0), (0, rows - half), (0, 0))).astype(FULL)
+        grad_tokens = (grad_tokens.reshape(batch, rows, width).astype(FULL) + received).astype(LOW)
+        sums = sums.reshape(-1)[: 8 * width + up_bias.shape[0]]
     else:
         qkv_grad = scattered(qkv_total, qkv_weight.shape)
-        sums = lax.psum(sums, ("dp", "row", "col"))
+        pair_sums = jnp.sum(pair_sums, axis=0)
+        pair_sums = [jnp.sum(pair_sums[:, i : i + 8], axis=1).reshape(width) for i in (0, 8)]
+        sums = lax.psum(cat([*pair_sums, *first_sums, *last_sums, bias_sum]), ("dp", "row", "col"))
     index = lax.axis_index("row") * grid_cols + place
     devices = grid_rows * grid_cols
     split = sums[: 8 * width].reshape(8, width)

time: 592 us -> 486 us (0.82)
  matrix products: 179 us -> 89.9 us
  other arithmetic: 35.3 us -> 23.3 us
    pallas_call x1 -> x4, Pallas kernels: 49.9 us -> 165 us  [the longest x1 51.8 us: attend_again(): pl.pallas_call(functools.partial(attend_again_kernel, head=head), grid=(b...]
    pallas_call x1, Pallas kernels: 192 us -> 92 us  [attend_back(): pl.pallas_call(functools.partial(attend_back_kernel, head=head, scale=hea...]
    dot_general x5 -> x1, matrix products: 69.8 us -> 4.59 us  [nt(): lax.dot_general(left, right, (((1,), (1,)), ((), ())), preferred_element_...]
    dot_general x5 -> x3, matrix products: 55.1 us -> 27.5 us  [tn(): lax.dot_general(left, right, (((0,), (0,)), ((), ())), preferred_element_...]
    pallas_call x1, Pallas kernels: 47.1 us -> 30.2 us  [begin(): pl.pallas_call(functools.partial(begin_kernel, grid=grid), in_specs=[anyw...]
    reduce_sum x3 -> x0, other arithmetic: 10.4 us -> none  [the longest x1 5.24 us: local(): own_sum = jnp.sum(own_grad.astype(FULL), axis=0)]
    convert_element_type x0 -> x2, other arithmetic: none -> 6.39 us  [the longest x1 3.57 us: local(): (grad_tokens.reshape(batch, rows, width).astype(FULL) + received).astype(...]
  transfers between devices with their start and end apart: 1 -> 2, of which waited for: 0 -> 0; matrix products, arithmetic and copies ran while one was open for 7% -> 6% of each run, Pallas kernels for 9% -> 10%
where the time goes in v4:
time: 486 us; the launch traced here: 479 us
  Pallas kernels  344 us (71%)
  matrix products  89.9 us (18%)
  other arithmetic  23.3 us (5%)
  local copies, waits for them, and re-layouts  16.6 us (3%)
    pallas_call x1, Pallas kernels, attend_back(): pl.pallas_call(functools.partial(attend_back_kernel, head=head, scale=hea...  92 us
    dot_general x5, matrix products, nn(): lax.dot_general(left, right, (((1,), (0,)), ((), ())), preferred_element_...  57.8 us
    pallas_call x1, Pallas kernels, attend(): pl.pallas_call(functools.partial(attend_kernel, head=head, grid=grid), gr...  56.4 us
    pallas_call x1, Pallas kernels, attend_again(): pl.pallas_call(functools.partial(attend_again_kernel, head=head), grid=(b...  51.8 us
    pallas_call x1, Pallas kernels, end(): pl.pallas_call(functools.partial(end_kernel, grid=grid, dp=dp), grid=(row...  45.8 us
    pallas_call x1, Pallas kernels, narrow(): pl.pallas_call(functools.partial(narrow_kernel, grid=grid, whens=(0, 1, 5...  34 us
    pallas_call x1, Pallas kernels, widen(): pl.pallas_call(functools.partial(widen_kernel, grid=grid, whens=(0, 1, 4)...  33.8 us
    pallas_call x1, Pallas kernels, begin(): pl.pallas_call(functools.partial(begin_kernel, grid=grid), in_specs=[anyw...  30.2 us
  transfers between devices with their start and end apart: 2, of which 0 were waited for; matrix products, arithmetic and copies ran while one was open for 6% of the time, Pallas kernels for 10%

profile of v4, /device:TPU:8, one launch (start us, length us, event | category | flops | bytes accessed | tf_op | source)
XLA Modules:
  0.0 478.9 jit_solution(12664591551472423507)
XLA Ops:
  0.6 0.0 copy-start
  0.6 0.0 copy-start.2
  0.7 2.2 slice.58
  2.9 30.2 %begin.1 = (bf16[512,768]{1,0:T(8,128)(2,1)}, bf16[768,2304]{1,0:T(8,128)(2,1)}) custom-call(bf16[2,1024,768]{2,1,0:T(8,128)(2,1)} %tokens_ref.1, bf16[192,1152]{1,0:T(8,128)(2,1)} %block_ref.1), custom_call_target="tpu_custom_call" | custom-call | bytes 28311552 | tf_op jit(solution)/shard_map/begin/pallas_call | solution.py:956
  33.1 0.6 collective-permute-start
  33.7 0.1 constant_dynamic-slice_fusion
  33.8 0.1 broadcast_bitcast_fusion
  33.9 2.2 slice_reduce_fusion.1
  36.1 1.4 convert_reduce_fusion
  37.6 12.4 %add_convert_fusion = bf16[2304,2048]{0,1:T(8,128)(2,1)} fusion(bf16[2048,768]{1,0:T(8,128)(2,1)} %bitcast.79, bf16[768,2304]{1,0:T(8,128)(2,1)} %get-tuple-element.72.rest_3_.rest_4_.matrix_ref, f32[2304]{0:T(1024)S(1)} %pad_maximum_fusion.2), kind=kOutput, calls=%fused_computation.12 | convolution fusion | flops 7257194496 | bytes 16131072 | tf_op jit(solution)/shard_map/dot_general | solution.py:26
  49.9 0.6 copy.32
  50.5 0.6 stack.14
  51.2 0.9 fusion.33.mask_ref
  52.1 0.0 collective-permute-done
  52.1 1.3 pad_maximum_fusion.1
  53.4 4.5 add_convert_fusion.2
  57.9 56.4 %attend.1 = (bf16[2,1024,768]{2,1,0:T(8,128)(2,1)}, f32[2,6,2,1024]{3,2,1,0:T(2,128)}, f32[2,6,8,512]{3,2,1,0:T(8,128)}, bf16[768,768]{1,0:T(8,128)(2,1)}, bf16[...) custom-call(bf16[2,1024,2304]{2,1,0:T(8,128)(2,1)} %bitcast.72, bf16[2,1024,2304]{2,1,0:T(8,128)(2,1)} %bitcast.73, ...), custom_call_target="tpu_custom_call" | custom-call | flops 28991029248 | bytes 18874368 | tf_op jit(solution)/shard_map/attend/pallas_call | solution.py:880
  114.2 1.6 reduce_max.9
  115.8 54.7 %while.12 = (f32[]{:T(128)}, bf16[2,1024,768]{2,1,0:T(8,128)(2,1)}, f32[2,6,2,1024]{3,2,1,0:T(2,128)}, bf16[2,1024,2304]{2,1,0:T(8,128)(2,1)}, bf16[2,512,1536]{...) while((f32[]{:T(128)}, bf16[2,1024,768]{2,1,0:T(8,128)(2,1)}, ...), condition=%region_2.3_spmd.clone, body=%region_1.2_spmd.clone | while | flops 393217 | bytes 593993 | solution.py:908
  116.7 0.9 fusion.3.refs_5_
  117.6 51.8 %attend_again.1 = (bf16[2,1024,768]{2,1,0:T(8,128)(2,1)}, f32[2,6,2,1024]{3,2,1,0:T(2,128)}) custom-call(bf16[2,1024,2304]{2,1,0:T(8,128)(2,1)} %get-tuple-element.186.refs_0_.refs_1_.refs_2_, bf16[2,1024,2304]{2,1,0:T(8,128)(2,1)} %get-tuple-element.186.refs_0_.refs_1_.refs_2_, bf16[2,1024,2304]{2,1,0:T(8,128)(2,1)} %get-tuple-element.186.refs_0_.refs_1_.refs_2_, ...), custom_call_target="tpu_custom_call" | custom-call | tf_op jit(solution)/shard_map/while/body/attend_again/pallas_call | solution.py:856
  170.5 6.1 %fusion.39 = (f32[2048]{0:T(1024)S(1)}, f32[2048,768]{1,0:T(8,128)S(1)}) fusion(f32[768]{0:T(1024)S(1)} %get-tuple-element.129, bf16[2048,768]{1,0:T(8,128)(2,1)} %bitcast.94, bf16[768,768]{1,0:T(8,128)(2,1)} %get-tuple-element.79.out_ref, bf16[2048,768]{1,0:T(8,128)(2,1)} %bitcast.80), kind=kOutput, calls=%fused_computation.85 | convolution fusion | flops 2422208512 | bytes 13773824 | tf_op jit(solution)/shard_map/dot_general | solution.py:26
  176.7 0.8 multiply_reduce_fusion.1
  177.5 0.0 copy-start.21
  177.5 0.0 slice-start.1
  177.5 2.8 multiply_convert_fusion.1
  180.4 19.9 %fusion.8 = (bf16[2048,3072]{1,0:T(8,128)(2,1)}, bf16[2048,3072]{1,0:T(8,128)(2,1)}) fusion(f32[3072]{0:T(1024)S(1)} %copy-done.21, bf16[2048,768]{1,0:T(8,128)(2,1)S(1)} %get-tuple-element.153.hidden_ref, bf16[768,3072]{1,0:T(8,128)(2,1)S(1)} %bitcast.97), kind=kOutput, calls=%fused_computation.9 | convolution fusion | flops 9739173888 | bytes 33042432 | tf_op jit(solution)/shard_map/dot_general | solution.py:26
  200.3 14.9 %fusion.40 = (f32[2048]{0:T(1024)S(1)}, f32[2048,768]{1,0:T(8,128)S(1)}) fusion(f32[768]{0:T(1024)S(1)} %get-tuple-element.126, bf16[2048,3072]{1,0:T(8,128)(2,1)} %get-tuple-element.150, bf16[3072,768]{1,0:T(8,128)(2,1)} %get-tuple-element.81.down_ref, f32[768]{0:T(1024)S(1)} %get-tuple-element.127, f32[768]{0:T(1024)S(1)} %get-tuple-element.128, ...), kind=kOutput, calls=%fused_computation.86 | convolution fusion | flops 9674684416 | bytes 29918208 | tf_op jit(solution)/shard_map/dot_general | solution.py:26
  215.2 0.0 copy-start.3
  215.2 0.0 copy-start.15
  215.2 0.9 multiply_reduce_fusion
  216.1 0.0 copy-start.16
  216.1 0.0 copy-start.17
  216.1 1.0 copy-done.3
  217.1 2.5 fusion.18
  219.6 4.0 fusion.37
  223.6 0.6 stack.12
  224.2 1.0 stack.13
  225.2 12.4 %convolution_convert_fusion.total_ref = bf16[3072,768]{1,0:T(8,128)(2,1)} fusion(bf16[2048,3072]{1,0:T(8,128)(2,1)S(1)} %bitcast.99, bf16[2048,768]{1,0:T(8,128)(2,1)S(1)} %get-tuple-element.148.second_ref), kind=kOutput, calls=%fused_computation.39 | convolution fusion | flops 9666035712 | bytes 20447232 | tf_op jit(solution)/shard_map/dot_general | solution.py:30
  237.6 1.3 copy.20.inverse_ref
  239.0 33.8 %widen.1 = (bf16[2048,3072]{1,0:T(8,128)(2,1)}, bf16[768,3072]{1,0:T(8,128)(2,1)}, f32[8,3072]{1,0:T(8,128)}, bf16[768,384]{1,0:T(8,128)(2,1)}) custom-call(bf16[2048,768]{1,0:T(8,128)(2,1)} %copy-done.6, bf16[2048,768]{1,0:T(8,128)(2,1)} %copy-done.5, bf16[3072,768]{1,0:T(8,128)(2,1)} %get-tuple-element.81.down_ref, ...), custom_call_target="tpu_custom_call" | custom-call | flops 19327352832 | bytes 37748736 | tf_op jit(solution)/shard_map/widen/pallas_call | solution.py:401
  272.8 34.0 %narrow.1 = (bf16[2048,768]{1,0:T(8,128)(2,1)}, bf16[2048,768]{1,0:T(8,128)(2,1)}, bf16[768,768]{1,0:T(8,128)(2,1)}, f32[24,768]{1,0:T(8,128)}, bf16[192,1536]{1,0:T(8,128)(2,1)}) custom-call(bf16[2048,3072]{1,0:T(8,128)(2,1)} %get-tuple-element.82.grad_ref, bf16[2048,768]{1,0:T(8,128)(2,1)} %copy-done.6, bf16[2048,768]{1,0:T(8,128)(2,1)} %get-tuple-element.152.normed_ref, ...), custom_call_target="tpu_custom_call" | custom-call | flops 14495514624 | bytes 12582912 | tf_op jit(solution)/shard_map/narrow/pallas_call | solution.py:478
  306.8 92.0 %attend_back.1 = (bf16[2,1024,2304]{2,1,0:T(8,128)(2,1)}, bf16[2,512,1536]{2,1,0:T(8,128)(2,1)}, f32[2,6,16,128]{3,2,1,0:T(8,128)}, f32[768,384]{1,0:T(8,128)}, ...) custom-call(bf16[2,1024,2304]{2,1,0:T(8,128)(2,1)} %get-tuple-element.206, ...), custom_call_target="tpu_custom_call" | custom-call | flops 72477573120 | bytes 47185920 | tf_op jit(solution)/shard_map/attend_back/pallas_call | solution.py:1197
  398.8 0.0 copy-start.4
  398.8 4.6 fusion.27
  403.4 10.6 %convolution_bitcast_fusion = f32[768,2304]{1,0:T(8,128)S(1)} fusion(bf16[2,1024,2304]{2,1,0:T(8,128)(2,1)} %get-tuple-element.91, bf16[2,1024,768]{2,1,0:T(8,128)(2,1)S(1)} %copy-done.4), kind=kOutput, calls=%fused_computation.38 | convolution fusion | flops 7247757312 | bytes 19660800 | tf_op jit(solution)/shard_map/dot_general | solution.py:30
  414.0 0.1 slice.101
  414.1 1.0 collective-permute-start.1
  415.2 4.5 fusion.20
  419.7 0.0 copy-start.19
  419.7 0.0 copy-start.20
  419.7 2.0 pad_maximum_fusion.total_ref
  421.7 0.6 pad_maximum_fusion.3.last_ref
  422.3 45.8 %end.1 = (bf16[2048,768]{1,0:T(8,128)(2,1)}, f32[192,1152]{1,0:T(8,128)}, f32[16,768]{1,0:T(8,128)}) custom-call(bf16[2048,2304]{1,0:T(8,128)(2,1)} %bitcast.92, bf16[768,2304]{1,0:T(8,128)(2,1)} %get-tuple-element.72.rest_3_.rest_4_.matrix_ref, bf16[2048,768]{1,0:T(8,128)(2,1)} %get-tuple-element.92.first_ref, bf16[768,2304]{1,0:T(8,128)(2,1)} %pad_maximum_fusion.total_ref, ...), custom_call_target="tpu_custom_call" | custom-call | flops 7247757312 | bytes 37748736 | tf_op jit(solution)/shard_map/end/pallas_call | solution.py:652
  468.2 0.9 slice.71
  469.1 0.7 slice.72
  469.9 0.7 dynamic_slice.16
  470.5 0.7 dynamic-slice_bitcast_fusion
  471.2 0.0 collective-permute-done.1
  471.2 3.6 fusion.11
  474.8 0.9 copy.49
  475.7 0.7 copy.50
  476.4 1.0 copy.51
  477.4 1.0 copy.52
  (63 shorter events, 0.2 us)
Async XLA Ops:
  0.6 33.1 %copy-start = (s32[2,1,8]{2,1,0:T(1,128)S(1)}, s32[2,1,8]{2,1,0:T(1,128)}, u32[]{:S(2)}) copy-start(s32[2,1,8]{2,1,0:T(1,128)} %param.18) | copy-start | bytes 196
  0.6 35.5 %copy-start.2 = (bf16[2,1024,768]{2,1,0:T(8,128)(2,1)S(1)}, bf16[2,1024,768]{2,1,0:T(8,128)(2,1)}, u32[]{:S(2)}) copy-start(bf16[2,1024,768]{2,1,0:T(8,128)(2,1)} %param.19) | copy-start | bytes 9437188
  33.1 19.0 %collective-permute-start = (bf16[1,512,768]{2,1,0:T(8,128)(2,1)}, bf16[1,512,768]{2,1,0:T(8,128)(2,1)}, u32[]{:S(2)}, u32[]{:S(2)}) collective-permute-start(bf16[1,512,768]{2,1,0:T(8,128)(2,1)} %slice.58), channel_id=1, source_target_pairs={{0,1},{1,0},{2,3},{3,2},{4,5},{5,4},{6,7},{7,6},{8,9},{9,8},{10,11... | collective-permute-start | bytes 2359304 | tf_op jit(solution)/shard_map/ppermute | solution.py:1232
  36.1 1.5 copy-start.14
  37.6 14.5 %copy-start.10 = (bf16[512,768]{1,0:T(8,128)(2,1)S(1)}, bf16[512,768]{1,0:T(8,128)(2,1)}, u32[]{:S(2)}) copy-start(bf16[512,768]{1,0:T(8,128)(2,1)} %get-tuple-element.73) | copy-start | bytes 2359300
  176.7 3.7 slice-start
  177.5 2.8 copy-start.21
  177.5 2.8 slice-start.1
  180.3 19.9 %copy-start.5 = (bf16[2048,768]{1,0:T(8,128)(2,1)}, bf16[2048,768]{1,0:T(8,128)(2,1)S(1)}, u32[]{:S(2)}) copy-start(bf16[2048,768]{1,0:T(8,128)(2,1)S(1)} %get-tuple-element.153.hidden_ref) | copy-start | bytes 9437188
  215.2 1.9 copy-start.3
  215.2 1.9 copy-start.15
  216.1 3.5 copy-start.16
  216.1 3.5 copy-start.17
  217.1 8.2 %slice-start.2 = ((s8[12582912]{0:T(1024)(128)(4,1)}), s8[4194304]{0:T(1024)(128)(4,1)S(1)}, s32[]{:S(2)}) async-start(s8[12582912]{0:T(1024)(128)(4,1)} %bitcast.98), calls=%async_computation.2 | async-start | bytes 8388608
  217.1 8.2 %slice-start.3 = ((s8[12582912]{0:T(1024)(128)(4,1)}), s8[4194304]{0:T(1024)(128)(4,1)S(1)}, s32[]{:S(2)}) async-start(s8[12582912]{0:T(1024)(128)(4,1)} %bitcast.98), calls=%async_computation.3 | async-start | bytes 8388608
  219.6 5.6 %slice-start.4 = ((s8[12582912]{0:T(1024)(128)(4,1)}), s8[4194304]{0:T(1024)(128)(4,1)S(1)}, s32[]{:S(2)}) async-start(s8[12582912]{0:T(1024)(128)(4,1)} %bitcast.98), calls=%async_computation.4 | async-start | bytes 8388608
  223.6 14.0 %copy-start.6 = (bf16[2048,768]{1,0:T(8,128)(2,1)}, bf16[2048,768]{1,0:T(8,128)(2,1)S(1)}, u32[]{:S(2)}) copy-start(bf16[2048,768]{1,0:T(8,128)(2,1)S(1)} %get-tuple-element.148.second_ref) | copy-start | bytes 9437188
  239.0 33.8 %copy-start.22 = (bf16[2,1024,768]{2,1,0:T(8,128)(2,1)S(1)}, bf16[2,1024,768]{2,1,0:T(8,128)(2,1)}, u32[]{:S(2)}) copy-start(bf16[2,1024,768]{2,1,0:T(8,128)(2,1)} %get-tuple-element.78.out_ref) | copy-start | bytes 9437188
  272.8 34.0 %copy-start.23 = (f32[2,6,2,1024]{3,2,1,0:T(2,128)S(1)}, f32[2,6,2,1024]{3,2,1,0:T(2,128)}, u32[]{:S(2)}) copy-start(f32[2,6,2,1024]{3,2,1,0:T(2,128)} %get-tuple-element.85.lse_ref) | copy-start | bytes 294916
  398.8 4.6 copy-start.4
  403.4 11.8 %copy-start.11 = (bf16[512,768]{1,0:T(8,128)(2,1)S(1)}, bf16[512,768]{1,0:T(8,128)(2,1)}, u32[]{:S(2)}) copy-start(bf16[512,768]{1,0:T(8,128)(2,1)} %get-tuple-element.73) | copy-start | bytes 2359300
  403.4 11.8 %copy-start.24 = (bf16[2,512,1536]{2,1,0:T(8,128)(2,1)S(1)}, bf16[2,512,1536]{2,1,0:T(8,128)(2,1)}, u32[]{:S(2)}) copy-start(bf16[2,512,1536]{2,1,0:T(8,128)(2,1)} %get-tuple-element.89) | copy-start | bytes 9437188
  414.1 57.1 %collective-permute-start.1 = (bf16[1,512,768]{2,1,0:T(8,128)(2,1)}, bf16[1,512,768]{2,1,0:T(8,128)(2,1)}, u32[]{:S(2)}, u32[]{:S(2)}) collective-permute-start(bf16[1,512,768]{2,1,0:T(8,128)(2,1)} %bitcast.22), channel_id=1, source_target_pairs={{0,1},{1,0},{2,3},{3,2},{4,5},{5,4},{6,7},{7,6},{8,9},{9,8},{10,11... | collective-permute-start | bytes 2359304 | tf_op jit(solution)/shard_map/ppermute | solution.py:1232
  419.7 2.0 copy-start.18
  419.7 2.0 copy-start.19
  419.7 2.0 copy-start.20
  422.3 48.9 %copy-start.12 = (bf16[512,768]{1,0:T(8,128)(2,1)S(1)}, bf16[512,768]{1,0:T(8,128)(2,1)}, u32[]{:S(2)}) copy-start(bf16[512,768]{1,0:T(8,128)(2,1)} %get-tuple-element.97) | copy-start | bytes 2359300
  468.2 6.6 %copy-start.9 = (f32[192,1152]{1,0:T(8,128)S(1)}, f32[192,1152]{1,0:T(8,128)}, u32[]{:S(2)}) copy-start(f32[192,1152]{1,0:T(8,128)} %get-tuple-element.200) | copy-start | bytes 2654212
  468.2 7.5 %copy-start.13 = (f32[192,384]{1,0:T(8,128)S(1)}, f32[192,384]{1,0:T(8,128)}, u32[]{:S(2)}) copy-start(f32[192,384]{1,0:T(8,128)} %get-tuple-element.201) | copy-start | bytes 884740
  468.2 8.2 %copy-start.8 = (f32[192,1536]{1,0:T(8,128)S(1)}, f32[192,1536]{1,0:T(8,128)}, u32[]{:S(2)}) copy-start(f32[192,1536]{1,0:T(8,128)} %get-tuple-element.202) | copy-start | bytes 3538948
  471.2 7.2 %copy-start.1 = (s32[2,1,8]{2,1,0:T(1,128)S(1)}, s32[2,1,8]{2,1,0:T(1,128)}, u32[]{:S(2)}) copy-start(s32[2,1,8]{2,1,0:T(1,128)} %param.18) | copy-start | bytes 196
  471.2 6.2 %copy-start.7 = (f32[768,384]{1,0:T(8,128)S(1)}, f32[768,384]{1,0:T(8,128)}, u32[]{:S(2)}) copy-start(f32[768,384]{1,0:T(8,128)} %get-tuple-element.203) | copy-start | bytes 3538948

commit v5 on v4

--- a/solution.py
+++ b/solution.py
@@ -74,24 +74,29 @@
 
 
 class Gather:
-    def __init__(self, own, whole, order, sends, arrivals, base):
+    def __init__(self, own, whole, order, sends, arrivals, base, rows=None, moved=None):
         self.own, self.whole, self.order = own, whole, order
         self.sends, self.arrivals, self.base = sends, arrivals, base
+        self.low, self.count = rows if rows else (0, own.shape[0])
         self.copies = spread(order)
         self.position = here(("row", "col"))
+        self.bit, self.moved = moved if moved else (None, None)
 
     def slot(self, position):
         depth, columns = self.own.shape
-        first = pl.multiple_of(position["row"] * depth, 16)
+        first = pl.multiple_of(position["row"] * depth + self.low, 16)
         start = pl.multiple_of(position["col"] * columns, LANES)
-        return self.whole.at[pl.ds(first, depth), pl.ds(start, columns)]
-
-    def copy(self, index):
-        stage, crossed = self.copies[index]
-        axis, mask = self.order[stage]
-        slot = self.slot(place_of(self.position, crossed))
+        return self.whole.at[pl.ds(first, self.count), pl.ds(start, columns)]
+
+    def origin(self, crossed):
+        if not crossed:
+            return self.own.at[pl.ds(self.low, self.count)]
+        return self.moved if crossed == (self.bit,) else self.slot(place_of(self.position, crossed))
+
+    def remote(self, index, source, slot):
+        axis, mask = self.order[self.copies[index][0]]
         return pltpu.make_async_remote_copy(
-            src_ref=slot if crossed else self.own,
+            src_ref=source,
             dst_ref=slot,
             send_sem=self.sends.at[self.base + index],
             recv_sem=self.arrivals.at[self.base + index],
@@ -99,35 +104,39 @@
             device_id_type=pl.DeviceIdType.MESH,
         )
 
+    def copy(self, index):
+        crossed = self.copies[index][1]
+        return self.remote(index, self.origin(crossed), self.slot(place_of(self.position, crossed)))
+
     def arrival(self, index):
         stage, crossed = self.copies[index]
-        axis, mask = self.order[stage]
         slot = self.slot(place_of(self.position, crossed + (self.order[stage],)))
-        return pltpu.make_async_remote_copy(
-            src_ref=slot,
-            dst_ref=slot,
-            send_sem=self.sends.at[self.base + index],
-            recv_sem=self.arrivals.at[self.base + index],
-            device_id=flipped(here((axis,)), axis, mask),
-            device_id_type=pl.DeviceIdType.MESH,
-        )
-
-    def loading(self, held, semaphores):
-        return pltpu.make_async_copy(self.own, held, semaphores.at[0])
-
-    def placing(self, held, semaphores):
-        return pltpu.make_async_copy(held, self.slot(self.position), semaphores.at[1])
+        return self.remote(index, slot, slot)
+
+    def placed(self):
+        pairs = [(self.origin(()), self.slot(self.position))]
+        if self.bit:
+            pairs.append((self.moved, self.slot(place_of(self.position, (self.bit,)))))
+        return pairs
 
     def source(self, index):
         crossed = self.copies[index][1]
         last = self.order.index(crossed[-1])
-        return self.copies.index((last, crossed[:-1]))
+        found = self.copies.index((last, crossed[:-1]))
+        return found if self.sent(found) else None
+
+    def sent(self, index):
+        stage, crossed = self.copies[index]
+        return bool(crossed) or self.order[stage] != self.bit
 
     def first(self):
-        return [i for i, (stage, crossed) in enumerate(self.copies) if not crossed]
+        return [i for i, (stage, crossed) in enumerate(self.copies) if not crossed and self.sent(i)]
 
     def later(self):
         return [i for i, (stage, crossed) in enumerate(self.copies) if crossed]
+
+    def used(self):
+        return [i for i in range(len(self.copies)) if self.sent(i)]
 
 
 class Reduce:
@@ -537,8 +546,8 @@
 
 
 def end_kernel(
-    own_ref, matrix_ref, first_ref, total_ref, pair_ref, norm_ref, bias_ref, last_ref,
-    tokens_ref, out_ref, all_ref, *scratch, grid, dp,
+    own_ref, matrix_ref, first_ref, total_ref, sent_ref, pair_ref, norm_ref, bias_ref, last_ref,
+    tokens_ref, out_ref, all_ref, came_ref, *scratch, grid, dp,
 ):
     step = pl.program_id(0)
     final = pl.num_programs(0) - 1
@@ -558,7 +567,15 @@
         )
         part.size = depth
         parts.append(part)
-    running, came, small_sends, small_arrivals = scratch[24:]
+    running, came, small_sends, small_arrivals, sent_sem, came_sem = scratch[24:]
+    exchange = pltpu.make_async_remote_copy(
+        src_ref=sent_ref,
+        dst_ref=came_ref,
+        send_sem=sent_sem,
+        recv_sem=came_sem,
+        device_id=flipped(here(("col",)), "col", 1),
+        device_id_type=pl.DeviceIdType.MESH,
+    )
     targets = [flipped(here((axis,)), axis, mask) for axis, mask in row_bits + col_bits]
     targets += [across_target(axis, mask) for axis, mask in across]
 
@@ -587,6 +604,8 @@
         for number, stage in batch:
             parts[number].prepare(stage)
             parts[number].launch(stage)
+            if number == 3 and stage == len(orders[0]) - 1:
+                exchange.start()
             if number == 1:
                 small(stage - 1).wait_recv()
                 running[stage] = running[stage - 1] + came[stage - 1]
@@ -633,9 +652,10 @@
         all_ref[...] = running[stages - 1] + came[stages - 1]
         for stage in range(stages):
             small(stage).wait_send()
-
-
-def end(own, matrix, first, total, sums, shape, grid, dp):
+        exchange.wait()
+
+
+def end(own, matrix, first, total, sent, sums, shape, grid, dp):
     lines = 8 + sums[2].shape[1] // first.shape[1]
     lines = (lines + -lines % 8, first.shape[1])
     hops = dp.bit_length() - 1
@@ -657,14 +677,16 @@
             whole(matrix.shape, pipeline_mode=pl.Buffered(buffer_count=1)),
             block(width),
             pl.BlockSpec(memory_space=pl.ANY),
+            pl.BlockSpec(memory_space=pl.ANY),
             pl.BlockSpec(sums[0].shape, lambda i: (0, 0, 0, 0)),
             *(whole(value.shape) for value in sums[1:]),
         ],
-        out_specs=[block(width), whole(shape), whole(lines)],
+        out_specs=[block(width), whole(shape), whole(lines), pl.BlockSpec(memory_space=pl.ANY)],
         out_shape=[
             jax.ShapeDtypeStruct((rows, width), LOW),
             jax.ShapeDtypeStruct(shape, FULL),
             jax.ShapeDtypeStruct(lines, FULL),
+            jax.ShapeDtypeStruct(sent.shape, LOW),
         ],
         scratch_shapes=reduce_scratch([(shape[0] // 4, shape[1])] * 4, grid, hops)
         + [
@@ -672,6 +694,8 @@
             pltpu.VMEM((stages,) + lines, FULL),
             pltpu.SemaphoreType.DMA((stages,)),
             pltpu.SemaphoreType.DMA((stages,)),
+            pltpu.SemaphoreType.DMA,
+            pltpu.SemaphoreType.DMA,
         ],
         compiler_params=pltpu.CompilerParams(
             collective_id=3, has_side_effects=True, vmem_limit_bytes=56 * 2**20
@@ -680,7 +704,7 @@
             flops=2 * rows * width * own.shape[1], bytes_accessed=8 * own.size, transcendentals=0
         ),
         name="end",
-    )(own, matrix, first, total, *sums)
+    )(own, matrix, first, total, sent, *sums)
 
 
 def attend_step(q_ref, k_ref, v_ref, ok_ref, ov_ref, mask_ref, out_ref, lse_ref, *, head, exact):
@@ -752,7 +776,7 @@
 
 
 def attend_kernel(
-    q_ref, k_ref, v_ref, ok_ref, ov_ref, mask_ref, out_block, up_block, down_block,
+    q_ref, k_ref, v_ref, ok_ref, ov_ref, mask_ref, out_block, up_block, down_block, moved_block,
     out_ref, lse_ref, flag_ref, out_whole, up_whole, down_whole,
     sends, arrivals, placed, *held, head, grid,
 ):
@@ -764,52 +788,63 @@
     first_order = tuple(col_bits + row_bits[::-1])
     second_order = tuple(row_bits[:0:-1] + col_bits + row_bits[:1])
     per = len(spread(first_order))
+    half = up_block.shape[0] // 2
+    down_moved = (row_bits[-1], moved_block)
     parts = [
         Gather(out_block, out_whole, first_order, sends, arrivals, 0),
-        Gather(down_block, down_whole, first_order, sends, arrivals, per),
-        Gather(up_block, up_whole, second_order, sends, arrivals, 2 * per),
+        Gather(down_block, down_whole, first_order, sends, arrivals, per, moved=down_moved),
+        Gather(up_block, up_whole, second_order, sends, arrivals, 2 * per, (0, half)),
+        Gather(up_block, up_whole, first_order, sends, arrivals, 3 * per, (half, half)),
     ]
+    locals_ = [pair for part in parts for pair in part.placed()]
+
+    def load(number):
+        return pltpu.make_async_copy(locals_[number][0], held[number], placed.at[number, 0])
+
+    def store(number):
+        return pltpu.make_async_copy(held[number], locals_[number][1], placed.at[number, 1])
 
     @pl.when(step == 0)
     def _():
         greet(row_bits + col_bits)
-        for index in parts[0].first():
+        for index in range(per):
             for part in parts:
-                part.copy(index).start()
-        for number, part in enumerate(parts):
-            part.loading(held[number], placed.at[number]).start()
+                if index in part.first():
+                    part.copy(index).start()
+        for number in range(len(held)):
+            load(number).start()
 
     @pl.when(step == 1)
     def _():
-        for number, part in enumerate(parts):
-            part.loading(held[number], placed.at[number]).wait()
-            part.placing(held[number], placed.at[number]).start()
-
-    last = len(first_order) - 1
+        for number in range(len(held)):
+            load(number).wait()
+            store(number).start()
+
+    reached = (
+        {("col",): 2, ("row",): 4, ("col", "row"): 7},
+        {("col",): 6, ("row",): 1},
+        {("row",): 3, ("col",): 10},
+        {("col",): 8, ("row",): 6},
+    )
     events = {}
     for number, part in enumerate(parts):
         for index in part.later():
-            stage, crossed = part.copies[index]
-            if len(crossed) > 1 and number:
-                when = final
-            elif stage == last:
-                when = (5, 10, 10)[number] + 2 * (len(crossed) > 1)
-            else:
-                when = (2, 6, 7)[number]
-            events.setdefault(min(when, final), []).append((part, index))
+            crossed = tuple(axis for axis, mask in part.copies[index][1])
+            when = min(reached[number].get(crossed, final), final)
+            events.setdefault(when, []).append((part, index))
     waited = set()
+
+    def forward(batch):
+        for part, index in batch:
+            origin = part.source(index)
+            if origin is not None and (part.base, origin) not in waited:
+                waited.add((part.base, origin))
+                part.arrival(origin).wait_recv()
+            part.copy(index).start()
+
     for when in sorted(events):
-        if when == final:
-            continue
-
-        @pl.when(step == when)
-        def _(batch=events[when]):
-            for part, index in batch:
-                origin = part.source(index)
-                if (part.base, origin) not in waited:
-                    waited.add((part.base, origin))
-                    part.arrival(origin).wait_recv()
-                part.copy(index).start()
+        if when < final:
+            pl.when(step == when)(functools.partial(forward, events[when]))
 
     flags = attend_step(
         q_ref, k_ref, v_ref, ok_ref, ov_ref, mask_ref, out_ref, lse_ref, head=head, exact=False
@@ -818,15 +853,11 @@
 
     @pl.when(step == final)
     def _():
-        for part, index in events.get(final, []):
-            origin = part.source(index)
-            if (part.base, origin) not in waited:
-                waited.add((part.base, origin))
-                part.arrival(origin).wait_recv()
-            part.copy(index).start()
-        for number, part in enumerate(parts):
-            part.placing(held[number], placed.at[number]).wait()
-            for index in range(per):
+        forward(events.get(final, []))
+        for number in range(len(held)):
+            store(number).wait()
+        for part in parts:
+            for index in part.used():
                 if (part.base, index) not in waited:
                     part.arrival(index).wait_recv()
                 part.copy(index).wait_send()
@@ -866,12 +897,15 @@
     )(own, own, own, other, other, mask)
 
 
-def attend(own, other, mask, blocks, grid, head):
+def attend(own, other, mask, blocks, moved, grid, head):
     batch, rows, steps, spec, ins = attend_specs(own, other, mask)
     heads = LANES // head
     half = rows // 2
     anywhere = pl.BlockSpec(memory_space=pl.ANY)
-    copies = 3 * (grid[0] * grid[1] - 1)
+    copies = 4 * (grid[0] * grid[1] - 1)
+    out_shape, up_shape, down_shape = (block.shape for block in blocks)
+    half_shape = (up_shape[0] // 2, up_shape[1])
+    held = [out_shape, down_shape, down_shape, half_shape, half_shape]
     work = batch * rows * (rows + CLEN) * steps * LANES
     wholes = [
         jax.ShapeDtypeStruct((block.shape[0] * grid[0], block.shape[1] * grid[1]), LOW)
@@ -880,7 +914,7 @@
     out, lse, flags, *wholes = pl.pallas_call(
         functools.partial(attend_kernel, head=head, grid=grid),
         grid=(batch, steps),
-        in_specs=ins + [anywhere] * 3,
+        in_specs=ins + [anywhere] * 4,
         out_specs=[
             spec(rows, 0),
             pl.BlockSpec((1, 1, heads, rows), lambda m, p: (m, p, 0, 0)),
@@ -896,15 +930,15 @@
         scratch_shapes=[
             pltpu.SemaphoreType.DMA((copies,)),
             pltpu.SemaphoreType.DMA((copies,)),
-            pltpu.SemaphoreType.DMA((3, 2)),
+            pltpu.SemaphoreType.DMA((len(held), 2)),
         ]
-        + [pltpu.VMEM(blocks[i].shape, LOW) for i in (0, 2, 1)],
+        + [pltpu.VMEM(shape, LOW) for shape in held],
         compiler_params=pltpu.CompilerParams(collective_id=1, has_side_effects=True),
         cost_estimate=pl.CostEstimate(
             flops=16 * work, bytes_accessed=own.size * 4, transcendentals=work // head
         ),
         name="attend",
-    )(own, own, own, other, other, mask, *blocks)
+    )(own, own, own, other, other, mask, *blocks, moved)
     _, out, lse = lax.while_loop(
         lambda state: state[0] > 0.5,
         lambda state: (jnp.zeros((), FULL), *attend_again(own, other, mask, head)),
@@ -931,9 +965,12 @@
     for index in part.first():
         part.copy(index).start()
     exchange.start()
-    part.loading(held, placed).start()
-    part.loading(held, placed).wait()
-    part.placing(held, placed).start()
+    source, slot = part.placed()[0]
+    load = pltpu.make_async_copy(source, held, placed.at[0])
+    store = pltpu.make_async_copy(held, slot, placed.at[1])
+    load.start()
+    load.wait()
+    store.start()
     waited = set()
     for index in part.later():
         origin = part.source(index)
@@ -945,7 +982,7 @@
         if index not in waited:
             part.arrival(index).wait_recv()
         part.copy(index).wait_send()
-    part.placing(held, placed).wait()
+    store.wait()
     exchange.wait()
 
 
@@ -1331,7 +1368,10 @@
     tokens = inputs.reshape(batch * rows, width)
     if direct:
         early, qkv_matrix = begin(inputs, qkv_weight, grid)
-        late, qkv_matrix = lax.optimization_barrier((inputs[1:, :half], qkv_matrix))
+        late, moved, qkv_matrix = lax.optimization_barrier(
+            (inputs[1:, :half], down_weight, qkv_matrix)
+        )
+        moved = swapped(moved, "row", masks_of("row")[-1])
         other_tokens = cat([early[None], swapped(late, "col", 1)], axis=0)
     else:
         other_tokens = swapped(inputs[:, :half], "col", 1)
@@ -1345,7 +1385,7 @@
     other = other.reshape(batch, half, 2 * width)
     if direct:
         attended, lse, (out_matrix, up_matrix, down_matrix) = attend(
-            own, other, mask, blocks, grid, head
+            own, other, mask, blocks, moved, grid, head
         )
     else:
         attended, lse = attend_again(own, other, mask, head)
@@ -1406,9 +1446,6 @@
             *operands, totals, qkv_matrix, shapes, grid, lax.axis_size("dp")
         )
         sent = nt(other_grad[1:].reshape(-1, 2 * width), pair_matrix).astype(LOW)
-        sent, own_grad = lax.optimization_barrier((sent, own_grad))
-        late = swapped(sent.reshape(batch - 1, half, width), "col", 1)
-        received = cat([received[None], late], axis=0)
         own_grad = own_grad.reshape(batch * rows, 3 * width)
         other_grad = other_grad.reshape(batch * half, 2 * width)
     else:
@@ -1432,11 +1469,12 @@
         jnp.sum(grad_out, axis=0),
     ]
     if direct:
-        grad_tokens, qkv_grad, sums = end(
-            own_grad, qkv_matrix, grad_first, qkv_total.astype(LOW),
+        grad_tokens, qkv_grad, sums, late = end(
+            own_grad, qkv_matrix, grad_first, qkv_total.astype(LOW), sent,
             (pair_sums, norm_sums, bias_sums, jnp.stack(last_sums)),
             qkv_weight.shape, grid, lax.axis_size("dp"),
         )
+        received = cat([received[None], late.reshape(batch - 1, half, width)], axis=0)
         received = jnp.pad(received, ((0, 0), (0, rows - half), (0, 0))).astype(FULL)
         grad_tokens = (grad_tokens.reshape(batch, rows, width).astype(FULL) + received).astype(LOW)
         sums = sums.reshape(-1)[: 8 * width + up_bias.shape[0]]

time: 486 us -> 474 us (0.975)
  Pallas kernels: 344 us -> 333 us
    pallas_call x1, Pallas kernels: 33.8 us -> 88 us  [widen(): pl.pallas_call(functools.partial(widen_kernel, grid=grid, whens=(0, 1, 4)...]
    pallas_call x1 -> x0, Pallas kernels: 51.8 us -> none  [attend_again(): pl.pallas_call(functools.partial(attend_again_kernel, head=head), grid=(b...]
    pallas_call x1, Pallas kernels: 56.4 us -> 44.5 us  [attend(): pl.pallas_call(functools.partial(attend_kernel, head=head, grid=grid), gr...]
  transfers between devices with their start and end apart: 2 -> 2, of which waited for: 0 -> 0; matrix products, arithmetic and copies ran while one was open for 6% -> 5% of each run, Pallas kernels for 10% -> 0%
where the time goes in v5:
time: 474 us; the launch traced here: 465 us
  Pallas kernels  333 us (70%)
  matrix products  87.9 us (19%)
  other arithmetic  22.2 us (5%)
  local copies, waits for them, and re-layouts  16.6 us (4%)
    pallas_call x1, Pallas kernels, attend_back(): pl.pallas_call(functools.partial(attend_back_kernel, head=head, scale=hea...  91.5 us
    pallas_call x1, Pallas kernels, widen(): pl.pallas_call(functools.partial(widen_kernel, grid=grid, whens=(0, 1, 4)...  88 us
    dot_general x5, matrix products, nn(): lax.dot_general(left, right, (((1,), (0,)), ((), ())), preferred_element_...  57.5 us
    pallas_call x1, Pallas kernels, end(): pl.pallas_call(functools.partial(end_kernel, grid=grid, dp=dp), grid=(row...  45.4 us
    pallas_call x1, Pallas kernels, attend(): pl.pallas_call(functools.partial(attend_kernel, head=head, grid=grid), gr...  44.5 us
    pallas_call x1, Pallas kernels, narrow(): pl.pallas_call(functools.partial(narrow_kernel, grid=grid, whens=(0, 1, 5...  33.7 us
    pallas_call x1, Pallas kernels, begin(): pl.pallas_call(functools.partial(begin_kernel, grid=grid), in_specs=[anyw...  30.2 us
    dot_general x3, matrix products, tn(): lax.dot_general(left, right, (((0,), (0,)), ((), ())), preferred_element_...  28.2 us
  transfers between devices with their start and end apart: 2, of which 0 were waited for; matrix products, arithmetic and copies ran while one was open for 5% of the time, Pallas kernels for 0%

profile of v5, /device:TPU:8, one launch (start us, length us, event | category | flops | bytes accessed | tf_op | source)
XLA Modules:
  0.0 464.7 jit_solution(8440151038911634936)
XLA Ops:
  0.6 0.0 copy-start
  0.6 0.0 copy-start.2
  0.7 2.2 slice.58
  2.9 30.2 %begin.1 = (bf16[512,768]{1,0:T(8,128)(2,1)}, bf16[768,2304]{1,0:T(8,128)(2,1)}) custom-call(bf16[2,1024,768]{2,1,0:T(8,128)(2,1)} %tokens_ref.1, bf16[192,1152]{1,0:T(8,128)(2,1)} %block_ref.1), custom_call_target="tpu_custom_call" | custom-call | bytes 28311552 | tf_op jit(solution)/shard_map/begin/pallas_call | solution.py:993
  33.1 0.6 collective-permute-start
  33.7 1.5 collective-permute-start.1
  35.2 0.1 constant_dynamic-slice_fusion
  35.3 0.1 broadcast_bitcast_fusion
  35.4 2.2 slice_reduce_fusion.1
  37.6 0.0 copy-done.2
  37.6 1.4 convert_reduce_fusion
  39.1 12.4 %add_convert_fusion = bf16[2304,2048]{0,1:T(8,128)(2,1)} fusion(bf16[2048,768]{1,0:T(8,128)(2,1)} %bitcast.79, bf16[768,2304]{1,0:T(8,128)(2,1)} %get-tuple-element.72.rest_3_.rest_4_.matrix_ref, f32[2304]{0:T(1024)S(1)} %pad_maximum_fusion.2), kind=kOutput, calls=%fused_computation.12 | convolution fusion | flops 7257194496 | bytes 16131072 | tf_op jit(solution)/shard_map/dot_general | solution.py:26
  51.4 0.6 copy.32
  52.0 0.6 stack.14
  52.7 0.9 fusion.33.mask_ref
  53.6 0.0 collective-permute-done
  53.6 1.3 pad_maximum_fusion.1
  54.8 4.5 add_convert_fusion.2
  59.3 0.0 collective-permute-done.1.moved_block
  59.4 44.5 %attend.1 = (bf16[2,1024,768]{2,1,0:T(8,128)(2,1)}, f32[2,6,2,1024]{3,2,1,0:T(2,128)}, f32[2,6,8,512]{3,2,1,0:T(8,128)}, bf16[768,768]{1,0:T(8,128)(2,1)}, bf16[...) custom-call(bf16[2,1024,2304]{2,1,0:T(8,128)(2,1)} %bitcast.72, bf16[2,1024,2304]{2,1,0:T(8,128)(2,1)} %bitcast.73, ...), custom_call_target="tpu_custom_call" | custom-call | flops 28991029248 | bytes 18874368 | tf_op jit(solution)/shard_map/attend/pallas_call | solution.py:914
  103.9 1.6 reduce_max.9
  105.5 0.9 while.12
  106.3 6.1 %fusion.39 = (f32[2048]{0:T(1024)S(1)}, f32[2048,768]{1,0:T(8,128)S(1)}) fusion(f32[768]{0:T(1024)S(1)} %get-tuple-element.129, bf16[2048,768]{1,0:T(8,128)(2,1)} %bitcast.95, bf16[768,768]{1,0:T(8,128)(2,1)} %get-tuple-element.80.out_ref, bf16[2048,768]{1,0:T(8,128)(2,1)} %bitcast.80), kind=kOutput, calls=%fused_computation.85 | convolution fusion | flops 2422208512 | bytes 13773824 | tf_op jit(solution)/shard_map/dot_general | solution.py:26
  112.5 0.0 slice-start
  112.5 0.8 multiply_reduce_fusion.1
  113.3 0.0 copy-start.21
  113.3 0.0 slice-start.1
  113.3 2.8 multiply_convert_fusion.1
  116.2 19.6 %fusion.8 = (bf16[2048,3072]{1,0:T(8,128)(2,1)}, bf16[2048,3072]{1,0:T(8,128)(2,1)}) fusion(f32[3072]{0:T(1024)S(1)} %copy-done.21, bf16[2048,768]{1,0:T(8,128)(2,1)S(1)} %get-tuple-element.153.hidden_ref, bf16[768,3072]{1,0:T(8,128)(2,1)S(1)} %bitcast.98), kind=kOutput, calls=%fused_computation.9 | convolution fusion | flops 9739173888 | bytes 33042432 | tf_op jit(solution)/shard_map/dot_general | solution.py:26
  135.8 14.9 %fusion.40 = (f32[2048]{0:T(1024)S(1)}, f32[2048,768]{1,0:T(8,128)S(1)}) fusion(f32[768]{0:T(1024)S(1)} %get-tuple-element.126, bf16[2048,3072]{1,0:T(8,128)(2,1)} %get-tuple-element.150, bf16[3072,768]{1,0:T(8,128)(2,1)} %get-tuple-element.82.down_ref, f32[768]{0:T(1024)S(1)} %get-tuple-element.127, f32[768]{0:T(1024)S(1)} %get-tuple-element.128, ...), kind=kOutput, calls=%fused_computation.86 | convolution fusion | flops 9674684416 | bytes 29918208 | tf_op jit(solution)/shard_map/dot_general | solution.py:26
  150.7 0.0 copy-start.3
  150.7 0.0 copy-start.14
  150.7 0.8 multiply_reduce_fusion
  151.5 0.0 copy-start.15
  151.5 0.0 copy-start.16
  151.6 1.0 copy-done.3
  152.6 2.3 fusion.18
  154.9 0.0 slice-start.4
  155.0 4.0 fusion.37
  159.0 0.6 stack.12
  159.6 1.0 stack.13
  160.6 12.2 %convolution_convert_fusion.total_ref = bf16[3072,768]{1,0:T(8,128)(2,1)} fusion(bf16[2048,3072]{1,0:T(8,128)(2,1)S(1)} %bitcast.100, bf16[2048,768]{1,0:T(8,128)(2,1)S(1)} %get-tuple-element.148.second_ref), kind=kOutput, calls=%fused_computation.39 | convolution fusion | flops 9666035712 | bytes 20447232 | tf_op jit(solution)/shard_map/dot_general | solution.py:30
  172.8 1.3 copy.20.inverse_ref
  174.1 88.0 %widen.1 = (bf16[2048,3072]{1,0:T(8,128)(2,1)}, bf16[768,3072]{1,0:T(8,128)(2,1)}, f32[8,3072]{1,0:T(8,128)}, bf16[768,384]{1,0:T(8,128)(2,1)}) custom-call(bf16[2048,768]{1,0:T(8,128)(2,1)} %copy-done.5, bf16[2048,768]{1,0:T(8,128)(2,1)} %copy-done.4, bf16[3072,768]{1,0:T(8,128)(2,1)} %get-tuple-element.82.down_ref, ...), custom_call_target="tpu_custom_call" | custom-call | flops 19327352832 | bytes 37748736 | tf_op jit(solution)/shard_map/widen/pallas_call | solution.py:410
  262.2 33.7 %narrow.1 = (bf16[2048,768]{1,0:T(8,128)(2,1)}, bf16[2048,768]{1,0:T(8,128)(2,1)}, bf16[768,768]{1,0:T(8,128)(2,1)}, f32[24,768]{1,0:T(8,128)}, bf16[192,1536]{1,0:T(8,128)(2,1)}) custom-call(bf16[2048,3072]{1,0:T(8,128)(2,1)} %get-tuple-element.83.grad_ref, bf16[2048,768]{1,0:T(8,128)(2,1)} %copy-done.5, bf16[2048,768]{1,0:T(8,128)(2,1)} %get-tuple-element.152.normed_ref, ...), custom_call_target="tpu_custom_call" | custom-call | flops 14495514624 | bytes 12582912 | tf_op jit(solution)/shard_map/narrow/pallas_call | solution.py:487
  295.9 91.5 %attend_back.1 = (bf16[2,1024,2304]{2,1,0:T(8,128)(2,1)}, bf16[2,512,1536]{2,1,0:T(8,128)(2,1)}, f32[2,6,16,128]{3,2,1,0:T(8,128)}, f32[768,384]{1,0:T(8,128)}, ...) custom-call(bf16[2,1024,2304]{2,1,0:T(8,128)(2,1)} %get-tuple-element.206, ...), custom_call_target="tpu_custom_call" | custom-call | flops 72477573120 | bytes 47185920 | tf_op jit(solution)/shard_map/attend_back/pallas_call | solution.py:1234
  387.5 11.5 %convolution_bitcast_fusion = f32[768,2304]{1,0:T(8,128)S(1)} fusion(bf16[2,1024,2304]{2,1,0:T(8,128)(2,1)} %get-tuple-element.90, bf16[2,1024,768]{2,1,0:T(8,128)(2,1)} %tokens_ref.1), kind=kOutput, calls=%fused_computation.38 | convolution fusion | flops 7247757312 | bytes 19660800 | tf_op jit(solution)/shard_map/dot_general | solution.py:30
  398.9 0.1 slice.101
  399.1 2.3 fusion.27.sent_ref
  401.4 4.5 fusion.20
  405.9 0.0 copy-start.18
  405.9 0.0 copy-start.19
  405.9 2.0 pad_maximum_fusion.total_ref
  408.0 0.6 pad_maximum_fusion.3.last_ref
  408.6 45.4 %end.1 = (bf16[2048,768]{1,0:T(8,128)(2,1)}, f32[192,1152]{1,0:T(8,128)}, f32[16,768]{1,0:T(8,128)}, bf16[512,768]{1,0:T(8,128)(2,1)}) custom-call(bf16[2048,2304]{1,0:T(8,128)(2,1)} %bitcast.93, bf16[768,2304]{1,0:T(8,128)(2,1)} %get-tuple-element.72.rest_3_.rest_4_.matrix_ref, bf16[2048,768]{1,0:T(8,128)(2,1)} %get-tuple-element.91.first_ref, ...), custom_call_target="tpu_custom_call" | custom-call | flops 7247757312 | bytes 37748736 | tf_op jit(solution)/shard_map/end/pallas_call | solution.py:672
  454.0 0.9 slice.71
  454.9 0.7 slice.72
  455.7 0.7 dynamic-slice_bitcast_fusion
  456.3 0.7 dynamic_slice.16
  457.0 3.6 fusion.11
  460.6 0.9 copy.49
  461.5 0.7 copy.50
  462.2 1.0 copy.51
  463.2 1.0 copy.52
  (61 shorter events, 0.2 us)
Async XLA Ops:
  0.6 34.6 %copy-start = (s32[2,1,8]{2,1,0:T(1,128)S(1)}, s32[2,1,8]{2,1,0:T(1,128)}, u32[]{:S(2)}) copy-start(s32[2,1,8]{2,1,0:T(1,128)} %param.18) | copy-start | bytes 196
  0.6 37.0 %copy-start.2 = (bf16[2,1024,768]{2,1,0:T(8,128)(2,1)S(1)}, bf16[2,1024,768]{2,1,0:T(8,128)(2,1)}, u32[]{:S(2)}) copy-start(bf16[2,1024,768]{2,1,0:T(8,128)(2,1)} %param.19) | copy-start | bytes 9437188
  33.1 20.5 %collective-permute-start = (bf16[1,512,768]{2,1,0:T(8,128)(2,1)}, bf16[1,512,768]{2,1,0:T(8,128)(2,1)}, u32[]{:S(2)}, u32[]{:S(2)}) collective-permute-start(bf16[1,512,768]{2,1,0:T(8,128)(2,1)} %slice.58), channel_id=1, source_target_pairs={{0,1},{1,0},{2,3},{3,2},{4,5},{5,4},{6,7},{7,6},{8,9},{9,8},{10,11... | collective-permute-start | bytes 2359304 | tf_op jit(solution)/shard_map/ppermute | solution.py:1269
  33.7 25.6 %collective-permute-start.1 = (bf16[768,384]{1,0:T(8,128)(2,1)}, bf16[768,384]{1,0:T(8,128)(2,1)}, u32[]{:S(2)}, u32[]{:S(2)}) collective-permute-start(bf16[768,384]{1,0:T(8,128)(2,1)} %down_block.1), channel_id=1, source_target_pairs={{0,4},{2,6},{4,0},{6,2},{1,5},{3,7},{5,1},{7,3},{8,12},{10,14},{12... | collective-permute-start | bytes 1769480 | tf_op jit(solution)/shard_map/ppermute | solution.py:1269
  37.6 1.5 copy-start.13
  39.1 14.5 %copy-start.9 = (bf16[512,768]{1,0:T(8,128)(2,1)S(1)}, bf16[512,768]{1,0:T(8,128)(2,1)}, u32[]{:S(2)}) copy-start(bf16[512,768]{1,0:T(8,128)(2,1)} %get-tuple-element.73) | copy-start | bytes 2359300
  112.5 3.7 slice-start
  113.3 2.9 copy-start.21
  113.3 2.9 slice-start.1
  116.2 19.7 %copy-start.4 = (bf16[2048,768]{1,0:T(8,128)(2,1)}, bf16[2048,768]{1,0:T(8,128)(2,1)S(1)}, u32[]{:S(2)}) copy-start(bf16[2048,768]{1,0:T(8,128)(2,1)S(1)} %get-tuple-element.153.hidden_ref) | copy-start | bytes 9437188
  150.7 1.9 copy-start.3
  150.7 1.9 copy-start.14
  151.5 3.4 copy-start.15
  151.5 3.4 copy-start.16
  152.6 8.0 %slice-start.2 = ((s8[12582912]{0:T(1024)(128)(4,1)}), s8[4194304]{0:T(1024)(128)(4,1)S(1)}, s32[]{:S(2)}) async-start(s8[12582912]{0:T(1024)(128)(4,1)} %bitcast.99), calls=%async_computation.2 | async-start | bytes 8388608
  152.6 8.0 %slice-start.3 = ((s8[12582912]{0:T(1024)(128)(4,1)}), s8[4194304]{0:T(1024)(128)(4,1)S(1)}, s32[]{:S(2)}) async-start(s8[12582912]{0:T(1024)(128)(4,1)} %bitcast.99), calls=%async_computation.3 | async-start | bytes 8388608
  154.9 5.6 %slice-start.4 = ((s8[12582912]{0:T(1024)(128)(4,1)}), s8[4194304]{0:T(1024)(128)(4,1)S(1)}, s32[]{:S(2)}) async-start(s8[12582912]{0:T(1024)(128)(4,1)} %bitcast.99), calls=%async_computation.4 | async-start | bytes 8388608
  159.0 13.8 %copy-start.5 = (bf16[2048,768]{1,0:T(8,128)(2,1)}, bf16[2048,768]{1,0:T(8,128)(2,1)S(1)}, u32[]{:S(2)}) copy-start(bf16[2048,768]{1,0:T(8,128)(2,1)S(1)} %get-tuple-element.148.second_ref) | copy-start | bytes 9437188
  174.1 88.0 %copy-start.22 = (bf16[2,1024,768]{2,1,0:T(8,128)(2,1)S(1)}, bf16[2,1024,768]{2,1,0:T(8,128)(2,1)}, u32[]{:S(2)}) copy-start(bf16[2,1024,768]{2,1,0:T(8,128)(2,1)} %get-tuple-element.79.out_ref) | copy-start | bytes 9437188
  262.2 33.8 %copy-start.23 = (f32[2,6,2,1024]{3,2,1,0:T(2,128)S(1)}, f32[2,6,2,1024]{3,2,1,0:T(2,128)}, u32[]{:S(2)}) copy-start(f32[2,6,2,1024]{3,2,1,0:T(2,128)} %get-tuple-element.86.lse_ref) | copy-start | bytes 294916
  387.4 11.6 %copy-start.20 = (bf16[768,2304]{1,0:T(8,128)(2,1)S(1)}, bf16[768,2304]{1,0:T(8,128)(2,1)}, u32[]{:S(2)}) copy-start(bf16[768,2304]{1,0:T(8,128)(2,1)} %get-tuple-element.72.rest_3_.rest_4_.matrix_ref) | copy-start | bytes 10616836
  387.5 11.6 %copy-start.24 = (bf16[2,512,1536]{2,1,0:T(8,128)(2,1)S(1)}, bf16[2,512,1536]{2,1,0:T(8,128)(2,1)}, u32[]{:S(2)}) copy-start(bf16[2,512,1536]{2,1,0:T(8,128)(2,1)} %get-tuple-element.92) | copy-start | bytes 9437188
  399.1 2.3 copy-start.10
  405.9 2.0 copy-start.17
  405.9 2.0 copy-start.18
  405.9 2.0 copy-start.19
  408.6 48.4 %copy-start.11 = (bf16[512,768]{1,0:T(8,128)(2,1)S(1)}, bf16[512,768]{1,0:T(8,128)(2,1)}, u32[]{:S(2)}) copy-start(bf16[512,768]{1,0:T(8,128)(2,1)} %get-tuple-element.97) | copy-start | bytes 2359300
  454.0 6.6 %copy-start.8 = (f32[192,1152]{1,0:T(8,128)S(1)}, f32[192,1152]{1,0:T(8,128)}, u32[]{:S(2)}) copy-start(f32[192,1152]{1,0:T(8,128)} %get-tuple-element.200) | copy-start | bytes 2654212
  454.0 7.5 %copy-start.12 = (f32[192,384]{1,0:T(8,128)S(1)}, f32[192,384]{1,0:T(8,128)}, u32[]{:S(2)}) copy-start(f32[192,384]{1,0:T(8,128)} %get-tuple-element.201) | copy-start | bytes 884740
  454.0 8.2 %copy-start.7 = (f32[192,1536]{1,0:T(8,128)S(1)}, f32[192,1536]{1,0:T(8,128)}, u32[]{:S(2)}) copy-start(f32[192,1536]{1,0:T(8,128)} %get-tuple-element.202) | copy-start | bytes 3538948
  457.0 7.2 %copy-start.1 = (s32[2,1,8]{2,1,0:T(1,128)S(1)}, s32[2,1,8]{2,1,0:T(1,128)}, u32[]{:S(2)}) copy-start(s32[2,1,8]{2,1,0:T(1,128)} %param.18) | copy-start | bytes 196
  457.0 6.2 %copy-start.6 = (f32[768,384]{1,0:T(8,128)S(1)}, f32[768,384]{1,0:T(8,128)}, u32[]{:S(2)}) copy-start(f32[768,384]{1,0:T(8,128)} %get-tuple-element.203) | copy-start | bytes 3538948

commit v6 on v5

--- a/solution.py
+++ b/solution.py
@@ -1108,6 +1108,7 @@
             def _(batch=launches[when]):
                 for part, stage in batch:
                     part.prepare(stage)
+                    part.launch(stage)
 
     own_keys = k_ref[0] * jnp.asarray(scale, LOW)
     own_values = v_ref[0]
@@ -1177,13 +1178,6 @@
     sums_ref[0, 0, 8:16] = folded(totals[1]) + folded(totals[3])
     for copy in stores(group, tile, slot):
         copy.start()
-    for when in sorted(launches):
-
-        @pl.when(step == when)
-        def _(batch=launches[when]):
-            for part, stage in batch:
-                part.launch(stage)
-
     if grid is not None:
 
         @pl.when(step == final)

time: 474 us -> 474 us (level)
    pallas_call x1, Pallas kernels: 88 us -> 33.6 us  [widen(): pl.pallas_call(functools.partial(widen_kernel, grid=grid, whens=(0, 1, 4)...]
    pallas_call x0 -> x1, Pallas kernels: none -> 51.8 us  [attend_again(): pl.pallas_call(functools.partial(attend_again_kernel, head=head), grid=(b...]
where the time goes in v6:
time: 474 us; the launch traced here: 464 us
  Pallas kernels  331 us (70%)
  matrix products  87.9 us (19%)
  other arithmetic  23.1 us (5%)
  local copies, waits for them, and re-layouts  16.6 us (4%)
    pallas_call x1, Pallas kernels, attend_back(): pl.pallas_call(functools.partial(attend_back_kernel, head=head, scale=hea...  91.6 us
    dot_general x5, matrix products, nn(): lax.dot_general(left, right, (((1,), (0,)), ((), ())), preferred_element_...  57.5 us
    pallas_call x1, Pallas kernels, attend_again(): pl.pallas_call(functools.partial(attend_again_kernel, head=head), grid=(b...  51.8 us
    pallas_call x1, Pallas kernels, end(): pl.pallas_call(functools.partial(end_kernel, grid=grid, dp=dp), grid=(row...  45.4 us
    pallas_call x1, Pallas kernels, attend(): pl.pallas_call(functools.partial(attend_kernel, head=head, grid=grid), gr...  44.5 us
    pallas_call x1, Pallas kernels, narrow(): pl.pallas_call(functools.partial(narrow_kernel, grid=grid, whens=(0, 1, 5...  33.7 us
    pallas_call x1, Pallas kernels, widen(): pl.pallas_call(functools.partial(widen_kernel, grid=grid, whens=(0, 1, 4)...  33.6 us
    pallas_call x1, Pallas kernels, begin(): pl.pallas_call(functools.partial(begin_kernel, grid=grid), in_specs=[anyw...  30.2 us
  transfers between devices with their start and end apart: 2, of which 0 were waited for; matrix products, arithmetic and copies ran while one was open for 5% of the time, Pallas kernels for 0%

profile of v6, /device:TPU:8, one launch (start us, length us, event | category | flops | bytes accessed | tf_op | source)
XLA Modules:
  0.0 464.1 jit_solution(1400930114116325445)
XLA Ops:
  0.6 0.0 copy-start
  0.6 0.0 copy-start.2
  0.7 2.2 slice.58
  2.9 30.2 %begin.1 = (bf16[512,768]{1,0:T(8,128)(2,1)}, bf16[768,2304]{1,0:T(8,128)(2,1)}) custom-call(bf16[2,1024,768]{2,1,0:T(8,128)(2,1)} %tokens_ref.1, bf16[192,1152]{1,0:T(8,128)(2,1)} %block_ref.1), custom_call_target="tpu_custom_call" | custom-call | bytes 28311552 | tf_op jit(solution)/shard_map/begin/pallas_call | solution.py:993
  33.1 0.6 collective-permute-start
  33.7 1.5 collective-permute-start.1
  35.2 0.1 constant_dynamic-slice_fusion
  35.3 0.1 broadcast_bitcast_fusion
  35.4 2.2 slice_reduce_fusion.1
  37.6 1.4 convert_reduce_fusion
  39.1 12.4 %add_convert_fusion = bf16[2304,2048]{0,1:T(8,128)(2,1)} fusion(bf16[2048,768]{1,0:T(8,128)(2,1)} %bitcast.79, bf16[768,2304]{1,0:T(8,128)(2,1)} %get-tuple-element.72.rest_3_.rest_4_.matrix_ref, f32[2304]{0:T(1024)S(1)} %pad_maximum_fusion.2), kind=kOutput, calls=%fused_computation.12 | convolution fusion | flops 7257194496 | bytes 16131072 | tf_op jit(solution)/shard_map/dot_general | solution.py:26
  51.4 0.6 copy.32
  52.0 0.6 stack.14
  52.7 0.9 fusion.33.mask_ref
  53.6 0.0 collective-permute-done
  53.6 1.3 pad_maximum_fusion.1
  54.8 4.5 add_convert_fusion.2
  59.3 0.0 collective-permute-done.1.moved_block
  59.4 44.5 %attend.1 = (bf16[2,1024,768]{2,1,0:T(8,128)(2,1)}, f32[2,6,2,1024]{3,2,1,0:T(2,128)}, f32[2,6,8,512]{3,2,1,0:T(8,128)}, bf16[768,768]{1,0:T(8,128)(2,1)}, bf16[...) custom-call(bf16[2,1024,2304]{2,1,0:T(8,128)(2,1)} %bitcast.72, bf16[2,1024,2304]{2,1,0:T(8,128)(2,1)} %bitcast.73, ...), custom_call_target="tpu_custom_call" | custom-call | flops 28991029248 | bytes 18874368 | tf_op jit(solution)/shard_map/attend/pallas_call | solution.py:914
  103.9 1.6 reduce_max.9
  105.5 54.7 %while.12 = (f32[]{:T(128)}, bf16[2,1024,768]{2,1,0:T(8,128)(2,1)}, f32[2,6,2,1024]{3,2,1,0:T(2,128)}, bf16[2,1024,2304]{2,1,0:T(8,128)(2,1)}, bf16[2,512,1536]{...) while((f32[]{:T(128)}, bf16[2,1024,768]{2,1,0:T(8,128)(2,1)}, ...), condition=%region_2.3_spmd.clone, body=%region_1.2_spmd.clone | while | flops 393217 | bytes 593993 | solution.py:942
  106.3 0.9 fusion.3.refs_5_
  107.2 51.8 %attend_again.1 = (bf16[2,1024,768]{2,1,0:T(8,128)(2,1)}, f32[2,6,2,1024]{3,2,1,0:T(2,128)}) custom-call(bf16[2,1024,2304]{2,1,0:T(8,128)(2,1)} %get-tuple-element.186.refs_0_.refs_1_.refs_2_, bf16[2,1024,2304]{2,1,0:T(8,128)(2,1)} %get-tuple-element.186.refs_0_.refs_1_.refs_2_, bf16[2,1024,2304]{2,1,0:T(8,128)(2,1)} %get-tuple-element.186.refs_0_.refs_1_.refs_2_, ...), custom_call_target="tpu_custom_call" | custom-call | tf_op jit(solution)/shard_map/while/body/attend_again/pallas_call | solution.py:887
  160.2 6.1 %fusion.39 = (f32[2048]{0:T(1024)S(1)}, f32[2048,768]{1,0:T(8,128)S(1)}) fusion(f32[768]{0:T(1024)S(1)} %get-tuple-element.129, bf16[2048,768]{1,0:T(8,128)(2,1)} %bitcast.95, bf16[768,768]{1,0:T(8,128)(2,1)} %get-tuple-element.80.out_ref, bf16[2048,768]{1,0:T(8,128)(2,1)} %bitcast.80), kind=kOutput, calls=%fused_computation.85 | convolution fusion | flops 2422208512 | bytes 13773824 | tf_op jit(solution)/shard_map/dot_general | solution.py:26
  166.3 0.0 slice-start
  166.3 0.8 multiply_reduce_fusion.1
  167.1 0.0 copy-start.21
  167.2 2.8 multiply_convert_fusion.1
  170.0 19.6 %fusion.8 = (bf16[2048,3072]{1,0:T(8,128)(2,1)}, bf16[2048,3072]{1,0:T(8,128)(2,1)}) fusion(f32[3072]{0:T(1024)S(1)} %copy-done.21, bf16[2048,768]{1,0:T(8,128)(2,1)S(1)} %get-tuple-element.153.hidden_ref, bf16[768,3072]{1,0:T(8,128)(2,1)S(1)} %bitcast.98), kind=kOutput, calls=%fused_computation.9 | convolution fusion | flops 9739173888 | bytes 33042432 | tf_op jit(solution)/shard_map/dot_general | solution.py:26
  189.7 14.9 %fusion.40 = (f32[2048]{0:T(1024)S(1)}, f32[2048,768]{1,0:T(8,128)S(1)}) fusion(f32[768]{0:T(1024)S(1)} %get-tuple-element.126, bf16[2048,3072]{1,0:T(8,128)(2,1)} %get-tuple-element.150, bf16[3072,768]{1,0:T(8,128)(2,1)} %get-tuple-element.82.down_ref, f32[768]{0:T(1024)S(1)} %get-tuple-element.127, f32[768]{0:T(1024)S(1)} %get-tuple-element.128, ...), kind=kOutput, calls=%fused_computation.86 | convolution fusion | flops 9674684416 | bytes 29918208 | tf_op jit(solution)/shard_map/dot_general | solution.py:26
  204.5 0.0 copy-start.3
  204.5 0.0 copy-start.14
  204.6 0.8 multiply_reduce_fusion
  205.4 0.0 copy-start.15
  205.4 0.0 copy-start.16
  205.4 1.0 copy-done.3
  206.4 2.3 fusion.18
  208.8 0.0 slice-start.4
  208.8 4.0 fusion.37
  212.8 0.6 stack.12
  213.4 1.0 stack.13
  214.4 12.2 %convolution_convert_fusion.total_ref = bf16[3072,768]{1,0:T(8,128)(2,1)} fusion(bf16[2048,3072]{1,0:T(8,128)(2,1)S(1)} %bitcast.100, bf16[2048,768]{1,0:T(8,128)(2,1)S(1)} %get-tuple-element.148.second_ref), kind=kOutput, calls=%fused_computation.39 | convolution fusion | flops 9666035712 | bytes 20447232 | tf_op jit(solution)/shard_map/dot_general | solution.py:30
  226.6 1.3 copy.20.inverse_ref
  228.0 33.6 %widen.1 = (bf16[2048,3072]{1,0:T(8,128)(2,1)}, bf16[768,3072]{1,0:T(8,128)(2,1)}, f32[8,3072]{1,0:T(8,128)}, bf16[768,384]{1,0:T(8,128)(2,1)}) custom-call(bf16[2048,768]{1,0:T(8,128)(2,1)} %copy-done.5, bf16[2048,768]{1,0:T(8,128)(2,1)} %copy-done.4, bf16[3072,768]{1,0:T(8,128)(2,1)} %get-tuple-element.82.down_ref, ...), custom_call_target="tpu_custom_call" | custom-call | flops 19327352832 | bytes 37748736 | tf_op jit(solution)/shard_map/widen/pallas_call | solution.py:410
  261.6 33.7 %narrow.1 = (bf16[2048,768]{1,0:T(8,128)(2,1)}, bf16[2048,768]{1,0:T(8,128)(2,1)}, bf16[768,768]{1,0:T(8,128)(2,1)}, f32[24,768]{1,0:T(8,128)}, bf16[192,1536]{1,0:T(8,128)(2,1)}) custom-call(bf16[2048,3072]{1,0:T(8,128)(2,1)} %get-tuple-element.83.grad_ref, bf16[2048,768]{1,0:T(8,128)(2,1)} %copy-done.5, bf16[2048,768]{1,0:T(8,128)(2,1)} %get-tuple-element.152.normed_ref, ...), custom_call_target="tpu_custom_call" | custom-call | flops 14495514624 | bytes 12582912 | tf_op jit(solution)/shard_map/narrow/pallas_call | solution.py:487
  295.3 91.6 %attend_back.1 = (bf16[2,1024,2304]{2,1,0:T(8,128)(2,1)}, bf16[2,512,1536]{2,1,0:T(8,128)(2,1)}, f32[2,6,16,128]{3,2,1,0:T(8,128)}, f32[768,384]{1,0:T(8,128)}, ...) custom-call(bf16[2,1024,2304]{2,1,0:T(8,128)(2,1)} %get-tuple-element.206, ...), custom_call_target="tpu_custom_call" | custom-call | flops 72477573120 | bytes 47185920 | tf_op jit(solution)/shard_map/attend_back/pallas_call | solution.py:1228
  386.9 11.5 %convolution_bitcast_fusion = f32[768,2304]{1,0:T(8,128)S(1)} fusion(bf16[2,1024,2304]{2,1,0:T(8,128)(2,1)} %get-tuple-element.90, bf16[2,1024,768]{2,1,0:T(8,128)(2,1)} %tokens_ref.1), kind=kOutput, calls=%fused_computation.38 | convolution fusion | flops 7247757312 | bytes 19660800 | tf_op jit(solution)/shard_map/dot_general | solution.py:30
  398.4 0.1 slice.101
  398.6 2.3 fusion.27.sent_ref
  400.9 4.5 fusion.20
  405.4 0.0 copy-start.18
  405.4 0.0 copy-start.19
  405.4 2.0 pad_maximum_fusion.total_ref
  407.4 0.6 pad_maximum_fusion.3.last_ref
  408.0 45.4 %end.1 = (bf16[2048,768]{1,0:T(8,128)(2,1)}, f32[192,1152]{1,0:T(8,128)}, f32[16,768]{1,0:T(8,128)}, bf16[512,768]{1,0:T(8,128)(2,1)}) custom-call(bf16[2048,2304]{1,0:T(8,128)(2,1)} %bitcast.93, bf16[768,2304]{1,0:T(8,128)(2,1)} %get-tuple-element.72.rest_3_.rest_4_.matrix_ref, bf16[2048,768]{1,0:T(8,128)(2,1)} %get-tuple-element.91.first_ref, ...), custom_call_target="tpu_custom_call" | custom-call | flops 7247757312 | bytes 37748736 | tf_op jit(solution)/shard_map/end/pallas_call | solution.py:672
  453.5 0.9 slice.71
  454.4 0.7 slice.72
  455.1 0.7 dynamic-slice_bitcast_fusion
  455.8 0.7 dynamic_slice.16
  456.5 3.6 fusion.11
  460.0 0.9 copy.49
  461.0 0.7 copy.50
  461.7 1.0 copy.51
  462.7 1.0 copy.52
  (63 shorter events, 0.2 us)
Async XLA Ops:
  0.6 34.6 %copy-start = (s32[2,1,8]{2,1,0:T(1,128)S(1)}, s32[2,1,8]{2,1,0:T(1,128)}, u32[]{:S(2)}) copy-start(s32[2,1,8]{2,1,0:T(1,128)} %param.18) | copy-start | bytes 196
  0.6 37.0 %copy-start.2 = (bf16[2,1024,768]{2,1,0:T(8,128)(2,1)S(1)}, bf16[2,1024,768]{2,1,0:T(8,128)(2,1)}, u32[]{:S(2)}) copy-start(bf16[2,1024,768]{2,1,0:T(8,128)(2,1)} %param.19) | copy-start | bytes 9437188
  33.1 20.5 %collective-permute-start = (bf16[1,512,768]{2,1,0:T(8,128)(2,1)}, bf16[1,512,768]{2,1,0:T(8,128)(2,1)}, u32[]{:S(2)}, u32[]{:S(2)}) collective-permute-start(bf16[1,512,768]{2,1,0:T(8,128)(2,1)} %slice.58), channel_id=1, source_target_pairs={{0,1},{1,0},{2,3},{3,2},{4,5},{5,4},{6,7},{7,6},{8,9},{9,8},{10,11... | collective-permute-start | bytes 2359304 | tf_op jit(solution)/shard_map/ppermute | solution.py:1263
  33.7 25.6 %collective-permute-start.1 = (bf16[768,384]{1,0:T(8,128)(2,1)}, bf16[768,384]{1,0:T(8,128)(2,1)}, u32[]{:S(2)}, u32[]{:S(2)}) collective-permute-start(bf16[768,384]{1,0:T(8,128)(2,1)} %down_block.1), channel_id=1, source_target_pairs={{0,4},{2,6},{4,0},{6,2},{1,5},{3,7},{5,1},{7,3},{8,12},{10,14},{12... | collective-permute-start | bytes 1769480 | tf_op jit(solution)/shard_map/ppermute | solution.py:1263
  37.6 1.5 copy-start.13
  39.1 14.5 %copy-start.9 = (bf16[512,768]{1,0:T(8,128)(2,1)S(1)}, bf16[512,768]{1,0:T(8,128)(2,1)}, u32[]{:S(2)}) copy-start(bf16[512,768]{1,0:T(8,128)(2,1)} %get-tuple-element.73) | copy-start | bytes 2359300
  166.3 3.7 slice-start
  167.1 2.9 copy-start.21
  167.2 2.9 slice-start.1
  170.0 19.7 %copy-start.4 = (bf16[2048,768]{1,0:T(8,128)(2,1)}, bf16[2048,768]{1,0:T(8,128)(2,1)S(1)}, u32[]{:S(2)}) copy-start(bf16[2048,768]{1,0:T(8,128)(2,1)S(1)} %get-tuple-element.153.hidden_ref) | copy-start | bytes 9437188
  204.5 1.9 copy-start.3
  204.5 1.9 copy-start.14
  205.4 3.4 copy-start.15
  205.4 3.4 copy-start.16
  206.4 8.0 %slice-start.2 = ((s8[12582912]{0:T(1024)(128)(4,1)}), s8[4194304]{0:T(1024)(128)(4,1)S(1)}, s32[]{:S(2)}) async-start(s8[12582912]{0:T(1024)(128)(4,1)} %bitcast.99), calls=%async_computation.2 | async-start | bytes 8388608
  206.4 8.0 %slice-start.3 = ((s8[12582912]{0:T(1024)(128)(4,1)}), s8[4194304]{0:T(1024)(128)(4,1)S(1)}, s32[]{:S(2)}) async-start(s8[12582912]{0:T(1024)(128)(4,1)} %bitcast.99), calls=%async_computation.3 | async-start | bytes 8388608
  208.8 5.6 %slice-start.4 = ((s8[12582912]{0:T(1024)(128)(4,1)}), s8[4194304]{0:T(1024)(128)(4,1)S(1)}, s32[]{:S(2)}) async-start(s8[12582912]{0:T(1024)(128)(4,1)} %bitcast.99), calls=%async_computation.4 | async-start | bytes 8388608
  212.8 13.8 %copy-start.5 = (bf16[2048,768]{1,0:T(8,128)(2,1)}, bf16[2048,768]{1,0:T(8,128)(2,1)S(1)}, u32[]{:S(2)}) copy-start(bf16[2048,768]{1,0:T(8,128)(2,1)S(1)} %get-tuple-element.148.second_ref) | copy-start | bytes 9437188
  228.0 33.6 %copy-start.22 = (bf16[2,1024,768]{2,1,0:T(8,128)(2,1)S(1)}, bf16[2,1024,768]{2,1,0:T(8,128)(2,1)}, u32[]{:S(2)}) copy-start(bf16[2,1024,768]{2,1,0:T(8,128)(2,1)} %get-tuple-element.79.out_ref) | copy-start | bytes 9437188
  261.5 33.7 %copy-start.23 = (f32[2,6,2,1024]{3,2,1,0:T(2,128)S(1)}, f32[2,6,2,1024]{3,2,1,0:T(2,128)}, u32[]{:S(2)}) copy-start(f32[2,6,2,1024]{3,2,1,0:T(2,128)} %get-tuple-element.86.lse_ref) | copy-start | bytes 294916
  386.9 11.6 %copy-start.20 = (bf16[768,2304]{1,0:T(8,128)(2,1)S(1)}, bf16[768,2304]{1,0:T(8,128)(2,1)}, u32[]{:S(2)}) copy-start(bf16[768,2304]{1,0:T(8,128)(2,1)} %get-tuple-element.72.rest_3_.rest_4_.matrix_ref) | copy-start | bytes 10616836
  386.9 11.6 %copy-start.24 = (bf16[2,512,1536]{2,1,0:T(8,128)(2,1)S(1)}, bf16[2,512,1536]{2,1,0:T(8,128)(2,1)}, u32[]{:S(2)}) copy-start(bf16[2,512,1536]{2,1,0:T(8,128)(2,1)} %get-tuple-element.92) | copy-start | bytes 9437188
  398.5 2.3 copy-start.10
  405.4 2.0 copy-start.17
  405.4 2.0 copy-start.18
  405.4 2.0 copy-start.19
  408.0 48.4 %copy-start.11 = (bf16[512,768]{1,0:T(8,128)(2,1)S(1)}, bf16[512,768]{1,0:T(8,128)(2,1)}, u32[]{:S(2)}) copy-start(bf16[512,768]{1,0:T(8,128)(2,1)} %get-tuple-element.97) | copy-start | bytes 2359300
  453.5 6.6 %copy-start.8 = (f32[192,1152]{1,0:T(8,128)S(1)}, f32[192,1152]{1,0:T(8,128)}, u32[]{:S(2)}) copy-start(f32[192,1152]{1,0:T(8,128)} %get-tuple-element.200) | copy-start | bytes 2654212
  453.5 7.5 %copy-start.12 = (f32[192,384]{1,0:T(8,128)S(1)}, f32[192,384]{1,0:T(8,128)}, u32[]{:S(2)}) copy-start(f32[192,384]{1,0:T(8,128)} %get-tuple-element.201) | copy-start | bytes 884740
  453.5 8.2 %copy-start.7 = (f32[192,1536]{1,0:T(8,128)S(1)}, f32[192,1536]{1,0:T(8,128)}, u32[]{:S(2)}) copy-start(f32[192,1536]{1,0:T(8,128)} %get-tuple-element.202) | copy-start | bytes 3538948
  456.5 7.2 %copy-start.1 = (s32[2,1,8]{2,1,0:T(1,128)S(1)}, s32[2,1,8]{2,1,0:T(1,128)}, u32[]{:S(2)}) copy-start(s32[2,1,8]{2,1,0:T(1,128)} %param.18) | copy-start | bytes 196
  456.5 6.2 %copy-start.6 = (f32[768,384]{1,0:T(8,128)S(1)}, f32[768,384]{1,0:T(8,128)}, u32[]{:S(2)}) copy-start(f32[768,384]{1,0:T(8,128)} %get-tuple-element.203) | copy-start | bytes 3538948
